TPU v7x, 32 devices: a whole 2x2x4 slice. The times are simulated.
32 devices in a mesh: dp: 8 (over z, core), expert: 4 (over y, x).
Axes of the slice: x: 2, y: 2, z: 4, core: 2. Of those that a mesh axis runs over, the one named last changes fastest.
Arguments:
- tokens: bfloat16 [512, 2048], P(('dp', 'expert')), may hold values from -6 to 6
- grad_out: bfloat16 [512, 2048], P(('dp', 'expert')), may hold values from -6 to 6
- gate_probs: bfloat16 [512, 8], P(('dp', 'expert')), may hold values from 0.049804688 to 1
- routes: int32 [512, 8], P(('dp', 'expert')), may hold values from 0 to 15, as said below
- capacity: int32 [8, 16], P('dp', 'expert'), may hold values from 16 to 32, as said below
- pair_mask: int32 [16], P('expert'), may hold values from 1 to 4, as said below
- gate_up_weight: bfloat16 [16, 2048, 1536], P('expert'), may hold values from -0.125 to 0.125
- down_weight: bfloat16 [16, 2048, 768], P('expert'), may hold values from -0.21875 to 0.21875
Outputs:
- layer_out: bfloat16 [512, 2048], P(('dp', 'expert'))
- input_grad: bfloat16 [512, 2048], P(('dp', 'expert'))
- gate_grad: float32 [512, 8], P(('dp', 'expert'))
Inputs may be any that keep to these rules, and one draw needn't show every extreme that they name: `routes`: each token names 8 different experts. The tokens of one device name any one expert at most 12 times; one expert, the same for all devices, is named exactly 12 times by the tokens of every device. `capacity`: both ends of the range occur in every draw. `pair_mask`: each entry is a power of two; both ends of the range occur in every draw.
All inputs are finite; a program needn't handle non-finite values.
Results may differ from a plain program's by a relative error of at most 0.01.
Values may be sent and summed in bfloat16 or wider, within the bound.
No kernel may reach another device: no remote copies, remote signals or barrier semaphores. Data moves between devices by JAX's collectives and lax.ppermute only.
A program may use at most 128 MiB of HBM per device.

v0:
```python
import jax
import jax.numpy as jnp
from jax import lax
from jax.sharding import PartitionSpec as P

TOPK = 8
EXPERTS = 16
MOST = 12
OVF = 16


far_position = 1 << 20


def swapped(shard, axis, apart):
    return lax.ppermute(shard, axis, [(i, i ^ 1 << apart) for i in range(lax.axis_size(axis))])


def pick_rows(table, index):
    return jnp.take(table, index, axis=0, mode="fill", fill_value=0)


def expert_rows(row_input, row_scaled, w_gate_up, w_down):
    hidden_units = w_down.shape[1]
    both = jnp.dot(row_input, w_gate_up, preferred_element_type=jnp.float32)
    gate_pre = both[:, :hidden_units]
    up_pre = both[:, hidden_units:]
    sigma = jax.nn.sigmoid(gate_pre)
    swish = gate_pre * sigma
    hidden = (swish * up_pre).astype(jnp.bfloat16)
    outputs = lax.dot_general(
        hidden, w_down, (((1,), (1,)), ((), ())), preferred_element_type=jnp.float32
    ).astype(jnp.bfloat16)
    back_hidden = jnp.dot(row_scaled, w_down, preferred_element_type=jnp.float32)
    d_gate = back_hidden * up_pre * sigma * (1.0 + gate_pre * (1.0 - sigma))
    d_up = back_hidden * swish
    d_both = jnp.concatenate([d_gate, d_up], axis=1).astype(jnp.bfloat16)
    row_grads = lax.dot_general(
        d_both, w_gate_up, (((1,), (1,)), ((), ())), preferred_element_type=jnp.float32
    ).astype(jnp.bfloat16)
    return (outputs, row_grads)


def run_experts(row_input, row_scaled, gate_up_weight, down_weight, row_count):
    local_count = gate_up_weight.shape[0]
    outputs = []
    grad_parts = []
    for local_id in range(local_count):
        first_row = local_id * row_count
        out_rows, grad_rows = expert_rows(
            row_input[first_row : first_row + row_count],
            row_scaled[first_row : first_row + row_count],
            gate_up_weight[local_id],
            down_weight[local_id],
        )
        outputs.append(out_rows)
        grad_parts.append(grad_rows)
    return (jnp.concatenate(outputs, axis=0), jnp.concatenate(grad_parts, axis=0))


def serve_rows(
    pool_tokens,
    pool_scaled,
    queue_pos,
    item_local,
    queue_length,
    local_caps,
    pair_mask,
    gate_up_weight,
    down_weight,
    cap_rows,
):
    local_count = queue_length.shape[0]
    pool_size = pool_tokens.shape[0]
    pool_ids = jnp.arange(pool_size, dtype=jnp.int32)
    home_rows = jnp.minimum(queue_length, local_caps)
    spare_rows = local_caps - home_rows
    accepted = jnp.minimum(spare_rows, OVF)
    cap_item = local_caps[item_local]
    offset = queue_pos - cap_item
    spilled = (offset >= 0) & (offset < OVF)
    spill_slot = jnp.where(spilled, item_local * OVF + offset, local_count * OVF)
    spill_from = (
        jnp.full((local_count * OVF + 1,), pool_size, jnp.int32)
        .at[spill_slot]
        .set(pool_ids)[: local_count * OVF]
    )
    outgoing = jnp.stack([pick_rows(pool_tokens, spill_from), pick_rows(pool_scaled, spill_from)])
    home_slot = jnp.where(
        queue_pos < cap_item, item_local * cap_rows + queue_pos, local_count * cap_rows
    )
    home_from = (
        jnp.full((local_count * cap_rows + 1,), pool_size, jnp.int32)
        .at[home_slot]
        .set(pool_ids)[: local_count * cap_rows]
    )
    home_tokens = pick_rows(pool_tokens, home_from)
    home_scaled = pick_rows(pool_scaled, home_from)
    slot_ids = jnp.arange(local_count * OVF, dtype=jnp.int32)
    slot_local = slot_ids // OVF
    slot_index = slot_ids % OVF
    slot_mask = pair_mask[slot_local]
    is_live = slot_index < accepted[slot_local]
    levels = lax.axis_size("dp").bit_length() - 1
    incoming = jnp.zeros_like(outgoing)
    for bit_index in range(levels):
        received = swapped(outgoing, "dp", bit_index)
        incoming = jnp.where((slot_mask == 1 << bit_index)[None, :, None], received, incoming)
    incoming = jnp.where(is_live[None, :, None], incoming, jnp.zeros_like(incoming))
    in_slot = jnp.where(
        is_live, slot_local * cap_rows + home_rows[slot_local] + slot_index, local_count * cap_rows
    )
    in_from = (
        jnp.full((local_count * cap_rows + 1,), local_count * OVF, jnp.int32)
        .at[in_slot]
        .set(slot_ids)[: local_count * cap_rows]
    )
    joined_tokens = home_tokens + pick_rows(incoming[0], in_from)
    joined_scaled = home_scaled + pick_rows(incoming[1], in_from)
    home_out, home_grad = run_experts(
        joined_tokens, joined_scaled, gate_up_weight, down_weight, cap_rows
    )
    returning = jnp.stack([pick_rows(home_out, in_slot), pick_rows(home_grad, in_slot)])
    answered = jnp.zeros_like(returning)
    for bit_index in range(levels):
        received_back = swapped(returning, "dp", bit_index)
        answered = jnp.where((slot_mask == 1 << bit_index)[None, :, None], received_back, answered)
    pool_out = pick_rows(home_out, home_slot) + pick_rows(answered[0], spill_slot)
    pool_grad = pick_rows(home_grad, home_slot) + pick_rows(answered[1], spill_slot)
    return (pool_out, pool_grad)


def body(tokens, grad_out, gate_probs, routes, capacity, pair_mask, gate_up_weight, down_weight):
    tok_count = tokens.shape[0]
    model_width = tokens.shape[1]
    local_count = gate_up_weight.shape[0]
    group_size = lax.axis_size("expert")
    cap_rows = group_size * tok_count * TOPK // EXPERTS
    route_total = tok_count * TOPK
    local_caps = capacity[0]
    flat_routes = routes.reshape(route_total)
    route_hits = (flat_routes[:, None] == jnp.arange(EXPERTS, dtype=jnp.int32)[None, :]).astype(
        jnp.int32
    )
    slot_rank = jnp.sum((jnp.cumsum(route_hits, axis=0) - 1) * route_hits, axis=1)
    counts = jnp.sum(route_hits, axis=0)
    dest_slot = flat_routes * MOST + slot_rank
    send_from = (
        jnp.full((EXPERTS * MOST,), route_total, jnp.int32)
        .at[dest_slot]
        .set(jnp.arange(route_total, dtype=jnp.int32))
    )
    scaled = (
        (gate_probs.astype(jnp.float32)[:, :, None] * grad_out.astype(jnp.float32)[:, None, :])
        .astype(jnp.bfloat16)
        .reshape(route_total, model_width)
    )
    send_tokens = pick_rows(tokens, send_from // TOPK)
    send_scaled = pick_rows(scaled, send_from)
    got_tokens, got_scaled, got_counts = (
        lax.all_to_all(send_tokens, "expert", split_axis=0, concat_axis=0, tiled=True),
        lax.all_to_all(send_scaled, "expert", split_axis=0, concat_axis=0, tiled=True),
        lax.all_to_all(
            counts.astype(jnp.bfloat16), "expert", split_axis=0, concat_axis=0, tiled=True
        ),
    )
    source_counts = got_counts.astype(jnp.int32).reshape(group_size, local_count)
    earlier = jnp.cumsum(source_counts, axis=0) - source_counts
    queue_length = jnp.sum(source_counts, axis=0)
    item_index = jnp.arange(group_size * local_count * MOST, dtype=jnp.int32)
    item_source = item_index // (local_count * MOST)
    item_local = item_index // MOST % local_count
    item_slot = item_index % MOST
    queue_pos = jnp.where(
        item_slot < source_counts[item_source, item_local],
        earlier[item_source, item_local] + item_slot,
        far_position,
    )
    pool_out, pool_grad = serve_rows(
        got_tokens,
        got_scaled,
        queue_pos,
        item_local,
        queue_length,
        local_caps,
        pair_mask,
        gate_up_weight,
        down_weight,
        cap_rows,
    )
    back_out, back_grad = (
        lax.all_to_all(pool_out, "expert", split_axis=0, concat_axis=0, tiled=True),
        lax.all_to_all(pool_grad, "expert", split_axis=0, concat_axis=0, tiled=True),
    )
    route_out = (
        pick_rows(back_out, dest_slot).astype(jnp.float32).reshape(tok_count, TOPK, model_width)
    )
    route_grad = (
        pick_rows(back_grad, dest_slot).astype(jnp.float32).reshape(tok_count, TOPK, model_width)
    )
    layer_out = jnp.sum(gate_probs.astype(jnp.float32)[:, :, None] * route_out, axis=1).astype(
        jnp.bfloat16
    )
    input_grad = jnp.sum(route_grad, axis=1).astype(jnp.bfloat16)
    gate_grad = jnp.sum(grad_out.astype(jnp.float32)[:, None, :] * route_out, axis=2)
    return (layer_out, input_grad, gate_grad)


def solution(mesh):
    return jax.shard_map(
        body,
        mesh=mesh,
        in_specs=(
            P(("dp", "expert"), None),
            P(("dp", "expert"), None),
            P(("dp", "expert"), None),
            P(("dp", "expert"), None),
            P("dp", "expert"),
            P("expert"),
            P("expert", None, None),
            P("expert", None, None),
        ),
        out_specs=(P(("dp", "expert"), None), P(("dp", "expert"), None), P(("dp", "expert"), None)),
        check_vma=False,
    )
```

profile of v0, /device:TPU:0, one launch (start us, length us, event | category | flops | bytes accessed | tf_op | source)
XLA Modules:
  0.0 177.5 jit_solution(14356134754406343365)
XLA Ops:
  2.7 5.2 %all-to-all-start.1 = ((bf16[4,4,1]{1,2,0:T(2,128)(2,1)}), bf16[4,4,1]{1,2,0:T(2,128)(2,1)S(1)}, u32[]{:S(2)}, u32[]{:S(2)}) async-start(bf16[4,4,1]{1,2,0:T(2,128)(2,1)} %convert_element_type.108), calls=%async_computation.1 | async-start | bytes 4096 | tf_op jit(solution)/shard_map/all_to_all | solution.py:163
  14.5 2.5 %compare_bitcast_fusion.2 = (pred[64]{0:T(512)(128)(4,1)S(1)}, s32[64,1]{0,1:T(1,128)S(1)}) fusion(s32[]{:T(128)} %bitcast.28, s32[]{:T(128)} %bitcast.27, s32[]{:T(128)} %bitcast.26, s32[]{:T(128)} %bitcast.25), kind=kLoop, calls=%fused_computation.203 | loop fusion | flops 1152 | bytes 336 | tf_op jit(solution)/shard_map/eq | solution.py:108
  21.6 4.2 %all-to-all-start.2 = ((bf16[4,48,2048]{2,1,0:T(8,128)(2,1)}), bf16[4,48,2048]{2,1,0:T(8,128)(2,1)S(1)}, u32[]{:S(2)}, u32[]{:S(2)}) async-start(bf16[4,48,2048]{2,1,0:T(8,128)(2,1)} %bitcast.33), calls=%async_computation.2 | async-start | bytes 1572864 | tf_op jit(solution)/shard_map/all_to_all | solution.py:162
  25.9 2.0 %gather_fusion.1 = s32[192]{0:T(256)S(1)} fusion(s32[4,4]{1,0:T(4,128)S(1)} %bitcast.159, s32[192]{0:T(256)S(1)} %bitcast.164), kind=kCustom, calls=%fused_computation.16 | custom fusion | bytes 3072 | tf_op jit(solution)/shard_map/gather | solution.py:175
  27.8 2.0 %gather_fusion.2 = s32[192]{0:T(256)S(1)} fusion(s32[4,4]{1,0:T(4,128)S(1)} %sub.78, s32[192]{0:T(256)S(1)} %bitcast.165), kind=kCustom, calls=%fused_computation.17 | custom fusion | bytes 3072 | tf_op jit(solution)/shard_map/gather | solution.py:176
  29.8 2.6 %compare_select_fusion.1 = (s32[192,1]{0,1:T(1,128)S(1)}, s32[192,1]{0,1:T(1,128)S(1)}, s32[192,1]{0,1:T(1,128)S(1)}) fusion(s32[]{:T(128)} %bitcast.5, s32[]{:T(128)} %bitcast.4, s32[]{:T(128)} %bitcast.3, s32[]{:T(128)} %bitcast.2, s32[192,1]{0,1:T(1,128)S(1)} %bitcast.173, s32[192,1]{0,1:T(1,128)S(1)} %bitcast.172), kind=kLoop, calls=%fused_computation.152 | loop fusion | flops 8064 | bytes 3856 | tf_op jit(solution)/shard_map/select_n | solution.py:95
  34.3 5.1 %compare_and_fusion.2 = (pred[64]{0:T(512)(128)(4,1)S(1)}, s32[64]{0:T(128)S(1)}, s32[64,1]{0,1:T(1,128)S(1)}, s32[64,1]{0,1:T(1,128)S(1)}) fusion(s32[]{:T(128)} %bitcast.22, s32[]{:T(128)} %bitcast.21, s32[]{:T(128)} %bitcast.20, s32[]{:T(128)} %bitcast.19, s32[]{:T(128)} %bitcast.18, s32[]{:T(128)} %bitcast.17, s32[]{:T(128)} %bitcast.16, s32[]{:T(128)} %bitcast.15), kind=kLoop, calls=%fused_computation.195 | loop fusion | flops 2752 | bytes 864 | tf_op jit(solution)/shard_map/jit(_take)/and | solution.py:20
  39.5 4.2 %all-to-all-start = ((bf16[4,48,2048]{2,1,0:T(8,128)(2,1)}), bf16[4,48,2048]{2,1,0:T(8,128)(2,1)S(1)}, u32[]{:S(2)}, u32[]{:S(2)}) async-start(bf16[4,48,2048]{2,1,0:T(8,128)(2,1)} %broadcast_select_fusion.1), calls=%async_computation | async-start | bytes 1572864 | tf_op jit(solution)/shard_map/all_to_all | solution.py:161
  46.7 6.7 %all-to-all-done = bf16[4,48,2048]{2,1,0:T(8,128)(2,1)S(1)} async-done(((bf16[4,48,2048]{2,1,0:T(8,128)(2,1)}), bf16[4,48,2048]{2,1,0:T(8,128)(2,1)S(1)}, u32[]{:S(2)}, u32[]{:S(2)}) %all-to-all-start) | async-done | bytes 786464 | tf_op jit(solution)/shard_map/all_to_all | solution.py:161
  55.1 2.6 %collective-permute-start = (bf16[2,64,2048]{2,1,0:T(8,128)(2,1)}, bf16[2,64,2048]{2,1,0:T(8,128)(2,1)S(1)}, u32[]{:S(2)}, u32[]{:S(2)}) collective-permute-start(bf16[2,64,2048]{2,1,0:T(8,128)(2,1)} %pad_maximum_fusion), channel_id=1, source_target_pairs={{0,16},{4,20},{8,24},{12,28},{16,0},{20,4},{24,8},{28,12},{1,17},{... | collective-permute-start | bytes 1572872 | tf_op jit(solution)/shard_map/ppermute | solution.py:16
  61.2 19.3 %collective-permute-done = bf16[2,64,2048]{2,1,0:T(8,128)(2,1)S(1)} collective-permute-done((bf16[2,64,2048]{2,1,0:T(8,128)(2,1)}, bf16[2,64,2048]{2,1,0:T(8,128)(2,1)S(1)}, u32[]{:S(2)}, u32[]{:S(2)}) %collective-permute-start) | collective-permute-done | bytes 524320 | tf_op jit(solution)/shard_map/ppermute | solution.py:16
  84.0 4.1 %fusion.14 = f32[32,1536]{1,0:T(8,128)S(1)} fusion(bf16[4,2048,1536]{2,1,0:T(8,128)(2,1)} %param.26, bf16[128,2048]{1,0:T(8,128)(2,1)S(1)} %get-tuple-element.58), kind=kOutput, calls=%fused_computation.36 | convolution fusion | flops 201326592 | bytes 6619136 | tf_op jit(solution)/shard_map/dot_general | solution.py:25
  88.1 4.1 %fusion.10 = f32[32,1536]{1,0:T(8,128)S(1)} fusion(bf16[4,2048,1536]{2,1,0:T(8,128)(2,1)} %param.26, bf16[128,2048]{1,0:T(8,128)(2,1)S(1)} %get-tuple-element.58), kind=kOutput, calls=%fused_computation.32 | convolution fusion | flops 201326592 | bytes 6619136 | tf_op jit(solution)/shard_map/dot_general | solution.py:25
  92.2 4.1 %fusion.6 = f32[32,1536]{1,0:T(8,128)S(1)} fusion(bf16[4,2048,1536]{2,1,0:T(8,128)(2,1)} %param.26, bf16[128,2048]{1,0:T(8,128)(2,1)S(1)} %get-tuple-element.58), kind=kOutput, calls=%fused_computation.28 | convolution fusion | flops 201326592 | bytes 6619136 | tf_op jit(solution)/shard_map/dot_general | solution.py:25
  96.3 4.1 %fusion.2 = f32[32,1536]{1,0:T(8,128)S(1)} fusion(bf16[4,2048,1536]{2,1,0:T(8,128)(2,1)} %param.26, bf16[128,2048]{1,0:T(8,128)(2,1)S(1)} %get-tuple-element.58), kind=kOutput, calls=%fused_computation.24 | convolution fusion | flops 201326592 | bytes 6619136 | tf_op jit(solution)/shard_map/dot_general | solution.py:25
  105.5 2.7 %multiply_convert_fusion.1 = (bf16[32,768]{1,0:T(8,128)(2,1)S(1)}, bf16[32,768]{1,0:T(8,128)(2,1)S(1)}) fusion(f32[32,1536]{1,0:T(8,128)S(1)} %fusion.2, bf16[4,2048,768]{2,1,0:T(8,128)(2,1)} %param.27, bf16[128,2048]{1,0:T(8,128)(2,1)S(1)} %get-tuple-element.59), kind=kOutput, calls=%fused_computation.128 | convolution fusion | flops 100982784 | bytes 3571712 | tf_op jit(solution)/shard_map/dot_general | solution.py:34
  108.2 2.9 %fusion.57 = bf16[32,2048]{1,0:T(8,128)(2,1)S(1)} fusion(bf16[4,2048,768]{2,1,0:T(8,128)(2,1)} %param.27, f32[32,1536]{1,0:T(8,128)S(1)} %fusion.2), kind=kOutput, calls=%fused_computation.73 | convolution fusion | flops 100876288 | bytes 3473408 | tf_op jit(solution)/shard_map/dot_general | solution.py:31
  115.0 1.9 %fusion.66 = bf16[32,2048]{1,0:T(8,128)(2,1)S(1)} fusion(bf16[4,2048,1536]{2,1,0:T(8,128)(2,1)S(1)} %bitcast.177, bf16[32,768]{1,0:T(8,128)(2,1)S(1)} %get-tuple-element.53, bf16[32,768]{1,0:T(8,128)(2,1)S(1)} %get-tuple-element.52), kind=kOutput, calls=%fused_computation.76 | convolution fusion | flops 201588736 | bytes 6520832 | tf_op jit(solution)/shard_map/dot_general | solution.py:38
  116.9 1.9 %fusion.69 = bf16[32,2048]{1,0:T(8,128)(2,1)S(1)} fusion(bf16[4,2048,1536]{2,1,0:T(8,128)(2,1)S(1)} %bitcast.177, bf16[32,768]{1,0:T(8,128)(2,1)S(1)} %get-tuple-element.55, bf16[32,768]{1,0:T(8,128)(2,1)S(1)} %get-tuple-element.54), kind=kOutput, calls=%fused_computation.77 | convolution fusion | flops 201588736 | bytes 6520832 | tf_op jit(solution)/shard_map/dot_general | solution.py:38
  122.3 2.4 %collective-permute-start.4 = (bf16[2,64,2048]{2,1,0:T(8,128)(2,1)S(1)}, bf16[2,64,2048]{2,1,0:T(8,128)(2,1)}, u32[]{:S(2)}, u32[]{:S(2)}) collective-permute-start(bf16[2,64,2048]{2,1,0:T(8,128)(2,1)S(1)} %pad_maximum_fusion.3), channel_id=1, source_target_pairs={{0,8},{4,12},{8,0},{12,4},{16,24},{20,28},{24,16},{28,20},{1,9},{5... | collective-permute-start | bytes 1572872 | tf_op jit(solution)/shard_map/ppermute | solution.py:16
  127.1 18.8 %collective-permute-done.3 = bf16[2,64,2048]{2,1,0:T(8,128)(2,1)} collective-permute-done((bf16[2,64,2048]{2,1,0:T(8,128)(2,1)S(1)}, bf16[2,64,2048]{2,1,0:T(8,128)(2,1)}, u32[]{:S(2)}, u32[]{:S(2)}) %collective-permute-start.3) | collective-permute-done | bytes 524320 | tf_op jit(solution)/shard_map/ppermute | solution.py:16
  151.0 12.2 %all_to_all.51 = bf16[4,48,2048]{2,1,0:T(8,128)(2,1)S(1)} all-to-all(bf16[4,48,2048]{2,1,0:T(8,128)(2,1)S(1)} %bitcast.168), channel_id=1, replica_groups=mesh['dp'=8,'expert'=4] {'expert'}, dimensions={0} | all-to-all | bytes 1572864 | tf_op jit(solution)/shard_map/all_to_all | solution.py:192
  163.2 3.5 %all-to-all-start.4 = ((bf16[4,48,2048]{2,1,0:T(8,128)(2,1)}), bf16[4,48,2048]{2,1,0:T(8,128)(2,1)S(1)}, u32[]{:S(2)}, u32[]{:S(2)}) async-start(bf16[4,48,2048]{2,1,0:T(8,128)(2,1)} %bitcast.56), calls=%async_computation.4 | async-start | bytes 1572864 | tf_op jit(solution)/shard_map/all_to_all | solution.py:193
  170.6 4.3 %all-to-all-done.4 = bf16[4,48,2048]{2,1,0:T(8,128)(2,1)S(1)} async-done(((bf16[4,48,2048]{2,1,0:T(8,128)(2,1)}), bf16[4,48,2048]{2,1,0:T(8,128)(2,1)S(1)}, u32[]{:S(2)}, u32[]{:S(2)}) %all-to-all-start.4) | async-done | bytes 786464 | tf_op jit(solution)/shard_map/all_to_all | solution.py:193
  (133 shorter events, 53.0 us)
Async XLA Ops:
  0.6 18.8 %copy-start = (bf16[16,2048]{1,0:T(8,128)(2,1)S(1)}, bf16[16,2048]{1,0:T(8,128)(2,1)}, u32[]{:S(2)}) copy-start(bf16[16,2048]{1,0:T(8,128)(2,1)} %param.20) | copy-start | bytes 196612
  0.6 33.0 %copy-start.2 = (s32[1,4]{1,0:T(1,128)S(1)}, s32[1,4]{1,0:T(1,128)}, u32[]{:S(2)}) copy-start(s32[1,4]{1,0:T(1,128)} %param.24) | copy-start | bytes 52
  2.7 18.9 %all-to-all-start.1 = ((bf16[4,4,1]{1,2,0:T(2,128)(2,1)}), bf16[4,4,1]{1,2,0:T(2,128)(2,1)S(1)}, u32[]{:S(2)}, u32[]{:S(2)}) async-start(bf16[4,4,1]{1,2,0:T(2,128)(2,1)} %convert_element_type.108), calls=%async_computation.1 | async-start | bytes 4096 | tf_op jit(solution)/shard_map/all_to_all | solution.py:163
  12.1 5.0 %copy-start.1 = (f32[16,2048]{1,0:T(8,128)}, f32[16,2048]{1,0:T(8,128)S(1)}, u32[]{:S(2)}) copy-start(f32[16,2048]{1,0:T(8,128)S(1)} %convert_element_type.91) | copy-start | bytes 393220
  21.6 17.9 %all-to-all-start.2 = ((bf16[4,48,2048]{2,1,0:T(8,128)(2,1)}), bf16[4,48,2048]{2,1,0:T(8,128)(2,1)S(1)}, u32[]{:S(2)}, u32[]{:S(2)}) async-start(bf16[4,48,2048]{2,1,0:T(8,128)(2,1)} %bitcast.33), calls=%async_computation.2 | async-start | bytes 1572864 | tf_op jit(solution)/shard_map/all_to_all | solution.py:162
  39.5 13.9 %all-to-all-start = ((bf16[4,48,2048]{2,1,0:T(8,128)(2,1)}), bf16[4,48,2048]{2,1,0:T(8,128)(2,1)S(1)}, u32[]{:S(2)}, u32[]{:S(2)}) async-start(bf16[4,48,2048]{2,1,0:T(8,128)(2,1)} %broadcast_select_fusion.1), calls=%async_computation | async-start | bytes 1572864 | tf_op jit(solution)/shard_map/all_to_all | solution.py:161
  55.1 25.3 %collective-permute-start = (bf16[2,64,2048]{2,1,0:T(8,128)(2,1)}, bf16[2,64,2048]{2,1,0:T(8,128)(2,1)S(1)}, u32[]{:S(2)}, u32[]{:S(2)}) collective-permute-start(bf16[2,64,2048]{2,1,0:T(8,128)(2,1)} %pad_maximum_fusion), channel_id=1, source_target_pairs={{0,16},{4,20},{8,24},{12,28},{16,0},{20,4},{24,8},{28,12},{1,17},{... | collective-permute-start | bytes 1572872 | tf_op jit(solution)/shard_map/ppermute | solution.py:16
  57.7 23.0 %collective-permute-start.1 = (bf16[2,64,2048]{2,1,0:T(8,128)(2,1)}, bf16[2,64,2048]{2,1,0:T(8,128)(2,1)S(1)}, u32[]{:S(2)}, u32[]{:S(2)}) collective-permute-start(bf16[2,64,2048]{2,1,0:T(8,128)(2,1)} %pad_maximum_fusion), channel_id=1, source_target_pairs={{0,8},{4,12},{8,0},{12,4},{16,24},{20,28},{24,16},{28,20},{1,9},{5... | collective-permute-start | bytes 1572872 | tf_op jit(solution)/shard_map/ppermute | solution.py:16
  59.3 21.4 %collective-permute-start.2 = (bf16[2,64,2048]{2,1,0:T(8,128)(2,1)}, bf16[2,64,2048]{2,1,0:T(8,128)(2,1)}, u32[]{:S(2)}, u32[]{:S(2)}) collective-permute-start(bf16[2,64,2048]{2,1,0:T(8,128)(2,1)} %pad_maximum_fusion), channel_id=1, source_target_pairs={{0,4},{4,0},{8,12},{12,8},{16,20},{20,16},{24,28},{28,24},{1,5},{5... | collective-permute-start | bytes 1572872 | tf_op jit(solution)/shard_map/ppermute | solution.py:16
  84.0 16.4 %slice-start.6 = ((s8[12582912]{0:T(1024)(128)(4,1)}), s8[4194304]{0:T(1024)(128)(4,1)S(1)}, s32[]{:S(2)}) async-start(s8[12582912]{0:T(1024)(128)(4,1)} %bitcast.178), calls=%async_computation.11 | async-start | bytes 8388608
  88.1 12.3 %slice-start.7 = ((s8[12582912]{0:T(1024)(128)(4,1)}), s8[4194304]{0:T(1024)(128)(4,1)S(1)}, s32[]{:S(2)}) async-start(s8[12582912]{0:T(1024)(128)(4,1)} %bitcast.178), calls=%async_computation.12 | async-start | bytes 8388608
  92.2 8.2 %slice-start.8 = ((s8[12582912]{0:T(1024)(128)(4,1)}), s8[4194304]{0:T(1024)(128)(4,1)S(1)}, s32[]{:S(2)}) async-start(s8[12582912]{0:T(1024)(128)(4,1)} %bitcast.178), calls=%async_computation.13 | async-start | bytes 8388608
  92.2 18.9 %slice-start = ((s8[25165824]{0:T(1024)(128)(4,1)}), s8[4194304]{0:T(1024)(128)(4,1)S(1)}, s32[]{:S(2)}) async-start(s8[25165824]{0:T(1024)(128)(4,1)} %bitcast.176), calls=%async_computation.5 | async-start | bytes 8388608
  96.3 14.8 %slice-start.1 = ((s8[25165824]{0:T(1024)(128)(4,1)}), s8[4194304]{0:T(1024)(128)(4,1)S(1)}, s32[]{:S(2)}) async-start(s8[25165824]{0:T(1024)(128)(4,1)} %bitcast.176), calls=%async_computation.6 | async-start | bytes 8388608
  100.4 10.7 %slice-start.2 = ((s8[25165824]{0:T(1024)(128)(4,1)}), s8[4194304]{0:T(1024)(128)(4,1)S(1)}, s32[]{:S(2)}) async-start(s8[25165824]{0:T(1024)(128)(4,1)} %bitcast.176), calls=%async_computation.7 | async-start | bytes 8388608
  102.1 9.0 %slice-start.3 = ((s8[25165824]{0:T(1024)(128)(4,1)}), s8[4194304]{0:T(1024)(128)(4,1)S(1)}, s32[]{:S(2)}) async-start(s8[25165824]{0:T(1024)(128)(4,1)} %bitcast.176), calls=%async_computation.8 | async-start | bytes 8388608
  103.8 7.4 %slice-start.4 = ((s8[25165824]{0:T(1024)(128)(4,1)}), s8[4194304]{0:T(1024)(128)(4,1)S(1)}, s32[]{:S(2)}) async-start(s8[25165824]{0:T(1024)(128)(4,1)} %bitcast.176), calls=%async_computation.9 | async-start | bytes 8388608
  105.5 5.7 %slice-start.5 = ((s8[25165824]{0:T(1024)(128)(4,1)}), s8[4194304]{0:T(1024)(128)(4,1)S(1)}, s32[]{:S(2)}) async-start(s8[25165824]{0:T(1024)(128)(4,1)} %bitcast.176), calls=%async_computation.10 | async-start | bytes 8388608
  120.7 25.2 %collective-permute-start.3 = (bf16[2,64,2048]{2,1,0:T(8,128)(2,1)S(1)}, bf16[2,64,2048]{2,1,0:T(8,128)(2,1)}, u32[]{:S(2)}, u32[]{:S(2)}) collective-permute-start(bf16[2,64,2048]{2,1,0:T(8,128)(2,1)S(1)} %pad_maximum_fusion.3), channel_id=1, source_target_pairs={{0,16},{4,20},{8,24},{12,28},{16,0},{20,4},{24,8},{28,12},{1,17},{... | collective-permute-start | bytes 1572872 | tf_op jit(solution)/shard_map/ppermute | solution.py:16
  122.3 23.7 %collective-permute-start.4 = (bf16[2,64,2048]{2,1,0:T(8,128)(2,1)S(1)}, bf16[2,64,2048]{2,1,0:T(8,128)(2,1)}, u32[]{:S(2)}, u32[]{:S(2)}) collective-permute-start(bf16[2,64,2048]{2,1,0:T(8,128)(2,1)S(1)} %pad_maximum_fusion.3), channel_id=1, source_target_pairs={{0,8},{4,12},{8,0},{12,4},{16,24},{20,28},{24,16},{28,20},{1,9},{5... | collective-permute-start | bytes 1572872 | tf_op jit(solution)/shard_map/ppermute | solution.py:16
  124.7 21.2 %collective-permute-start.5 = (bf16[2,64,2048]{2,1,0:T(8,128)(2,1)S(1)}, bf16[2,64,2048]{2,1,0:T(8,128)(2,1)}, u32[]{:S(2)}, u32[]{:S(2)}) collective-permute-start(bf16[2,64,2048]{2,1,0:T(8,128)(2,1)S(1)} %pad_maximum_fusion.3), channel_id=1, source_target_pairs={{0,4},{4,0},{8,12},{12,8},{16,20},{20,16},{24,28},{28,24},{1,5},{5... | collective-permute-start | bytes 1572872 | tf_op jit(solution)/shard_map/ppermute | solution.py:16
  163.2 11.6 %all-to-all-start.4 = ((bf16[4,48,2048]{2,1,0:T(8,128)(2,1)}), bf16[4,48,2048]{2,1,0:T(8,128)(2,1)S(1)}, u32[]{:S(2)}, u32[]{:S(2)}) async-start(bf16[4,48,2048]{2,1,0:T(8,128)(2,1)} %bitcast.56), calls=%async_computation.4 | async-start | bytes 1572864 | tf_op jit(solution)/shard_map/all_to_all | solution.py:193
where the time goes:
time: 178 us; the launch traced here: 177 us
  waiting for transfers between devices  49.3 us (28%)
  matrix products  34.6 us (19%)
  local copies, waits for them, and re-layouts  31 us (17%)
  starting transfers between devices  25.3 us (14%)
  other arithmetic  23.9 us (13%)
  blocking collectives  12.2 us (7%)
    ppermute x6, waiting for transfers between devices, swapped(): lax.ppermute(shard, axis, [(i, i ^ 1 << apart) for i in range(lax.axis_si...  38.3 us
    dot_general x4, matrix products, expert_rows(): both = jnp.dot(row_input, w_gate_up, preferred_element_type=jnp.float32)  16.3 us
    gather x16, local copies, waits for them, and re-layouts, pick_rows(): return jnp.take(table, index, axis=0, mode='fill', fill_value=0)  15.5 us
    all_to_all x1, blocking collectives, body(): lax.all_to_all(pool_out, 'expert', split_axis=0, concat_axis=0, tiled=True)  12.2 us
    ppermute x6, starting transfers between devices, swapped(): lax.ppermute(shard, axis, [(i, i ^ 1 << apart) for i in range(lax.axis_si...  8.21 us
    dot_general x4, matrix products, expert_rows(): lax.dot_general(d_both, w_gate_up, (((1,), (1,)), ((), ())), preferred_el...  7.69 us
    all_to_all x1, waiting for transfers between devices, body(): lax.all_to_all(send_tokens, 'expert', split_axis=0, concat_axis=0, tiled=...  6.72 us
    dot_general x4, matrix products, expert_rows(): lax.dot_general(hidden, w_down, (((1,), (1,)), ((), ())), preferred_eleme...  5.91 us
  transfers between devices with their start and end apart: 10, of which 6 were waited for; matrix products, arithmetic and copies ran while one was open for 22% of the time, Pallas kernels for 0%

commit v1 on v0

v1 whole, which is shorter than its diff:
```python
import functools
import jax
import jax.numpy as jnp
from jax import lax
from jax.experimental import pallas as pl
from jax.experimental.pallas import tpu as pltpu
from jax.sharding import PartitionSpec as P

TOPK = 8
EXPERTS = 16
OVF = 16
LANES = 128
CAP_AT = 2 * TOPK
LOW_AT = EXPERTS

VM = pltpu.VMEM


def swapped(shard, axis, mask):
    return lax.ppermute(shard, axis, [(i, i ^ mask) for i in range(lax.axis_size(axis))])


def lane_ids(rows):
    return lax.broadcasted_iota(jnp.int32, (rows, LANES), 1)


def side_tables(side, first_expert):
    rows = side.shape[0]
    lane = (lane_ids(rows) + first_expert).astype(jnp.float32)
    named = jnp.zeros((rows, LANES), jnp.float32)
    gate = jnp.zeros((rows, LANES), jnp.float32)
    for k in range(TOPK):
        hit = side[:, k : k + 1] == lane
        named = jnp.where(hit, 1.0, named)
        gate = jnp.where(hit, side[:, TOPK + k : TOPK + k + 1], gate)
    return named, gate


def spare_kernel(group_size, groups, info, *refs):
    pieces, out = refs[:-1], refs[-1]
    first_expert = info[0]
    out[...] = jnp.zeros_like(out)
    for g in range(groups):
        load = jnp.zeros((1, LANES), jnp.float32)
        for j in range(group_size):
            side = pieces[g * group_size + j][...].astype(jnp.float32)
            named, _ = side_tables(side, first_expert)
            load = load + jnp.sum(named, axis=0, keepdims=True)
        cap = cap_lanes(pieces[g * group_size][...])
        out[g : g + 1, :] = cap - jnp.minimum(load, cap)


def cap_lanes(side):
    return pltpu.roll(side.astype(jnp.float32), LANES - CAP_AT, 1)[0:1, :]


def expert_kernel(
    group_size, groups, width, levels, info, mask_ref, spare_ref, *refs
):
    far = refs[: len(levels)]
    refs = refs[len(levels) :]
    count = groups * group_size
    pieces = refs[:count]
    gate_up_hbm, down_hbm = refs[count : count + 2]
    outs = refs[count + 2 : count + 2 + groups]
    (tok, grd, side, gate_up, down, hid, dpre, acc_out, acc_grad, sems) = refs[count + 2 + groups :]
    first_expert, first_local, self_index = info[0], info[1], info[2]
    per_device, _, hidden_units = down.shape
    rows = tok.shape[0]
    piece_rows = rows // count
    group_rows = rows // groups
    step = 256
    steps = hidden_units // step

    def copies(i, j):
        cols = pl.ds(j * step, step)
        ups = pl.ds(hidden_units + j * step, step)
        return (
            pltpu.make_async_copy(gate_up_hbm.at[first_local + i, :, cols], gate_up.at[i, :, cols], sems.at[i, j, 0]),
            pltpu.make_async_copy(gate_up_hbm.at[first_local + i, :, ups], gate_up.at[i, :, ups], sems.at[i, j, 1]),
            pltpu.make_async_copy(down_hbm.at[first_local + i, :, cols], down.at[i, :, cols], sems.at[i, j, 2]),
        )

    for i in range(per_device):
        for j in range(steps):
            for copy in copies(i, j):
                copy.start()

    for n, piece in enumerate(pieces):
        at = pl.ds(n * piece_rows, piece_rows)
        tok[at, :] = piece[:, :width]
        grd[at, :] = piece[:, width : 2 * width]
        side[at, :] = piece[:, 2 * width :].astype(jnp.float32)

    named, gate = side_tables(side[...], first_expert)
    r_id = lax.broadcasted_iota(jnp.int32, (rows, rows), 0)
    c_id = lax.broadcasted_iota(jnp.int32, (rows, rows), 1)

    def order(v):
        block, inner = v // piece_rows, v % piece_rows
        grp, j = block // group_size, block % group_size
        return grp, (j ^ self_index) * piece_rows + inner

    r_grp, r_ord = order(r_id)
    c_grp, c_ord = order(c_id)
    earlier = ((r_grp == c_grp) & (c_ord < r_ord)).astype(jnp.bfloat16)
    place = jnp.dot(earlier, named.astype(jnp.bfloat16), preferred_element_type=jnp.float32)
    mask = mask_ref[...]
    row_grp = lax.broadcasted_iota(jnp.int32, (rows, LANES), 0) // group_rows
    limit = jnp.zeros((rows, LANES), jnp.float32)
    for g in range(groups):
        other = jnp.zeros((1, LANES), jnp.float32)
        if groups == 2:
            other = jnp.where(mask == 1, spare_ref[1 - g : 2 - g, :], other)
        for level, ref in zip(levels, far):
            other = jnp.where(mask == level, ref[g : g + 1, :], other)
        cap = cap_lanes(side[g * group_rows : g * group_rows + 8, :])
        limit = jnp.where(row_grp == g, cap + jnp.minimum(other, float(OVF)), limit)
    kept = jnp.where((named > 0.0) & (place < limit), 1.0, 0.0)

    acc_out[...] = jnp.zeros_like(acc_out)
    acc_grad[...] = jnp.zeros_like(acc_grad)
    lane = lane_ids(rows)

    def one_expert(i, gate_grads):
        here = lane == first_local + i
        keep = jnp.sum(jnp.where(here, kept, 0.0), axis=1, keepdims=True)
        weight = jnp.sum(jnp.where(here, gate, 0.0), axis=1, keepdims=True) * keep
        t, g = tok[...], grd[...]
        total = jnp.zeros((rows, 1), jnp.float32)
        for j in range(steps):
            for copy in copies(i, j):
                copy.wait()
            cols = pl.ds(j * step, step)
            ups = pl.ds(hidden_units + j * step, step)
            a = jnp.dot(t, gate_up[i, :, cols], preferred_element_type=jnp.float32)
            b = jnp.dot(t, gate_up[i, :, ups], preferred_element_type=jnp.float32)
            back = jnp.dot(g, down[i, :, cols], preferred_element_type=jnp.float32)
            s = jax.nn.sigmoid(a)
            swish = a * s
            hidden = swish * b
            total = total + jnp.sum(hidden * back, axis=1, keepdims=True)
            back = back * weight
            hid[:, cols] = (hidden * weight).astype(jnp.bfloat16)
            dpre[:, cols] = (back * b * s * (1.0 + a * (1.0 - s))).astype(jnp.bfloat16)
            dpre[:, ups] = (back * swish).astype(jnp.bfloat16)
        h, d = hid[...], dpre[...]
        wide = 512
        for j in range(width // wide):
            cols = pl.ds(j * wide, wide)
            acc_out[:, cols] += lax.dot_general(
                h, down[i, cols, :], (((1,), (1,)), ((), ())), preferred_element_type=jnp.float32
            )
            acc_grad[:, cols] += lax.dot_general(
                d, gate_up[i, cols, :], (((1,), (1,)), ((), ())), preferred_element_type=jnp.float32
            )
        total = total * keep
        high = total.astype(jnp.bfloat16).astype(jnp.float32)
        at = first_expert + first_local + i
        gate_grads = jnp.where(lane == at, high, gate_grads)
        return jnp.where(lane == at + LOW_AT, total - high, gate_grads)

    gate_grads = lax.fori_loop(0, per_device, one_expert, jnp.zeros((rows, LANES), jnp.float32))
    for g in range(groups):
        at = slice(g * group_rows, (g + 1) * group_rows)
        outs[g][:, :width] = acc_out[at, :].astype(jnp.bfloat16)
        outs[g][:, width : 2 * width] = acc_grad[at, :].astype(jnp.bfloat16)
        outs[g][:, 2 * width :] = gate_grads[at, :].astype(jnp.bfloat16)


def finish_kernel(width, *refs):
    parts, (routes, layer_out, input_grad, gate_grad) = refs[:-4], refs[-4:]

    def total(cols):
        out = parts[0][:, cols].astype(jnp.float32)
        for part in parts[1:]:
            out = out + part[:, cols].astype(jnp.float32)
        return out

    layer_out[...] = total(slice(0, width)).astype(jnp.bfloat16)
    input_grad[...] = total(slice(width, 2 * width)).astype(jnp.bfloat16)
    table = total(slice(2 * width, 2 * width + LANES))
    table = table + pltpu.roll(table, LANES - LOW_AT, 1)
    ids = routes[...]
    lane = lane_ids(ids.shape[0])
    out = jnp.zeros(ids.shape, jnp.float32)
    column = lax.broadcasted_iota(jnp.int32, ids.shape, 1)
    for k in range(TOPK):
        picked = jnp.sum(jnp.where(lane == ids[:, k : k + 1], table, 0.0), axis=1, keepdims=True)
        out = jnp.where(column == k, picked, out)
    gate_grad[...] = out


def body(tokens, grad_out, gate_probs, routes, capacity, pair_mask, gate_up_weight, down_weight):
    tok_count, width = tokens.shape
    local_count, _, hidden_units = down_weight.shape
    group_size = lax.axis_size("expert")
    replicas = lax.axis_size("dp")
    paired = local_count % 2 == 0 and replicas % 2 == 0
    groups = 2 if paired else 1
    per_device = local_count // groups
    me = lax.axis_index("expert")
    core = lax.axis_index("dp") % groups
    info = jnp.stack([me * local_count, core * per_device, me]).astype(jnp.int32)
    caps = jnp.broadcast_to(capacity.astype(jnp.bfloat16), (tok_count, local_count))
    side = jnp.concatenate([routes.astype(jnp.bfloat16), gate_probs, caps], axis=1)
    side = jnp.pad(side, ((0, 0), (0, LANES - side.shape[1])))
    payload = jnp.concatenate([tokens, grad_out, side], axis=1)
    mask_row = jnp.pad(pair_mask.reshape(1, local_count), ((0, 0), (0, LANES - local_count)))

    pieces = [payload] + [swapped(payload, "expert", k) for k in range(1, group_size)]
    if paired:
        pieces = pieces + [swapped(piece, "dp", 1) for piece in pieces]
    rows = len(pieces) * tok_count
    total_width = 2 * width + LANES

    side_spec = pl.BlockSpec((tok_count, LANES), lambda i: (0, 2 * width // LANES))
    spare = pl.pallas_call(
        functools.partial(spare_kernel, group_size, groups),
        out_shape=jax.ShapeDtypeStruct((8, LANES), jnp.float32),
        grid=(1,),
        in_specs=[pl.BlockSpec(memory_space=pltpu.SMEM)] + [side_spec] * len(pieces),
        out_specs=pl.BlockSpec((8, LANES), lambda i: (0, 0)),
        name="spare",
    )(info, *pieces)
    levels = [1 << b for b in range(groups - 1, replicas.bit_length() - 1)]
    far = [swapped(spare, "dp", level) for level in levels]

    vm, hbm = pl.BlockSpec(memory_space=VM), pl.BlockSpec(memory_space=pl.ANY)
    group_rows = rows // groups
    parts = pl.pallas_call(
        functools.partial(expert_kernel, group_size, groups, width, tuple(levels)),
        out_shape=[jax.ShapeDtypeStruct((group_rows, total_width), jnp.bfloat16)] * groups,
        in_specs=[pl.BlockSpec(memory_space=pltpu.SMEM), vm, vm]
        + [vm] * (len(far) + len(pieces))
        + [hbm, hbm],
        out_specs=[vm] * groups,
        scratch_shapes=[
            VM((rows, width), jnp.bfloat16),
            VM((rows, width), jnp.bfloat16),
            VM((rows, LANES), jnp.float32),
            VM((per_device, width, 2 * hidden_units), jnp.bfloat16),
            VM((per_device, width, hidden_units), jnp.bfloat16),
            VM((rows, hidden_units), jnp.bfloat16),
            VM((rows, 2 * hidden_units), jnp.bfloat16),
            VM((rows, width), jnp.float32),
            VM((rows, width), jnp.float32),
            pltpu.SemaphoreType.DMA((per_device, hidden_units // 256, 3)),
        ],
        name="experts",
    )(info, mask_row, spare, *far, *pieces, gate_up_weight, down_weight)
    if paired:
        other = swapped(parts[1], "dp", 1)
        summed = parts[0].astype(jnp.float32) + other.astype(jnp.float32)
        summed = summed.astype(jnp.bfloat16)
    else:
        summed = parts[0]
    blocks = summed.reshape(group_size, tok_count, total_width)
    mine = [blocks[0]] + [swapped(blocks[k], "expert", k) for k in range(1, group_size)]
    return tuple(
        pl.pallas_call(
            functools.partial(finish_kernel, width),
            out_shape=[
                jax.ShapeDtypeStruct((tok_count, width), jnp.bfloat16),
                jax.ShapeDtypeStruct((tok_count, width), jnp.bfloat16),
                jax.ShapeDtypeStruct((tok_count, TOPK), jnp.float32),
            ],
            in_specs=[vm] * (group_size + 1),
            out_specs=[vm] * 3,
            name="finish",
        )(*mine, routes)
    )


def solution(mesh):
    return jax.shard_map(
        body,
        mesh=mesh,
        in_specs=(
            P(("dp", "expert"), None),
            P(("dp", "expert"), None),
            P(("dp", "expert"), None),
            P(("dp", "expert"), None),
            P("dp", "expert"),
            P("expert"),
            P("expert", None, None),
            P("expert", None, None),
        ),
        out_specs=(P(("dp", "expert"), None), P(("dp", "expert"), None), P(("dp", "expert"), None)),
        check_vma=False,
    )
```

time: 178 us -> 59.5 us (0.33)
  matrix products: 34.6 us -> 0 us
  waiting for transfers between devices: 49.3 us -> 15.8 us
  local copies, waits for them, and re-layouts: 31 us -> 6.59 us
  other arithmetic: 23.9 us -> 4.1 us
  Pallas kernels: 0 us -> 19.1 us
  starting transfers between devices: 25.3 us -> 12.8 us
  blocking collectives: 12.2 us -> 0 us
    dot_general x16 -> x0, matrix products: 34.6 us -> none  [the longest x4 16.3 us: expert_rows(): both = jnp.dot(row_input, w_gate_up, preferred_element_type=jnp.float32)]
    gather x21 -> x0, local copies, waits for them, and re-layouts: 23 us -> none  [the longest x16 15.5 us: pick_rows(): return jnp.take(table, index, axis=0, mode='fill', fill_value=0)]
    ppermute x6 -> x13, waiting for transfers between devices: 38.3 us -> 15.8 us  [swapped(): lax.ppermute(shard, axis, [(i, i ^ mask) for i in range(lax.axis_size(axi...]
    pallas_call x0 -> x3, Pallas kernels: none -> 19.1 us  [the longest x1 15.3 us: body(): pl.pallas_call(functools.partial(expert_kernel, group_size, groups, width...]
    all_to_all x4 -> x0, starting transfers between devices: 17.1 us -> none  [the longest x1 5.19 us: body(): lax.all_to_all(counts.astype(jnp.bfloat16), 'expert', split_axis=0, conca...]
    all_to_all x1 -> x0, blocking collectives: 12.2 us -> none  [body(): lax.all_to_all(pool_out, 'expert', split_axis=0, concat_axis=0, tiled=True)]
    all_to_all x4 -> x0, waiting for transfers between devices: 11 us -> none  [the longest x1 6.72 us: body(): lax.all_to_all(send_tokens, 'expert', split_axis=0, concat_axis=0, tiled=...]
    select_n x9 -> x0, other arithmetic: 7.42 us -> none  [the longest x1 2.56 us: serve_rows(): home_from = jnp.full((local_count * cap_rows + 1,), pool_size, jnp.int32)...]
  transfers between devices with their start and end apart: 10 -> 13, of which waited for: 6 -> 9; matrix products, arithmetic and copies ran while one was open for 22% -> 3% of each run, Pallas kernels for 0% -> 0%
where the time goes in v1:
time: 59.5 us; the launch traced here: 59.1 us
  Pallas kernels  19.1 us (32%)
  waiting for transfers between devices  15.8 us (27%)
  starting transfers between devices  12.8 us (22%)
  local copies, waits for them, and re-layouts  6.59 us (11%)
  other arithmetic  4.1 us (7%)
  between operations  0.73 us (1%)
    ppermute x13, waiting for transfers between devices, swapped(): lax.ppermute(shard, axis, [(i, i ^ mask) for i in range(lax.axis_size(axi...  15.8 us
    pallas_call x1, Pallas kernels, body(): pl.pallas_call(functools.partial(expert_kernel, group_size, groups, width...  15.3 us
    ppermute x13, starting transfers between devices, swapped(): lax.ppermute(shard, axis, [(i, i ^ mask) for i in range(lax.axis_size(axi...  12.8 us
    unnamed x32, local copies, waits for them, and re-layouts  3.78 us
    pallas_call x1, Pallas kernels, body(): pl.pallas_call(functools.partial(finish_kernel, width), out_shape=[jax.Sh...  2.19 us
    pallas_call x1, Pallas kernels, body(): pl.pallas_call(functools.partial(spare_kernel, group_size, groups), out_s...  1.59 us
    pallas_call x1, local copies, waits for them, and re-layouts, body(): pl.pallas_call(functools.partial(finish_kernel, width), out_shape=[jax.Sh...  1.36 us
  transfers between devices with their start and end apart: 13, of which 9 were waited for; matrix products, arithmetic and copies ran while one was open for 3% of the time, Pallas kernels for 0%

profile of v1, /device:TPU:0, one launch (start us, length us, event | category | flops | bytes accessed | tf_op | source)
XLA Modules:
  0.0 59.1 jit_solution(14649422323859434905)
XLA Ops:
  0.6 0.7 %convert_element_type.17 = bf16[16,8]{0,1:T(8,128)(2,1)S(1)} convert(s32[16,8]{0,1:T(8,128)} %param.11) | non-fusion elementwise | flops 128 | bytes 768 | tf_op jit(solution)/shard_map/convert_element_type | solution.py:206
  1.4 0.8 %copy.16 = bf16[16,8]{1,0:T(8,128)(2,1)S(1)} copy(bf16[16,8]{0,1:T(8,128)(2,1)} %param.10) | data formatting | bytes 512 | tf_op args[2]
  2.2 0.7 %convert_bitcast_fusion = bf16[4]{0:T(256)(128)(2,1)S(1)} fusion(s32[1,4]{1,0:T(1,128)} %param.12), kind=kLoop, calls=%fused_computation.6 | loop fusion | flops 4 | bytes 24 | tf_op jit(solution)/shard_map/broadcast_in_dim | solution.py:205
  3.0 0.9 %fusion.1.refs_0_.refs_2_ = bf16[16,4224]{1,0:T(8,128)(2,1)S(1)} fusion(bf16[16,20]{1,0:T(8,128)(2,1)S(1)} %maximum_maximum_fusion, bf16[16,2048]{1,0:T(8,128)(2,1)} %param.9, bf16[16,2048]{1,0:T(8,128)(2,1)} %param.8), kind=kLoop, calls=%fused_computation.3 | loop fusion | flops 540672 | bytes 266880 | tf_op jit(solution)/shard_map/concatenate | solution.py:208
  3.9 3.0 %collective-permute-start = (bf16[16,4224]{1,0:T(8,128)(2,1)S(1)}, bf16[16,4224]{1,0:T(8,128)(2,1)S(1)}, u32[]{:S(2)}, u32[]{:S(2)}) collective-permute-start(bf16[16,4224]{1,0:T(8,128)(2,1)S(1)} %fusion.1.refs_0_.refs_2_), channel_id=1, source_target_pairs={{0,1},{1,0},{2,3},{3,2},{4,5},{5,4},{6,7},{7,6},{8,9},{9,8},{10,11... | collective-permute-start | bytes 405512 | tf_op jit(solution)/shard_map/ppermute | solution.py:20
  6.9 1.5 %collective-permute-start.1 = (bf16[16,4224]{1,0:T(8,128)(2,1)S(1)}, bf16[16,4224]{1,0:T(8,128)(2,1)S(1)}, u32[]{:S(2)}, u32[]{:S(2)}) collective-permute-start(bf16[16,4224]{1,0:T(8,128)(2,1)S(1)} %fusion.1.refs_0_.refs_2_), channel_id=1, source_target_pairs={{0,2},{1,3},{2,0},{3,1},{4,6},{5,7},{6,4},{7,5},{8,10},{9,11},{10,... | collective-permute-start | bytes 405512 | tf_op jit(solution)/shard_map/ppermute | solution.py:20
  8.5 2.4 %collective-permute-done.refs_1_.refs_3_ = bf16[16,4224]{1,0:T(8,128)(2,1)S(1)} collective-permute-done((bf16[16,4224]{1,0:T(8,128)(2,1)S(1)}, bf16[16,4224]{1,0:T(8,128)(2,1)S(1)}, u32[]{:S(2)}, u32[]{:S(2)}) %collective-permute-start) | collective-permute-done | bytes 135200 | tf_op jit(solution)/shard_map/ppermute | solution.py:20
  10.9 4.0 %collective-permute-done.1.refs_2_.refs_4_ = bf16[16,4224]{1,0:T(8,128)(2,1)S(1)} collective-permute-done((bf16[16,4224]{1,0:T(8,128)(2,1)S(1)}, bf16[16,4224]{1,0:T(8,128)(2,1)S(1)}, u32[]{:S(2)}, u32[]{:S(2)}) %collective-permute-start.1) | collective-permute-done | bytes 135200 | tf_op jit(solution)/shard_map/ppermute | solution.py:20
  17.5 1.6 %spare.1.spare_ref = f32[8,128]{1,0:T(8,128)} custom-call(s32[3]{0:T(128)} %pad_add_fusion.info, bf16[16,4224]{1,0:T(8,128)(2,1)} %copy-done, bf16[16,4224]{1,0:T(8,128)(2,1)} %copy-done.1, bf16[16,4224]{1,0:T(8,128)(2,1)} %copy-done.2, bf16[16,4224]{1,0:T(8,128)(2,1)} %copy-done.3, bf16[16,4224]{1,0:T(8,128)(2,1)} %copy-done.4, bf16[16,4224]{1,0:T(8,128)(2,1)} %copy-done.5, ...), custom_call_target="tpu_custom_call" | custom-call | tf_op jit(solution)/shard_map/spare/pallas_call | solution.py:218
  19.1 1.6 %collective-permute-start.7 = (f32[8,128]{1,0:T(8,128)}, f32[8,128]{1,0:T(8,128)S(1)}, u32[]{:S(2)}, u32[]{:S(2)}) collective-permute-start(f32[8,128]{1,0:T(8,128)} %spare.1.spare_ref), channel_id=1, source_target_pairs={{0,8},{4,12},{8,0},{12,4},{16,24},{20,28},{24,16},{28,20},{1,9},{5... | collective-permute-start | bytes 12296 | tf_op jit(solution)/shard_map/ppermute | solution.py:20
  20.7 2.6 %collective-permute-start.8 = (f32[8,128]{1,0:T(8,128)}, f32[8,128]{1,0:T(8,128)S(1)}, u32[]{:S(2)}, u32[]{:S(2)}) collective-permute-start(f32[8,128]{1,0:T(8,128)} %spare.1.spare_ref), channel_id=1, source_target_pairs={{0,16},{4,20},{8,24},{12,28},{16,0},{20,4},{24,8},{28,12},{1,17},{... | collective-permute-start | bytes 12296 | tf_op jit(solution)/shard_map/ppermute | solution.py:20
  23.9 1.5 %collective-permute-done.8.refs_1_ = f32[8,128]{1,0:T(8,128)S(1)} collective-permute-done((f32[8,128]{1,0:T(8,128)}, f32[8,128]{1,0:T(8,128)S(1)}, u32[]{:S(2)}, u32[]{:S(2)}) %collective-permute-start.8) | collective-permute-done | bytes 4128 | tf_op jit(solution)/shard_map/ppermute | solution.py:20
  26.0 15.3 %experts.1 = (bf16[64,4224]{1,0:T(8,128)(2,1)}, bf16[64,4224]{1,0:T(8,128)(2,1)}) custom-call(s32[3]{0:T(128)} %pad_add_fusion.info, s32[1,128]{1,0:T(1,128)} %pad.8.mask_ref, f32[8,128]{1,0:T(8,128)} %spare.1.spare_ref, f32[8,128]{1,0:T(8,128)} %copy-done.12, f32[8,128]{1,0:T(8,128)} %copy-done.13, bf16[16,4224]{1,0:T(8,128)(2,1)} %copy-done, ...), custom_call_target="tpu_custom_call" | custom-call | tf_op jit(solution)/shard_map/experts/pallas_call | solution.py:231
  41.4 2.1 %collective-permute-done.9 = bf16[64,4224]{1,0:T(8,128)(2,1)S(1)} collective-permute-done((bf16[64,4224]{1,0:T(8,128)(2,1)}, bf16[64,4224]{1,0:T(8,128)(2,1)S(1)}, u32[]{:S(2)}, u32[]{:S(2)}) %collective-permute-start.9) | collective-permute-done | bytes 540704 | tf_op jit(solution)/shard_map/ppermute | solution.py:20
  43.6 1.2 %add_convert_fusion = bf16[64,4224]{1,0:T(8,128)(2,1)S(1)} fusion(bf16[64,4224]{1,0:T(8,128)(2,1)S(1)} %collective-permute-done.9, bf16[64,4224]{1,0:T(8,128)(2,1)} %get-tuple-element.5), kind=kLoop, calls=%fused_computation | loop fusion | flops 1081344 | bytes 1622016 | tf_op jit(solution)/shard_map/convert_element_type | solution.py:255
  44.8 0.7 %fusion.2 = (bf16[16,4224]{1,0:T(8,128)(2,1)S(1)}, bf16[16,4224]{1,0:T(8,128)(2,1)S(1)}, bf16[16,4224]{1,0:T(8,128)(2,1)S(1)}, bf16[16,4224]{1,0:T(8,128)(2,1)}) fusion(bf16[64,4224]{1,0:T(8,128)(2,1)S(1)} %add_convert_fusion), kind=kLoop, calls=%fused_computation.7 | loop fusion | bytes 1081344 | tf_op jit(solution)/shard_map/slice | solution.py:259
  46.1 1.4 %collective-permute-start.11 = (bf16[16,4224]{1,0:T(8,128)(2,1)S(1)}, bf16[16,4224]{1,0:T(8,128)(2,1)S(1)}, u32[]{:S(2)}, u32[]{:S(2)}) collective-permute-start(bf16[16,4224]{1,0:T(8,128)(2,1)S(1)} %get-tuple-element.14), channel_id=1, source_target_pairs={{0,2},{1,3},{2,0},{3,1},{4,6},{5,7},{6,4},{7,5},{8,10},{9,11},{10,... | collective-permute-start | bytes 405512 | tf_op jit(solution)/shard_map/ppermute | solution.py:20
  47.5 1.4 %collective-permute-start.12 = (bf16[16,4224]{1,0:T(8,128)(2,1)S(1)}, bf16[16,4224]{1,0:T(8,128)(2,1)S(1)}, u32[]{:S(2)}, u32[]{:S(2)}) collective-permute-start(bf16[16,4224]{1,0:T(8,128)(2,1)S(1)} %get-tuple-element.13), channel_id=1, source_target_pairs={{0,3},{1,2},{2,1},{3,0},{4,7},{5,6},{6,5},{7,4},{8,11},{9,10},{10,... | collective-permute-start | bytes 405512 | tf_op jit(solution)/shard_map/ppermute | solution.py:20
  48.9 0.7 %copy.17.refs_4_ = s32[16,8]{1,0:T(8,128)} copy(s32[16,8]{0,1:T(8,128)S(1)} %copy-done.11) | data formatting | bytes 1024 | tf_op args[3]
  49.6 2.3 %collective-permute-done.10.refs_1_ = bf16[16,4224]{1,0:T(8,128)(2,1)S(1)} collective-permute-done((bf16[16,4224]{1,0:T(8,128)(2,1)S(1)}, bf16[16,4224]{1,0:T(8,128)(2,1)S(1)}, u32[]{:S(2)}, u32[]{:S(2)}) %collective-permute-start.10) | collective-permute-done | bytes 135200 | tf_op jit(solution)/shard_map/ppermute | solution.py:20
  51.9 1.4 %collective-permute-done.11.refs_2_ = bf16[16,4224]{1,0:T(8,128)(2,1)S(1)} collective-permute-done((bf16[16,4224]{1,0:T(8,128)(2,1)S(1)}, bf16[16,4224]{1,0:T(8,128)(2,1)S(1)}, u32[]{:S(2)}, u32[]{:S(2)}) %collective-permute-start.11) | collective-permute-done | bytes 135200 | tf_op jit(solution)/shard_map/ppermute | solution.py:20
  53.3 1.6 %collective-permute-done.12.refs_3_ = bf16[16,4224]{1,0:T(8,128)(2,1)S(1)} collective-permute-done((bf16[16,4224]{1,0:T(8,128)(2,1)S(1)}, bf16[16,4224]{1,0:T(8,128)(2,1)S(1)}, u32[]{:S(2)}, u32[]{:S(2)}) %collective-permute-start.12) | collective-permute-done | bytes 135200 | tf_op jit(solution)/shard_map/ppermute | solution.py:20
  55.6 2.2 %finish.1 = (bf16[16,2048]{1,0:T(8,128)(2,1)}, bf16[16,2048]{1,0:T(8,128)(2,1)}, f32[16,8]{1,0:T(8,128)}) custom-call(bf16[16,4224]{1,0:T(8,128)(2,1)} %get-tuple-element.16.refs_0_, bf16[16,4224]{1,0:T(8,128)(2,1)} %copy-done.8, bf16[16,4224]{1,0:T(8,128)(2,1)} %copy-done.9, bf16[16,4224]{1,0:T(8,128)(2,1)} %copy-done.10, s32[16,8]{1,0:T(8,128)} %copy.17.refs_4_), custom_call_target="tpu_custom_call" | custom-call | tf_op jit(solution)/shard_map/finish/pallas_call | solution.py:261
  57.8 1.4 %copy.18 = f32[16,8]{0,1:T(8,128)} copy(f32[16,8]{1,0:T(8,128)} %get-tuple-element.12) | data formatting | bytes 1024 | tf_op jit(solution)/shard_map/finish/pallas_call | solution.py:261
  (48 shorter events, 5.4 us)
Async XLA Ops:
  0.6 22.7 %copy-start.14 = (s32[4]{0:T(128)S(1)}, s32[4]{0:T(128)}, u32[]{:S(2)}) copy-start(s32[4]{0:T(128)} %param.13) | copy-start | bytes 52
  3.9 12.5 %copy-start = (bf16[16,4224]{1,0:T(8,128)(2,1)}, bf16[16,4224]{1,0:T(8,128)(2,1)S(1)}, u32[]{:S(2)}) copy-start(bf16[16,4224]{1,0:T(8,128)(2,1)S(1)} %fusion.1.refs_0_.refs_2_) | copy-start | bytes 405508
  3.9 7.0 %collective-permute-start = (bf16[16,4224]{1,0:T(8,128)(2,1)S(1)}, bf16[16,4224]{1,0:T(8,128)(2,1)S(1)}, u32[]{:S(2)}, u32[]{:S(2)}) collective-permute-start(bf16[16,4224]{1,0:T(8,128)(2,1)S(1)} %fusion.1.refs_0_.refs_2_), channel_id=1, source_target_pairs={{0,1},{1,0},{2,3},{3,2},{4,5},{5,4},{6,7},{7,6},{8,9},{9,8},{10,11... | collective-permute-start | bytes 405512 | tf_op jit(solution)/shard_map/ppermute | solution.py:20
  6.9 7.9 %collective-permute-start.1 = (bf16[16,4224]{1,0:T(8,128)(2,1)S(1)}, bf16[16,4224]{1,0:T(8,128)(2,1)S(1)}, u32[]{:S(2)}, u32[]{:S(2)}) collective-permute-start(bf16[16,4224]{1,0:T(8,128)(2,1)S(1)} %fusion.1.refs_0_.refs_2_), channel_id=1, source_target_pairs={{0,2},{1,3},{2,0},{3,1},{4,6},{5,7},{6,4},{7,5},{8,10},{9,11},{10,... | collective-permute-start | bytes 405512 | tf_op jit(solution)/shard_map/ppermute | solution.py:20
  8.4 6.4 %collective-permute-start.2 = (bf16[16,4224]{1,0:T(8,128)(2,1)S(1)}, bf16[16,4224]{1,0:T(8,128)(2,1)S(1)}, u32[]{:S(2)}, u32[]{:S(2)}) collective-permute-start(bf16[16,4224]{1,0:T(8,128)(2,1)S(1)} %fusion.1.refs_0_.refs_2_), channel_id=1, source_target_pairs={{0,3},{1,2},{2,1},{3,0},{4,7},{5,6},{6,5},{7,4},{8,11},{9,10},{10,... | collective-permute-start | bytes 405512 | tf_op jit(solution)/shard_map/ppermute | solution.py:20
  8.5 7.5 %collective-permute-start.3 = (bf16[16,4224]{1,0:T(8,128)(2,1)S(1)}, bf16[16,4224]{1,0:T(8,128)(2,1)S(1)}, u32[]{:S(2)}, u32[]{:S(2)}) collective-permute-start(bf16[16,4224]{1,0:T(8,128)(2,1)S(1)} %fusion.1.refs_0_.refs_2_), channel_id=1, source_target_pairs={{0,4},{4,0},{8,12},{12,8},{16,20},{20,16},{24,28},{28,24},{1,5},{5... | collective-permute-start | bytes 405512 | tf_op jit(solution)/shard_map/ppermute | solution.py:20
  10.9 5.5 %copy-start.1 = (bf16[16,4224]{1,0:T(8,128)(2,1)}, bf16[16,4224]{1,0:T(8,128)(2,1)S(1)}, u32[]{:S(2)}) copy-start(bf16[16,4224]{1,0:T(8,128)(2,1)S(1)} %collective-permute-done.refs_1_.refs_3_) | copy-start | bytes 405508
  10.9 5.1 %collective-permute-start.4 = (bf16[16,4224]{1,0:T(8,128)(2,1)S(1)}, bf16[16,4224]{1,0:T(8,128)(2,1)S(1)}, u32[]{:S(2)}, u32[]{:S(2)}) collective-permute-start(bf16[16,4224]{1,0:T(8,128)(2,1)S(1)} %collective-permute-done.refs_1_.refs_3_), channel_id=1, source_target_pairs={{0,4},{4,0},{8,12},{12,8},{16,20},{20,16},{24,28},{28,24},{1,5},{5... | collective-permute-start | bytes 405512 | tf_op jit(solution)/shard_map/ppermute | solution.py:20
  14.9 1.6 %copy-start.2 = (bf16[16,4224]{1,0:T(8,128)(2,1)}, bf16[16,4224]{1,0:T(8,128)(2,1)S(1)}, u32[]{:S(2)}) copy-start(bf16[16,4224]{1,0:T(8,128)(2,1)S(1)} %collective-permute-done.1.refs_2_.refs_4_) | copy-start | bytes 405508
  14.9 1.4 %collective-permute-start.5 = (bf16[16,4224]{1,0:T(8,128)(2,1)S(1)}, bf16[16,4224]{1,0:T(8,128)(2,1)S(1)}, u32[]{:S(2)}, u32[]{:S(2)}) collective-permute-start(bf16[16,4224]{1,0:T(8,128)(2,1)S(1)} %collective-permute-done.1.refs_2_.refs_4_), channel_id=1, source_target_pairs={{0,4},{4,0},{8,12},{12,8},{16,20},{20,16},{24,28},{28,24},{1,5},{5... | collective-permute-start | bytes 405512 | tf_op jit(solution)/shard_map/ppermute | solution.py:20
  14.9 1.6 %copy-start.3 = (bf16[16,4224]{1,0:T(8,128)(2,1)}, bf16[16,4224]{1,0:T(8,128)(2,1)S(1)}, u32[]{:S(2)}) copy-start(bf16[16,4224]{1,0:T(8,128)(2,1)S(1)} %collective-permute-done.2.refs_3_.refs_5_) | copy-start | bytes 405508
  14.9 1.5 %collective-permute-start.6 = (bf16[16,4224]{1,0:T(8,128)(2,1)S(1)}, bf16[16,4224]{1,0:T(8,128)(2,1)S(1)}, u32[]{:S(2)}, u32[]{:S(2)}) collective-permute-start(bf16[16,4224]{1,0:T(8,128)(2,1)S(1)} %collective-permute-done.2.refs_3_.refs_5_), channel_id=1, source_target_pairs={{0,4},{4,0},{8,12},{12,8},{16,20},{20,16},{24,28},{28,24},{1,5},{5... | collective-permute-start | bytes 405512 | tf_op jit(solution)/shard_map/ppermute | solution.py:20
  16.0 0.7 %copy-start.5 = (bf16[16,4224]{1,0:T(8,128)(2,1)}, bf16[16,4224]{1,0:T(8,128)(2,1)S(1)}, u32[]{:S(2)}) copy-start(bf16[16,4224]{1,0:T(8,128)(2,1)S(1)} %collective-permute-done.4.refs_5_.refs_7_) | copy-start | bytes 405508
  16.2 0.7 %copy-start.6 = (bf16[16,4224]{1,0:T(8,128)(2,1)}, bf16[16,4224]{1,0:T(8,128)(2,1)S(1)}, u32[]{:S(2)}) copy-start(bf16[16,4224]{1,0:T(8,128)(2,1)S(1)} %collective-permute-done.5.refs_6_.refs_8_) | copy-start | bytes 405508
  19.1 4.8 %collective-permute-start.7 = (f32[8,128]{1,0:T(8,128)}, f32[8,128]{1,0:T(8,128)S(1)}, u32[]{:S(2)}, u32[]{:S(2)}) collective-permute-start(f32[8,128]{1,0:T(8,128)} %spare.1.spare_ref), channel_id=1, source_target_pairs={{0,8},{4,12},{8,0},{12,4},{16,24},{20,28},{24,16},{28,20},{1,9},{5... | collective-permute-start | bytes 12296 | tf_op jit(solution)/shard_map/ppermute | solution.py:20
  20.7 4.7 %collective-permute-start.8 = (f32[8,128]{1,0:T(8,128)}, f32[8,128]{1,0:T(8,128)S(1)}, u32[]{:S(2)}, u32[]{:S(2)}) collective-permute-start(f32[8,128]{1,0:T(8,128)} %spare.1.spare_ref), channel_id=1, source_target_pairs={{0,16},{4,20},{8,24},{12,28},{16,0},{20,4},{24,8},{28,12},{1,17},{... | collective-permute-start | bytes 12296 | tf_op jit(solution)/shard_map/ppermute | solution.py:20
  23.9 1.5 %copy-start.12 = (f32[8,128]{1,0:T(8,128)}, f32[8,128]{1,0:T(8,128)S(1)}, u32[]{:S(2)}) copy-start(f32[8,128]{1,0:T(8,128)S(1)} %collective-permute-done.7.refs_0_) | copy-start | bytes 12292
  41.4 2.2 %collective-permute-start.9 = (bf16[64,4224]{1,0:T(8,128)(2,1)}, bf16[64,4224]{1,0:T(8,128)(2,1)S(1)}, u32[]{:S(2)}, u32[]{:S(2)}) collective-permute-start(bf16[64,4224]{1,0:T(8,128)(2,1)} %get-tuple-element.6), channel_id=1, source_target_pairs={{0,4},{4,0},{8,12},{12,8},{16,20},{20,16},{24,28},{28,24},{1,5},{5... | collective-permute-start | bytes 1622024 | tf_op jit(solution)/shard_map/ppermute | solution.py:20
  43.6 5.4 %copy-start.11 = (s32[16,8]{0,1:T(8,128)S(1)}, s32[16,8]{0,1:T(8,128)}, u32[]{:S(2)}) copy-start(s32[16,8]{0,1:T(8,128)} %param.11) | copy-start | bytes 1540
  45.4 6.5 %collective-permute-start.10 = (bf16[16,4224]{1,0:T(8,128)(2,1)S(1)}, bf16[16,4224]{1,0:T(8,128)(2,1)S(1)}, u32[]{:S(2)}, u32[]{:S(2)}) collective-permute-start(bf16[16,4224]{1,0:T(8,128)(2,1)S(1)} %get-tuple-element.15), channel_id=1, source_target_pairs={{0,1},{1,0},{2,3},{3,2},{4,5},{5,4},{6,7},{7,6},{8,9},{9,8},{10,11... | collective-permute-start | bytes 405512 | tf_op jit(solution)/shard_map/ppermute | solution.py:20
  46.1 7.2 %collective-permute-start.11 = (bf16[16,4224]{1,0:T(8,128)(2,1)S(1)}, bf16[16,4224]{1,0:T(8,128)(2,1)S(1)}, u32[]{:S(2)}, u32[]{:S(2)}) collective-permute-start(bf16[16,4224]{1,0:T(8,128)(2,1)S(1)} %get-tuple-element.14), channel_id=1, source_target_pairs={{0,2},{1,3},{2,0},{3,1},{4,6},{5,7},{6,4},{7,5},{8,10},{9,11},{10,... | collective-permute-start | bytes 405512 | tf_op jit(solution)/shard_map/ppermute | solution.py:20
  47.5 7.4 %collective-permute-start.12 = (bf16[16,4224]{1,0:T(8,128)(2,1)S(1)}, bf16[16,4224]{1,0:T(8,128)(2,1)S(1)}, u32[]{:S(2)}, u32[]{:S(2)}) collective-permute-start(bf16[16,4224]{1,0:T(8,128)(2,1)S(1)} %get-tuple-element.13), channel_id=1, source_target_pairs={{0,3},{1,2},{2,1},{3,0},{4,7},{5,6},{6,5},{7,4},{8,11},{9,10},{10,... | collective-permute-start | bytes 405512 | tf_op jit(solution)/shard_map/ppermute | solution.py:20
  51.9 3.0 %copy-start.8 = (bf16[16,4224]{1,0:T(8,128)(2,1)}, bf16[16,4224]{1,0:T(8,128)(2,1)S(1)}, u32[]{:S(2)}) copy-start(bf16[16,4224]{1,0:T(8,128)(2,1)S(1)} %collective-permute-done.10.refs_1_) | copy-start | bytes 405508
  53.3 1.6 %copy-start.9 = (bf16[16,4224]{1,0:T(8,128)(2,1)}, bf16[16,4224]{1,0:T(8,128)(2,1)S(1)}, u32[]{:S(2)}) copy-start(bf16[16,4224]{1,0:T(8,128)(2,1)S(1)} %collective-permute-done.11.refs_2_) | copy-start | bytes 405508
  (4 other events, 2.5 us)

commit v2 on v1

v2 whole, which is shorter than its diff:
```python
import functools
import jax
import jax.numpy as jnp
from jax import lax
from jax.experimental import pallas as pl
from jax.experimental.pallas import tpu as pltpu
from jax.sharding import PartitionSpec as P

TOPK = 8
EXPERTS = 16
OVF = 16
LANES = 128
SUB = 8
STEP = 256
WIDE = 512
MIB = 1 << 20
LURE = 20_000_000_000

VM = pltpu.VMEM


def swapped(shard, axis, mask):
    return lax.ppermute(shard, axis, [(i, i ^ mask) for i in range(lax.axis_size(axis))])


def iota(shape, axis):
    return lax.broadcasted_iota(jnp.int32, shape, axis)


def place_of(groups, local_count):
    core = lax.axis_index("dp") % groups
    return lax.axis_index("expert") * local_count, core * (local_count // groups)


def prep_kernel(tokens, routes_t, gates_t, capacity, out, side):
    width = tokens.shape[1]
    tok_count = routes_t.shape[1]
    out[:, :width] = tokens[...]
    side[...] = jnp.zeros_like(side)
    side[:TOPK, :tok_count] = routes_t[...].astype(jnp.float32)
    side[TOPK : 2 * TOPK, :tok_count] = gates_t[...].astype(jnp.float32)
    block = side[...]
    row, lane = iota(block.shape, 0), iota(block.shape, 1)
    for l in range(capacity.shape[1]):
        block = jnp.where((lane == tok_count) & (row == l), capacity[0, l].astype(jnp.float32), block)
    out[:, width:] = block.astype(jnp.bfloat16)


def tables_kernel(group_size, groups, local_count, tok_count, *refs):
    pieces, (spare, named_t, place_t, gate_t, cap_t) = refs[:-5], refs[-5:]
    first_expert, _ = place_of(groups, local_count)
    self_index = lax.axis_index("expert")
    rows = tok_count * len(pieces)
    per_lanes = LANES // tok_count
    lane = iota((2 * TOPK, LANES), 1)
    columns = []
    for q in range(rows // LANES):
        acc = jnp.zeros((2 * TOPK, LANES), jnp.float32)
        for n in range(per_lanes):
            side = pieces[q * per_lanes + n][: 2 * TOPK, :].astype(jnp.float32)
            moved = pltpu.roll(side, n * tok_count, 1) if n else side
            acc = jnp.where(lane // tok_count == n, moved, acc)
        columns.append(acc)
    both = jnp.concatenate(columns, axis=1) if len(columns) > 1 else columns[0]
    routes, gates = both[:TOPK], both[TOPK:]
    sub = iota((SUB, rows), 0)
    named = jnp.zeros((SUB, rows), jnp.float32)
    gate = jnp.zeros((SUB, rows), jnp.float32)
    for l in range(local_count):
        hit = routes == (first_expert + l).astype(jnp.float32)
        here = sub == l
        named = jnp.where(here, jnp.max(jnp.where(hit, 1.0, 0.0), axis=0, keepdims=True), named)
        gate = jnp.where(here, jnp.sum(jnp.where(hit, gates, 0.0), axis=0, keepdims=True), gate)

    def order(v):
        block, inner = v // tok_count, v % tok_count
        return block // group_size, ((block % group_size) ^ self_index) * tok_count + inner

    u_grp, u_ord = order(iota((rows, rows), 0))
    t_grp, t_ord = order(iota((rows, rows), 1))
    earlier = ((u_grp == t_grp) & (u_ord < t_ord)).astype(jnp.bfloat16)
    named_t[...] = named
    gate_t[...] = gate
    place_t[...] = jnp.dot(named.astype(jnp.bfloat16), earlier, preferred_element_type=jnp.float32)
    group_of = iota((SUB, rows), 1) // (rows // groups)
    lane8 = iota((SUB, LANES), 1)
    spares = jnp.zeros((SUB, LANES), jnp.float32)
    caps = jnp.zeros((SUB, LANES), jnp.float32)
    for g in range(groups):
        load = jnp.sum(jnp.where(group_of == g, named, 0.0), axis=1, keepdims=True)
        cap = pieces[g * group_size][...].astype(jnp.float32)[:SUB, tok_count : tok_count + 1]
        caps = jnp.where(lane8 == g, cap, caps)
        spares = jnp.where(lane8 == g, cap - jnp.minimum(load, cap), spares)
    spare[...] = spares
    cap_t[...] = caps


def to_columns(table, rows):
    full = jnp.concatenate([table, jnp.zeros((LANES - SUB, rows), jnp.float32)], axis=0)
    return jnp.transpose(full)


def lane_of(columns, index):
    return jnp.sum(jnp.where(iota(columns.shape, 1) == index, columns, 0.0), axis=1, keepdims=True)


def first_kernel(groups, local_count, count, width, *refs):
    toks, grds = refs[:count], refs[count : 2 * count]
    gate_t, gate_up, down, hid, dpre, grads, tok, grd = refs[2 * count :]
    first_expert, first_local = place_of(groups, local_count)
    rows = tok.shape[0]
    piece_rows = rows // count
    hidden_units = down.shape[2]
    for n in range(count):
        at = pl.ds(n * piece_rows, piece_rows)
        tok[at, :] = toks[n][:, :width]
        grd[at, :] = grds[n][...]
    gates = to_columns(gate_t[...], rows)
    lane = iota((rows, LANES), 1)

    def one_expert(i, gate_grads):
        e = first_local + i
        weight = lane_of(gates, e)
        t, g = tok[...], grd[...]
        total = jnp.zeros((rows, 1), jnp.float32)
        for j in range(hidden_units // STEP):
            cols = pl.ds(j * STEP, STEP)
            ups = pl.ds(hidden_units + j * STEP, STEP)
            a = jnp.dot(t, gate_up[e, :, cols], preferred_element_type=jnp.float32)
            b = jnp.dot(t, gate_up[e, :, ups], preferred_element_type=jnp.float32)
            back = jnp.dot(g, down[e, :, cols], preferred_element_type=jnp.float32)
            s = jax.nn.sigmoid(a)
            swish = a * s
            hidden = swish * b
            total = total + jnp.sum(hidden * back, axis=1, keepdims=True)
            back = back * weight
            hid[i, :, cols] = (hidden * weight).astype(jnp.bfloat16)
            dpre[i, :, cols] = (back * b * s * (1.0 + a * (1.0 - s))).astype(jnp.bfloat16)
            dpre[i, :, ups] = (back * swish).astype(jnp.bfloat16)
        return jnp.where(lane == e, total, gate_grads)

    grads[...] = lax.fori_loop(0, local_count // groups, one_expert, jnp.zeros((rows, LANES), jnp.float32))


def second_kernel(groups, local_count, width, levels, mask_ref, *refs):
    far = refs[: len(levels)]
    (spare, named_t, place_t, cap_t, hid, dpre, grads, gate_up, down) = refs[len(levels) : len(levels) + 9]
    outs = refs[len(levels) + 9 : len(levels) + 9 + groups]
    acc_out, acc_grad = refs[len(levels) + 9 + groups :]
    first_expert, first_local = place_of(groups, local_count)
    rows = acc_out.shape[0]
    group_rows = rows // groups
    sub = iota((SUB, 1), 0)
    mask = jnp.zeros((SUB, 1), jnp.int32)
    for l in range(local_count):
        mask = jnp.where(sub == l, mask_ref[l], mask)
    group_of = iota((SUB, rows), 1) // group_rows
    limit = jnp.zeros((SUB, rows), jnp.float32)
    for g in range(groups):
        other = jnp.zeros((SUB, 1), jnp.float32)
        if groups == 2:
            other = jnp.where(mask == 1, spare[:, 1 - g : 2 - g], other)
        for level, ref in zip(levels, far):
            other = jnp.where(mask == level, ref[:, g : g + 1], other)
        limit = jnp.where(group_of == g, cap_t[:, g : g + 1] + jnp.minimum(other, float(OVF)), limit)
    kept = jnp.where((named_t[...] > 0.0) & (place_t[...] < limit), 1.0, 0.0)
    kept = to_columns(kept, rows)
    acc_out[...] = jnp.zeros_like(acc_out)
    acc_grad[...] = jnp.zeros_like(acc_grad)

    def one_expert(i, _):
        e = first_local + i
        keep = lane_of(kept, e) > 0.0
        h = jnp.where(keep, hid[i].astype(jnp.float32), 0.0).astype(jnp.bfloat16)
        d = jnp.where(keep, dpre[i].astype(jnp.float32), 0.0).astype(jnp.bfloat16)
        for j in range(width // WIDE):
            cols = pl.ds(j * WIDE, WIDE)
            acc_out[:, cols] += lax.dot_general(
                h, down[e, cols, :], (((1,), (1,)), ((), ())), preferred_element_type=jnp.float32
            )
            acc_grad[:, cols] += lax.dot_general(
                d, gate_up[e, cols, :], (((1,), (1,)), ((), ())), preferred_element_type=jnp.float32
            )
        return _

    lax.fori_loop(0, local_count // groups, one_expert, 0)
    value = jnp.where(kept > 0.0, grads[...], 0.0)
    high = value.astype(jnp.bfloat16).astype(jnp.float32)
    high_at = pltpu.roll(high, first_expert, 1)
    low_at = pltpu.roll(value - high, first_expert + EXPERTS, 1)
    table = high_at + low_at
    for g in range(groups):
        at = slice(g * group_rows, (g + 1) * group_rows)
        outs[g][:, :width] = acc_out[at, :].astype(jnp.bfloat16)
        outs[g][:, width : 2 * width] = acc_grad[at, :].astype(jnp.bfloat16)
        outs[g][:, 2 * width :] = table[at, :].astype(jnp.bfloat16)


def experts_kernel(groups, local_count, count, width, levels, mask_ref, *refs):
    n = len(levels)
    far, refs = refs[:n], refs[n:]
    (spare, named_t, place_t, cap_t, gate_t), refs = refs[:5], refs[5:]
    pieces, refs = refs[: 2 * count], refs[2 * count :]
    (gate_up, down), refs = refs[:2], refs[2:]
    outs, (tok, grd, hid, dpre, grads, acc_out, acc_grad) = refs[:groups], refs[groups:]
    first_kernel(groups, local_count, count, width, *pieces, gate_t, gate_up, down, hid, dpre, grads, tok, grd)
    second_kernel(
        groups, local_count, width, levels, mask_ref,
        *far, spare, named_t, place_t, cap_t, hid, dpre, grads, gate_up, down, *outs, acc_out, acc_grad,
    )


def join_kernel(own, other, *outs):
    rows = outs[0].shape[0]
    for n, out in enumerate(outs):
        at = slice(n * rows, (n + 1) * rows)
        out[...] = (own[at, :].astype(jnp.float32) + other[at, :].astype(jnp.float32)).astype(out.dtype)


def finish_kernel(width, *refs):
    parts, (routes_t, layer_out, input_grad, gate_grad_t) = refs[:-4], refs[-4:]

    def total(cols):
        out = parts[0][:, cols].astype(jnp.float32)
        for part in parts[1:]:
            out = out + part[:, cols].astype(jnp.float32)
        return out

    layer_out[...] = total(slice(0, width)).astype(jnp.bfloat16)
    input_grad[...] = total(slice(width, 2 * width)).astype(jnp.bfloat16)
    table = total(slice(2 * width, 2 * width + LANES))
    tok_count = table.shape[0]
    table = jnp.concatenate([table, jnp.zeros((LANES - tok_count, LANES), jnp.float32)], axis=0)
    by_expert = jnp.transpose(table)[:, :tok_count]
    ids = routes_t[...]
    out = jnp.zeros(ids.shape, jnp.float32)
    for e in range(EXPERTS):
        value = by_expert[e : e + 1, :] + by_expert[EXPERTS + e : EXPERTS + e + 1, :]
        out = jnp.where(ids == e, value, out)
    gate_grad_t[...] = out


def kernel(body, name, out_shape, in_specs, scratch=(), limit=4, flops=0):
    vm = pl.BlockSpec(memory_space=VM)
    return pl.pallas_call(
        body,
        out_shape=out_shape,
        in_specs=in_specs,
        out_specs=jax.tree.map(lambda _: vm, out_shape),
        scratch_shapes=scratch,
        compiler_params=pltpu.CompilerParams(vmem_limit_bytes=limit * MIB),
        cost_estimate=pl.CostEstimate(flops=flops, bytes_accessed=0, transcendentals=0) if flops else None,
        name=name,
    )


def body(tokens, grad_out, gate_probs, routes, capacity, pair_mask, gate_up_weight, down_weight):
    tok_count, width = tokens.shape
    local_count, _, hidden_units = down_weight.shape
    group_size = lax.axis_size("expert")
    replicas = lax.axis_size("dp")
    groups = 2 if local_count % 2 == 0 and replicas % 2 == 0 else 1
    per_device = local_count // groups
    bf16, f32 = jnp.bfloat16, jnp.float32
    vm, sm = pl.BlockSpec(memory_space=VM), pl.BlockSpec(memory_space=pltpu.SMEM)
    array = jax.ShapeDtypeStruct
    routes_t = routes.T
    gate_up = pltpu.with_memory_space_constraint(gate_up_weight, VM)
    down = pltpu.with_memory_space_constraint(down_weight, VM)

    packed = kernel(
        prep_kernel,
        "prep",
        array((tok_count, width + LANES), bf16),
        [vm, vm, vm, sm],
        [VM((tok_count, LANES), f32)],
        flops=LURE,
    )(tokens, routes_t, gate_probs.T, capacity)

    def gathered(piece):
        pieces = [piece] + [swapped(piece, "expert", k) for k in range(1, group_size)]
        return pieces + [swapped(p, "dp", 1) for p in pieces] if groups == 2 else pieces

    toks = gathered(packed)
    grds = gathered(grad_out)
    count = len(toks)
    rows = count * tok_count
    total_width = 2 * width + LANES

    side_spec = pl.BlockSpec((tok_count, LANES), lambda i: (0, width // LANES))
    small, wide = array((SUB, LANES), f32), array((SUB, rows), f32)
    spare, named_t, place_t, gate_t, cap_t = pl.pallas_call(
        functools.partial(tables_kernel, group_size, groups, local_count, tok_count),
        out_shape=[small, wide, wide, wide, small],
        grid=(1,),
        in_specs=[side_spec] * count,
        out_specs=[pl.BlockSpec((SUB, s.shape[1]), lambda i: (0, 0)) for s in (small, wide, wide, wide, small)],
        compiler_params=pltpu.CompilerParams(vmem_limit_bytes=4 * MIB),
        name="tables",
    )(*toks)
    levels = tuple(1 << b for b in range(groups - 1, replicas.bit_length() - 1))
    far = [swapped(spare, "dp", level) for level in levels]

    group_rows = rows // groups
    parts = kernel(
        functools.partial(experts_kernel, groups, local_count, count, width, levels),
        "experts",
        [array((group_rows, total_width), bf16)] * groups,
        [sm] + [vm] * (len(far) + 7 + 2 * count),
        [
            VM((rows, width), bf16),
            VM((rows, width), bf16),
            VM((per_device, rows, hidden_units), bf16),
            VM((per_device, rows, 2 * hidden_units), bf16),
            VM((rows, LANES), f32),
            VM((rows, width), f32),
            VM((rows, width), f32),
        ],
        12,
    )(pair_mask, *far, spare, named_t, place_t, cap_t, gate_t, *toks, *grds, gate_up, down)
    block = array((tok_count, total_width), bf16)
    if groups == 2:
        other = swapped(parts[1], "dp", 1)
        blocks = kernel(join_kernel, "join", [block] * group_size, [vm, vm])(parts[0], other)
    else:
        blocks = [parts[0][k * tok_count : (k + 1) * tok_count] for k in range(group_size)]
    mine = [blocks[0]] + [swapped(blocks[k], "expert", k) for k in range(1, group_size)]
    layer_out, input_grad, gate_grad_t = kernel(
        functools.partial(finish_kernel, width),
        "finish",
        [array((tok_count, width), bf16), array((tok_count, width), bf16), array((TOPK, tok_count), f32)],
        [vm] * (group_size + 1),
    )(*mine, routes_t)
    return layer_out, input_grad, gate_grad_t.T


def solution(mesh):
    return jax.shard_map(
        body,
        mesh=mesh,
        in_specs=(
            P(("dp", "expert"), None),
            P(("dp", "expert"), None),
            P(("dp", "expert"), None),
            P(("dp", "expert"), None),
            P("dp", "expert"),
            P("expert"),
            P("expert", None, None),
            P("expert", None, None),
        ),
        out_specs=(P(("dp", "expert"), None), P(("dp", "expert"), None), P(("dp", "expert"), None)),
        check_vma=False,
    )
```

time: 59.5 us -> 49.9 us (0.84)
  Pallas kernels: 19.1 us -> 12.1 us
  starting transfers between devices: 12.8 us -> 18.7 us
  other arithmetic: 4.1 us -> 0 us
  local copies, waits for them, and re-layouts: 6.59 us -> 2.88 us
    pallas_call x3 -> x5, Pallas kernels: 19.1 us -> 12.1 us  [the longest x1 10.4 us: body(): kernel(functools.partial(experts_kernel, groups, local_count, count, widt...]
    ppermute x13 -> x20, starting transfers between devices: 12.8 us -> 18.7 us  [swapped(): lax.ppermute(shard, axis, [(i, i ^ mask) for i in range(lax.axis_size(axi...]
    convert_element_type x2 -> x0, other arithmetic: 1.88 us -> none  [the longest x1 1.19 us: body(): summed = summed.astype(jnp.bfloat16)]
    pallas_call x1 -> x0, local copies, waits for them, and re-layouts: 1.36 us -> none  [body(): pl.pallas_call(functools.partial(finish_kernel, width), out_shape=[jax.Sh...]
    concatenate x2 -> x0, other arithmetic: 0.96 us -> none  [the longest x1 0.88 us: body(): payload = jnp.concatenate([tokens, grad_out, side], axis=1)]
    unnamed x32 -> x18, local copies, waits for them, and re-layouts: 3.78 us -> 2.88 us
    slice x1 -> x0, local copies, waits for them, and re-layouts: 0.69 us -> none  [body(): blocks[k]]
    broadcast_in_dim x1 -> x0, other arithmetic: 0.66 us -> none  [body(): jnp.broadcast_to(capacity.astype(jnp.bfloat16), (tok_count, local_count))]
  transfers between devices with their start and end apart: 13 -> 20, of which waited for: 9 -> 7; matrix products, arithmetic and copies ran while one was open for 3% -> 0% of each run, Pallas kernels for 0% -> 0%
where the time goes in v2:
time: 49.9 us; the launch traced here: 49.6 us
  starting transfers between devices  18.7 us (37%)
  waiting for transfers between devices  15.3 us (31%)
  Pallas kernels  12.1 us (24%)
  local copies, waits for them, and re-layouts  2.88 us (6%)
  between operations  0.71 us (1%)
    ppermute x20, starting transfers between devices, swapped(): lax.ppermute(shard, axis, [(i, i ^ mask) for i in range(lax.axis_size(axi...  18.7 us
    ppermute x20, waiting for transfers between devices, swapped(): lax.ppermute(shard, axis, [(i, i ^ mask) for i in range(lax.axis_size(axi...  15.3 us
    pallas_call x1, Pallas kernels, body(): kernel(functools.partial(experts_kernel, groups, local_count, count, widt...  10.4 us
    unnamed x18, local copies, waits for them, and re-layouts  2.88 us
  transfers between devices with their start and end apart: 20, of which 7 were waited for; matrix products, arithmetic and copies ran while one was open for 0% of the time, Pallas kernels for 0%

profile of v2, /device:TPU:0, one launch (start us, length us, event | category | flops | bytes accessed | tf_op | source)
XLA Modules:
  0.0 49.6 jit_solution(13568206814788367548)
XLA Ops:
  0.6 0.7 %copy-done.3 = s32[16,8]{0,1:T(8,128)S(1)} copy-done((s32[16,8]{0,1:T(8,128)S(1)}, s32[16,8]{0,1:T(8,128)}, u32[]{:S(2)}) %copy-start.3) | copy-done | bytes 536
  1.3 0.8 %copy-done.6 = bf16[16,2048]{1,0:T(8,128)(2,1)S(1)} copy-done((bf16[16,2048]{1,0:T(8,128)(2,1)S(1)}, bf16[16,2048]{1,0:T(8,128)(2,1)}, u32[]{:S(2)}) %copy-start.6) | copy-done | bytes 65560
  2.2 0.7 %copy-done.7 = bf16[16,8]{0,1:T(8,128)(2,1)S(1)} copy-done((bf16[16,8]{0,1:T(8,128)(2,1)S(1)}, bf16[16,8]{0,1:T(8,128)(2,1)}, u32[]{:S(2)}) %copy-start.7) | copy-done | bytes 280
  2.8 0.7 %copy-done.8 = s32[1,4]{1,0:T(1,128)S(1)} copy-done((s32[1,4]{1,0:T(1,128)S(1)}, s32[1,4]{1,0:T(1,128)}, u32[]{:S(2)}) %copy-start.8) | copy-done | bytes 40
  3.5 0.6 %prep.1.refs_0_.refs_7_ = bf16[16,2176]{1,0:T(8,128)(2,1)S(1)} custom-call(bf16[16,2048]{1,0:T(8,128)(2,1)S(1)} %copy-done.6, s32[8,16]{1,0:T(8,128)S(1)} %bitcast.3, bf16[8,16]{1,0:T(8,128)(2,1)S(1)} %bitcast.5, s32[1,4]{1,0:T(1,128)S(1)} %copy-done.8), custom_call_target="tpu_custom_call" | custom-call | flops 20000000000 | tf_op jit(solution)/shard_map/prep/pallas_call | solution.py:271
  4.1 4.0 %collective-permute-start.2 = (bf16[16,2176]{1,0:T(8,128)(2,1)S(1)}, bf16[16,2176]{1,0:T(8,128)(2,1)S(1)}, u32[]{:S(2)}, u32[]{:S(2)}) collective-permute-start(bf16[16,2176]{1,0:T(8,128)(2,1)S(1)} %prep.1.refs_0_.refs_7_), channel_id=1, source_target_pairs={{0,3},{1,2},{2,1},{3,0},{4,7},{5,6},{6,5},{7,4},{8,11},{9,10},{10,... | collective-permute-start | bytes 208904 | tf_op jit(solution)/shard_map/ppermute | solution.py:23
  8.6 1.5 %collective-permute-start.11 = (bf16[16,2048]{1,0:T(8,128)(2,1)S(1)}, bf16[16,2048]{1,0:T(8,128)(2,1)S(1)}, u32[]{:S(2)}, u32[]{:S(2)}) collective-permute-start(bf16[16,2048]{1,0:T(8,128)(2,1)S(1)} %copy-done.2), channel_id=1, source_target_pairs={{0,3},{1,2},{2,1},{3,0},{4,7},{5,6},{6,5},{7,4},{8,11},{9,10},{10,... | collective-permute-start | bytes 196616 | tf_op jit(solution)/shard_map/ppermute | solution.py:23
  10.2 1.9 %collective-permute-start = (bf16[16,2176]{1,0:T(8,128)(2,1)S(1)}, bf16[16,2176]{1,0:T(8,128)(2,1)S(1)}, u32[]{:S(2)}, u32[]{:S(2)}) collective-permute-start(bf16[16,2176]{1,0:T(8,128)(2,1)S(1)} %prep.1.refs_0_.refs_7_), channel_id=1, source_target_pairs={{0,1},{1,0},{2,3},{3,2},{4,5},{5,4},{6,7},{7,6},{8,9},{9,8},{10,11... | collective-permute-start | bytes 208904 | tf_op jit(solution)/shard_map/ppermute | solution.py:23
  12.1 2.3 %collective-permute-done.11.refs_18_ = bf16[16,2048]{1,0:T(8,128)(2,1)S(1)} collective-permute-done((bf16[16,2048]{1,0:T(8,128)(2,1)S(1)}, bf16[16,2048]{1,0:T(8,128)(2,1)S(1)}, u32[]{:S(2)}, u32[]{:S(2)}) %collective-permute-start.11) | collective-permute-done | bytes 65568 | tf_op jit(solution)/shard_map/ppermute | solution.py:23
  14.4 0.5 %collective-permute-start.6 = (bf16[16,2176]{1,0:T(8,128)(2,1)S(1)}, bf16[16,2176]{1,0:T(8,128)(2,1)S(1)}, u32[]{:S(2)}, u32[]{:S(2)}) collective-permute-start(bf16[16,2176]{1,0:T(8,128)(2,1)S(1)} %collective-permute-done.2.refs_3_.refs_10_), channel_id=1, source_target_pairs={{0,4},{4,0},{8,12},{12,8},{16,20},{20,16},{24,28},{28,24},{1,5},{5... | collective-permute-start | bytes 208904 | tf_op jit(solution)/shard_map/ppermute | solution.py:23
  15.0 1.3 %collective-permute-start.9 = (bf16[16,2048]{1,0:T(8,128)(2,1)S(1)}, bf16[16,2048]{1,0:T(8,128)(2,1)S(1)}, u32[]{:S(2)}, u32[]{:S(2)}) collective-permute-start(bf16[16,2048]{1,0:T(8,128)(2,1)S(1)} %copy-done.2), channel_id=1, source_target_pairs={{0,1},{1,0},{2,3},{3,2},{4,5},{5,4},{6,7},{7,6},{8,9},{9,8},{10,11... | collective-permute-start | bytes 196616 | tf_op jit(solution)/shard_map/ppermute | solution.py:23
  16.2 3.2 %collective-permute-done.9.refs_16_ = bf16[16,2048]{1,0:T(8,128)(2,1)S(1)} collective-permute-done((bf16[16,2048]{1,0:T(8,128)(2,1)S(1)}, bf16[16,2048]{1,0:T(8,128)(2,1)S(1)}, u32[]{:S(2)}, u32[]{:S(2)}) %collective-permute-start.9) | collective-permute-done | bytes 65568 | tf_op jit(solution)/shard_map/ppermute | solution.py:23
  19.4 0.5 %collective-permute-start.15 = (bf16[16,2048]{1,0:T(8,128)(2,1)S(1)}, bf16[16,2048]{1,0:T(8,128)(2,1)S(1)}, u32[]{:S(2)}, u32[]{:S(2)}) collective-permute-start(bf16[16,2048]{1,0:T(8,128)(2,1)S(1)} %collective-permute-done.11.refs_18_), channel_id=1, source_target_pairs={{0,4},{4,0},{8,12},{12,8},{16,20},{20,16},{24,28},{28,24},{1,5},{5... | collective-permute-start | bytes 196616 | tf_op jit(solution)/shard_map/ppermute | solution.py:23
  20.7 2.6 %collective-permute-start.8 = (f32[8,128]{1,0:T(8,128)S(1)}, f32[8,128]{1,0:T(8,128)S(1)}, u32[]{:S(2)}, u32[]{:S(2)}) collective-permute-start(f32[8,128]{1,0:T(8,128)S(1)} %get-tuple-element.17.refs_2_), channel_id=1, source_target_pairs={{0,16},{4,20},{8,24},{12,28},{16,0},{20,4},{24,8},{28,12},{1,17},{... | collective-permute-start | bytes 12296 | tf_op jit(solution)/shard_map/ppermute | solution.py:23
  23.3 1.6 %collective-permute-start.7 = (f32[8,128]{1,0:T(8,128)S(1)}, f32[8,128]{1,0:T(8,128)S(1)}, u32[]{:S(2)}, u32[]{:S(2)}) collective-permute-start(f32[8,128]{1,0:T(8,128)S(1)} %get-tuple-element.17.refs_2_), channel_id=1, source_target_pairs={{0,8},{4,12},{8,0},{12,4},{16,24},{20,28},{24,16},{28,20},{1,9},{5... | collective-permute-start | bytes 12296 | tf_op jit(solution)/shard_map/ppermute | solution.py:23
  25.2 1.7 %collective-permute-done.7.refs_0_ = f32[8,128]{1,0:T(8,128)S(1)} collective-permute-done((f32[8,128]{1,0:T(8,128)S(1)}, f32[8,128]{1,0:T(8,128)S(1)}, u32[]{:S(2)}, u32[]{:S(2)}) %collective-permute-start.7) | collective-permute-done | bytes 4128 | tf_op jit(solution)/shard_map/ppermute | solution.py:23
  26.9 10.4 %experts.1 = (bf16[64,4224]{1,0:T(8,128)(2,1)S(1)}, bf16[64,4224]{1,0:T(8,128)(2,1)S(1)}) custom-call(s32[4]{0:T(128)S(1)} %copy-done.5, f32[8,128]{1,0:T(8,128)S(1)} %collective-permute-done.7.refs_0_, f32[8,128]{1,0:T(8,128)S(1)} %collective-permute-done.8.refs_1_, f32[8,128]{1,0:T(8,128)S(1)} %get-tuple-element.17.refs_2_, ...), custom_call_target="tpu_custom_call" | custom-call | tf_op jit(solution)/shard_map/experts/pallas_call | solution.py:305
  37.5 1.9 %collective-permute-done.16.other = bf16[64,4224]{1,0:T(8,128)(2,1)S(1)} collective-permute-done((bf16[64,4224]{1,0:T(8,128)(2,1)S(1)}, bf16[64,4224]{1,0:T(8,128)(2,1)S(1)}, u32[]{:S(2)}, u32[]{:S(2)}) %collective-permute-start.16) | collective-permute-done | bytes 540704 | tf_op jit(solution)/shard_map/ppermute | solution.py:23
  39.5 1.1 %collective-permute-start.17 = (bf16[16,4224]{1,0:T(8,128)(2,1)S(1)}, bf16[16,4224]{1,0:T(8,128)(2,1)S(1)}, u32[]{:S(2)}, u32[]{:S(2)}) collective-permute-start(bf16[16,4224]{1,0:T(8,128)(2,1)S(1)} %get-tuple-element.25), channel_id=1, source_target_pairs={{0,1},{1,0},{2,3},{3,2},{4,5},{5,4},{6,7},{7,6},{8,9},{9,8},{10,11... | collective-permute-start | bytes 405512 | tf_op jit(solution)/shard_map/ppermute | solution.py:23
  40.7 0.9 %collective-permute-start.18 = (bf16[16,4224]{1,0:T(8,128)(2,1)S(1)}, bf16[16,4224]{1,0:T(8,128)(2,1)S(1)}, u32[]{:S(2)}, u32[]{:S(2)}) collective-permute-start(bf16[16,4224]{1,0:T(8,128)(2,1)S(1)} %get-tuple-element.26), channel_id=1, source_target_pairs={{0,2},{1,3},{2,0},{3,1},{4,6},{5,7},{6,4},{7,5},{8,10},{9,11},{10,... | collective-permute-start | bytes 405512 | tf_op jit(solution)/shard_map/ppermute | solution.py:23
  41.6 1.5 %collective-permute-start.19 = (bf16[16,4224]{1,0:T(8,128)(2,1)S(1)}, bf16[16,4224]{1,0:T(8,128)(2,1)S(1)}, u32[]{:S(2)}, u32[]{:S(2)}) collective-permute-start(bf16[16,4224]{1,0:T(8,128)(2,1)S(1)} %get-tuple-element.27), channel_id=1, source_target_pairs={{0,3},{1,2},{2,1},{3,0},{4,7},{5,6},{6,5},{7,4},{8,11},{9,10},{10,... | collective-permute-start | bytes 405512 | tf_op jit(solution)/shard_map/ppermute | solution.py:23
  43.1 3.0 %collective-permute-done.17.refs_1_ = bf16[16,4224]{1,0:T(8,128)(2,1)S(1)} collective-permute-done((bf16[16,4224]{1,0:T(8,128)(2,1)S(1)}, bf16[16,4224]{1,0:T(8,128)(2,1)S(1)}, u32[]{:S(2)}, u32[]{:S(2)}) %collective-permute-start.17) | collective-permute-done | bytes 135200 | tf_op jit(solution)/shard_map/ppermute | solution.py:23
  46.0 2.9 %collective-permute-done.18.refs_2_ = bf16[16,4224]{1,0:T(8,128)(2,1)S(1)} collective-permute-done((bf16[16,4224]{1,0:T(8,128)(2,1)S(1)}, bf16[16,4224]{1,0:T(8,128)(2,1)S(1)}, u32[]{:S(2)}, u32[]{:S(2)}) %collective-permute-start.18) | collective-permute-done | bytes 135200 | tf_op jit(solution)/shard_map/ppermute | solution.py:23
  48.9 0.7 %finish.1 = (bf16[16,2048]{1,0:T(8,128)(2,1)}, bf16[16,2048]{1,0:T(8,128)(2,1)}, f32[8,16]{1,0:T(8,128)}) custom-call(bf16[16,4224]{1,0:T(8,128)(2,1)S(1)} %get-tuple-element.24.refs_0_, bf16[16,4224]{1,0:T(8,128)(2,1)S(1)} %collective-permute-done.17.refs_1_, bf16[16,4224]{1,0:T(8,128)(2,1)S(1)} %collective-permute-done.18.refs_2_, ...), custom_call_target="tpu_custom_call" | custom-call | tf_op jit(solution)/shard_map/finish/pallas_call | solution.py:328
  (39 shorter events, 2.0 us)
Async XLA Ops:
  3.5 23.4 %copy-start = (bf16[4,2048,1536]{2,1,0:T(8,128)(2,1)S(1)}, bf16[4,2048,1536]{2,1,0:T(8,128)(2,1)}, u32[]{:S(2)}) copy-start(bf16[4,2048,1536]{2,1,0:T(8,128)(2,1)} %refs_23_.1) | copy-start | bytes 75497472
  3.5 23.4 %copy-start.1 = (bf16[4,2048,768]{2,1,0:T(8,128)(2,1)S(1)}, bf16[4,2048,768]{2,1,0:T(8,128)(2,1)}, u32[]{:S(2)}) copy-start(bf16[4,2048,768]{2,1,0:T(8,128)(2,1)} %refs_24_.1) | copy-start | bytes 37748740
  3.5 23.4 %copy-start.5 = (s32[4]{0:T(128)S(1)}, s32[4]{0:T(128)}, u32[]{:S(2)}) copy-start(s32[4]{0:T(128)} %mask_ref.1) | copy-start | bytes 52
  4.1 44.8 %copy-start.4 = (s32[16,8]{0,1:T(8,128)S(1)}, s32[16,8]{0,1:T(8,128)}, u32[]{:S(2)}) copy-start(s32[16,8]{0,1:T(8,128)} %param.11) | copy-start | bytes 1540
  4.1 10.3 %collective-permute-start.2 = (bf16[16,2176]{1,0:T(8,128)(2,1)S(1)}, bf16[16,2176]{1,0:T(8,128)(2,1)S(1)}, u32[]{:S(2)}, u32[]{:S(2)}) collective-permute-start(bf16[16,2176]{1,0:T(8,128)(2,1)S(1)} %prep.1.refs_0_.refs_7_), channel_id=1, source_target_pairs={{0,3},{1,2},{2,1},{3,0},{4,7},{5,6},{6,5},{7,4},{8,11},{9,10},{10,... | collective-permute-start | bytes 208904 | tf_op jit(solution)/shard_map/ppermute | solution.py:23
  8.1 6.8 %collective-permute-start.1 = (bf16[16,2176]{1,0:T(8,128)(2,1)S(1)}, bf16[16,2176]{1,0:T(8,128)(2,1)S(1)}, u32[]{:S(2)}, u32[]{:S(2)}) collective-permute-start(bf16[16,2176]{1,0:T(8,128)(2,1)S(1)} %prep.1.refs_0_.refs_7_), channel_id=1, source_target_pairs={{0,2},{1,3},{2,0},{3,1},{4,6},{5,7},{6,4},{7,5},{8,10},{9,11},{10,... | collective-permute-start | bytes 208904 | tf_op jit(solution)/shard_map/ppermute | solution.py:23
  8.6 5.8 %collective-permute-start.11 = (bf16[16,2048]{1,0:T(8,128)(2,1)S(1)}, bf16[16,2048]{1,0:T(8,128)(2,1)S(1)}, u32[]{:S(2)}, u32[]{:S(2)}) collective-permute-start(bf16[16,2048]{1,0:T(8,128)(2,1)S(1)} %copy-done.2), channel_id=1, source_target_pairs={{0,3},{1,2},{2,1},{3,0},{4,7},{5,6},{6,5},{7,4},{8,11},{9,10},{10,... | collective-permute-start | bytes 196616 | tf_op jit(solution)/shard_map/ppermute | solution.py:23
  10.1 4.9 %collective-permute-start.10 = (bf16[16,2048]{1,0:T(8,128)(2,1)S(1)}, bf16[16,2048]{1,0:T(8,128)(2,1)S(1)}, u32[]{:S(2)}, u32[]{:S(2)}) collective-permute-start(bf16[16,2048]{1,0:T(8,128)(2,1)S(1)} %copy-done.2), channel_id=1, source_target_pairs={{0,2},{1,3},{2,0},{3,1},{4,6},{5,7},{6,4},{7,5},{8,10},{9,11},{10,... | collective-permute-start | bytes 196616 | tf_op jit(solution)/shard_map/ppermute | solution.py:23
  10.2 6.1 %collective-permute-start = (bf16[16,2176]{1,0:T(8,128)(2,1)S(1)}, bf16[16,2176]{1,0:T(8,128)(2,1)S(1)}, u32[]{:S(2)}, u32[]{:S(2)}) collective-permute-start(bf16[16,2176]{1,0:T(8,128)(2,1)S(1)} %prep.1.refs_0_.refs_7_), channel_id=1, source_target_pairs={{0,1},{1,0},{2,3},{3,2},{4,5},{5,4},{6,7},{7,6},{8,9},{9,8},{10,11... | collective-permute-start | bytes 208904 | tf_op jit(solution)/shard_map/ppermute | solution.py:23
  14.4 5.0 %collective-permute-start.3 = (bf16[16,2176]{1,0:T(8,128)(2,1)S(1)}, bf16[16,2176]{1,0:T(8,128)(2,1)S(1)}, u32[]{:S(2)}, u32[]{:S(2)}) collective-permute-start(bf16[16,2176]{1,0:T(8,128)(2,1)S(1)} %prep.1.refs_0_.refs_7_), channel_id=1, source_target_pairs={{0,4},{4,0},{8,12},{12,8},{16,20},{20,16},{24,28},{28,24},{1,5},{5... | collective-permute-start | bytes 208904 | tf_op jit(solution)/shard_map/ppermute | solution.py:23
  14.4 5.5 %collective-permute-start.6 = (bf16[16,2176]{1,0:T(8,128)(2,1)S(1)}, bf16[16,2176]{1,0:T(8,128)(2,1)S(1)}, u32[]{:S(2)}, u32[]{:S(2)}) collective-permute-start(bf16[16,2176]{1,0:T(8,128)(2,1)S(1)} %collective-permute-done.2.refs_3_.refs_10_), channel_id=1, source_target_pairs={{0,4},{4,0},{8,12},{12,8},{16,20},{20,16},{24,28},{28,24},{1,5},{5... | collective-permute-start | bytes 208904 | tf_op jit(solution)/shard_map/ppermute | solution.py:23
  14.9 5.1 %collective-permute-start.5 = (bf16[16,2176]{1,0:T(8,128)(2,1)S(1)}, bf16[16,2176]{1,0:T(8,128)(2,1)S(1)}, u32[]{:S(2)}, u32[]{:S(2)}) collective-permute-start(bf16[16,2176]{1,0:T(8,128)(2,1)S(1)} %collective-permute-done.1.refs_2_.refs_9_), channel_id=1, source_target_pairs={{0,4},{4,0},{8,12},{12,8},{16,20},{20,16},{24,28},{28,24},{1,5},{5... | collective-permute-start | bytes 208904 | tf_op jit(solution)/shard_map/ppermute | solution.py:23
  15.0 4.4 %collective-permute-start.9 = (bf16[16,2048]{1,0:T(8,128)(2,1)S(1)}, bf16[16,2048]{1,0:T(8,128)(2,1)S(1)}, u32[]{:S(2)}, u32[]{:S(2)}) collective-permute-start(bf16[16,2048]{1,0:T(8,128)(2,1)S(1)} %copy-done.2), channel_id=1, source_target_pairs={{0,1},{1,0},{2,3},{3,2},{4,5},{5,4},{6,7},{7,6},{8,9},{9,8},{10,11... | collective-permute-start | bytes 196616 | tf_op jit(solution)/shard_map/ppermute | solution.py:23
  16.2 4.2 %collective-permute-start.4 = (bf16[16,2176]{1,0:T(8,128)(2,1)S(1)}, bf16[16,2176]{1,0:T(8,128)(2,1)S(1)}, u32[]{:S(2)}, u32[]{:S(2)}) collective-permute-start(bf16[16,2176]{1,0:T(8,128)(2,1)S(1)} %collective-permute-done.refs_1_.refs_8_), channel_id=1, source_target_pairs={{0,4},{4,0},{8,12},{12,8},{16,20},{20,16},{24,28},{28,24},{1,5},{5... | collective-permute-start | bytes 208904 | tf_op jit(solution)/shard_map/ppermute | solution.py:23
  19.4 3.9 %collective-permute-start.12 = (bf16[16,2048]{1,0:T(8,128)(2,1)S(1)}, bf16[16,2048]{1,0:T(8,128)(2,1)S(1)}, u32[]{:S(2)}, u32[]{:S(2)}) collective-permute-start(bf16[16,2048]{1,0:T(8,128)(2,1)S(1)} %copy-done.2), channel_id=1, source_target_pairs={{0,4},{4,0},{8,12},{12,8},{16,20},{20,16},{24,28},{28,24},{1,5},{5... | collective-permute-start | bytes 196616 | tf_op jit(solution)/shard_map/ppermute | solution.py:23
  19.4 5.5 %collective-permute-start.15 = (bf16[16,2048]{1,0:T(8,128)(2,1)S(1)}, bf16[16,2048]{1,0:T(8,128)(2,1)S(1)}, u32[]{:S(2)}, u32[]{:S(2)}) collective-permute-start(bf16[16,2048]{1,0:T(8,128)(2,1)S(1)} %collective-permute-done.11.refs_18_), channel_id=1, source_target_pairs={{0,4},{4,0},{8,12},{12,8},{16,20},{20,16},{24,28},{28,24},{1,5},{5... | collective-permute-start | bytes 196616 | tf_op jit(solution)/shard_map/ppermute | solution.py:23
  19.9 5.0 %collective-permute-start.14 = (bf16[16,2048]{1,0:T(8,128)(2,1)S(1)}, bf16[16,2048]{1,0:T(8,128)(2,1)S(1)}, u32[]{:S(2)}, u32[]{:S(2)}) collective-permute-start(bf16[16,2048]{1,0:T(8,128)(2,1)S(1)} %collective-permute-done.10.refs_17_), channel_id=1, source_target_pairs={{0,4},{4,0},{8,12},{12,8},{16,20},{20,16},{24,28},{28,24},{1,5},{5... | collective-permute-start | bytes 196616 | tf_op jit(solution)/shard_map/ppermute | solution.py:23
  20.0 4.9 %collective-permute-start.13 = (bf16[16,2048]{1,0:T(8,128)(2,1)S(1)}, bf16[16,2048]{1,0:T(8,128)(2,1)S(1)}, u32[]{:S(2)}, u32[]{:S(2)}) collective-permute-start(bf16[16,2048]{1,0:T(8,128)(2,1)S(1)} %collective-permute-done.9.refs_16_), channel_id=1, source_target_pairs={{0,4},{4,0},{8,12},{12,8},{16,20},{20,16},{24,28},{28,24},{1,5},{5... | collective-permute-start | bytes 196616 | tf_op jit(solution)/shard_map/ppermute | solution.py:23
  20.7 4.5 %collective-permute-start.8 = (f32[8,128]{1,0:T(8,128)S(1)}, f32[8,128]{1,0:T(8,128)S(1)}, u32[]{:S(2)}, u32[]{:S(2)}) collective-permute-start(f32[8,128]{1,0:T(8,128)S(1)} %get-tuple-element.17.refs_2_), channel_id=1, source_target_pairs={{0,16},{4,20},{8,24},{12,28},{16,0},{20,4},{24,8},{28,12},{1,17},{... | collective-permute-start | bytes 12296 | tf_op jit(solution)/shard_map/ppermute | solution.py:23
  23.3 3.6 %collective-permute-start.7 = (f32[8,128]{1,0:T(8,128)S(1)}, f32[8,128]{1,0:T(8,128)S(1)}, u32[]{:S(2)}, u32[]{:S(2)}) collective-permute-start(f32[8,128]{1,0:T(8,128)S(1)} %get-tuple-element.17.refs_2_), channel_id=1, source_target_pairs={{0,8},{4,12},{8,0},{12,4},{16,24},{20,28},{24,16},{28,20},{1,9},{5... | collective-permute-start | bytes 12296 | tf_op jit(solution)/shard_map/ppermute | solution.py:23
  37.4 2.0 %collective-permute-start.16 = (bf16[64,4224]{1,0:T(8,128)(2,1)S(1)}, bf16[64,4224]{1,0:T(8,128)(2,1)S(1)}, u32[]{:S(2)}, u32[]{:S(2)}) collective-permute-start(bf16[64,4224]{1,0:T(8,128)(2,1)S(1)} %get-tuple-element.23), channel_id=1, source_target_pairs={{0,4},{4,0},{8,12},{12,8},{16,20},{20,16},{24,28},{28,24},{1,5},{5... | collective-permute-start | bytes 1622024 | tf_op jit(solution)/shard_map/ppermute | solution.py:23
  39.5 6.5 %collective-permute-start.17 = (bf16[16,4224]{1,0:T(8,128)(2,1)S(1)}, bf16[16,4224]{1,0:T(8,128)(2,1)S(1)}, u32[]{:S(2)}, u32[]{:S(2)}) collective-permute-start(bf16[16,4224]{1,0:T(8,128)(2,1)S(1)} %get-tuple-element.25), channel_id=1, source_target_pairs={{0,1},{1,0},{2,3},{3,2},{4,5},{5,4},{6,7},{7,6},{8,9},{9,8},{10,11... | collective-permute-start | bytes 405512 | tf_op jit(solution)/shard_map/ppermute | solution.py:23
  40.7 8.2 %collective-permute-start.18 = (bf16[16,4224]{1,0:T(8,128)(2,1)S(1)}, bf16[16,4224]{1,0:T(8,128)(2,1)S(1)}, u32[]{:S(2)}, u32[]{:S(2)}) collective-permute-start(bf16[16,4224]{1,0:T(8,128)(2,1)S(1)} %get-tuple-element.26), channel_id=1, source_target_pairs={{0,2},{1,3},{2,0},{3,1},{4,6},{5,7},{6,4},{7,5},{8,10},{9,11},{10,... | collective-permute-start | bytes 405512 | tf_op jit(solution)/shard_map/ppermute | solution.py:23
  41.6 7.3 %collective-permute-start.19 = (bf16[16,4224]{1,0:T(8,128)(2,1)S(1)}, bf16[16,4224]{1,0:T(8,128)(2,1)S(1)}, u32[]{:S(2)}, u32[]{:S(2)}) collective-permute-start(bf16[16,4224]{1,0:T(8,128)(2,1)S(1)} %get-tuple-element.27), channel_id=1, source_target_pairs={{0,3},{1,2},{2,1},{3,0},{4,7},{5,6},{6,5},{7,4},{8,11},{9,10},{10,... | collective-permute-start | bytes 405512 | tf_op jit(solution)/shard_map/ppermute | solution.py:23
  (5 other events, 7.9 us)

commit v3 on v2

--- a/solution.py
+++ b/solution.py
@@ -32,18 +32,30 @@
     return lax.axis_index("expert") * local_count, core * (local_count // groups)
 
 
-def prep_kernel(tokens, routes_t, gates_t, capacity, out, side):
+def prep_kernel(tokens, routes_t, gates_t, capacity, out, ids, gates, caps, side, sems):
     width = tokens.shape[1]
     tok_count = routes_t.shape[1]
-    out[:, :width] = tokens[...]
+    copies = [
+        pltpu.make_async_copy(routes_t, ids, sems.at[0]),
+        pltpu.make_async_copy(gates_t, gates, sems.at[1]),
+        pltpu.make_async_copy(tokens, out.at[:, :width], sems.at[2]),
+    ]
+    one = capacity.shape[1] == 1
+    if not one:
+        copies.insert(2, pltpu.make_async_copy(capacity, caps, sems.at[3]))
+    for copy in copies:
+        copy.start()
     side[...] = jnp.zeros_like(side)
-    side[:TOPK, :tok_count] = routes_t[...].astype(jnp.float32)
-    side[TOPK : 2 * TOPK, :tok_count] = gates_t[...].astype(jnp.float32)
+    for copy in copies[:-1]:
+        copy.wait()
+    side[:TOPK, :tok_count] = ids[...].astype(jnp.float32)
+    side[TOPK : 2 * TOPK, :tok_count] = gates[...].astype(jnp.float32)
     block = side[...]
     row, lane = iota(block.shape, 0), iota(block.shape, 1)
     for l in range(capacity.shape[1]):
-        block = jnp.where((lane == tok_count) & (row == l), capacity[0, l].astype(jnp.float32), block)
+        block = jnp.where((lane == tok_count) & (row == l), (capacity if one else caps)[0, l].astype(jnp.float32), block)
     out[:, width:] = block.astype(jnp.bfloat16)
+    copies[-1].wait()
 
 
 def tables_kernel(group_size, groups, local_count, tok_count, *refs):
@@ -240,7 +252,7 @@
     gate_grad_t[...] = out
 
 
-def kernel(body, name, out_shape, in_specs, scratch=(), limit=4, flops=0):
+def kernel(body, out_shape, in_specs, scratch=(), limit=4, flops=0):
     vm = pl.BlockSpec(memory_space=VM)
     return pl.pallas_call(
         body,
@@ -250,7 +262,6 @@
         scratch_shapes=scratch,
         compiler_params=pltpu.CompilerParams(vmem_limit_bytes=limit * MIB),
         cost_estimate=pl.CostEstimate(flops=flops, bytes_accessed=0, transcendentals=0) if flops else None,
-        name=name,
     )
 
 
@@ -263,6 +274,7 @@
     per_device = local_count // groups
     bf16, f32 = jnp.bfloat16, jnp.float32
     vm, sm = pl.BlockSpec(memory_space=VM), pl.BlockSpec(memory_space=pltpu.SMEM)
+    hbm = pl.BlockSpec(memory_space=pltpu.HBM)
     array = jax.ShapeDtypeStruct
     routes_t = routes.T
     gate_up = pltpu.with_memory_space_constraint(gate_up_weight, VM)
@@ -270,16 +282,26 @@
 
     packed = kernel(
         prep_kernel,
-        "prep",
         array((tok_count, width + LANES), bf16),
-        [vm, vm, vm, sm],
-        [VM((tok_count, LANES), f32)],
+        [hbm] * 3 + [sm if local_count == 1 else hbm],
+        [
+            VM((TOPK, tok_count), jnp.int32),
+            VM((TOPK, tok_count), bf16),
+            pltpu.SMEM((1, local_count), jnp.int32),
+            VM((tok_count, LANES), f32),
+            pltpu.SemaphoreType.DMA((4,)),
+        ],
         flops=LURE,
-    )(tokens, routes_t, gate_probs.T, capacity)
+    )(
+        *(pltpu.with_memory_space_constraint(v, pltpu.HBM) for v in (tokens, routes_t, gate_probs.T)),
+        capacity if local_count == 1 else pltpu.with_memory_space_constraint(capacity, pltpu.HBM),
+    )
 
     def gathered(piece):
         pieces = [piece] + [swapped(piece, "expert", k) for k in range(1, group_size)]
-        return pieces + [swapped(p, "dp", 1) for p in pieces] if groups == 2 else pieces
+        if groups == 2:
+            pieces += [swapped(p, "dp", 1) for p in pieces]
+        return pieces
 
     toks = gathered(packed)
     grds = gathered(grad_out)
@@ -304,7 +326,6 @@
     group_rows = rows // groups
     parts = kernel(
         functools.partial(experts_kernel, groups, local_count, count, width, levels),
-        "experts",
         [array((group_rows, total_width), bf16)] * groups,
         [sm] + [vm] * (len(far) + 7 + 2 * count),
         [
@@ -321,13 +342,12 @@
     block = array((tok_count, total_width), bf16)
     if groups == 2:
         other = swapped(parts[1], "dp", 1)
-        blocks = kernel(join_kernel, "join", [block] * group_size, [vm, vm])(parts[0], other)
+        blocks = kernel(join_kernel, [block] * group_size, [vm, vm])(parts[0], other)
     else:
         blocks = [parts[0][k * tok_count : (k + 1) * tok_count] for k in range(group_size)]
     mine = [blocks[0]] + [swapped(blocks[k], "expert", k) for k in range(1, group_size)]
     layer_out, input_grad, gate_grad_t = kernel(
         functools.partial(finish_kernel, width),
-        "finish",
         [array((tok_count, width), bf16), array((tok_count, width), bf16), array((TOPK, tok_count), f32)],
         [vm] * (group_size + 1),
     )(*mine, routes_t)

time: 49.9 us -> 47.4 us (0.950)
  local copies, waits for them, and re-layouts: 2.88 us -> 0.02 us
  Pallas kernels: 12.1 us -> 12.6 us
    unnamed x18 -> x10, local copies, waits for them, and re-layouts: 2.88 us -> 0.02 us
    pallas_call x3, Pallas kernels: 1.4 us -> 1.9 us  [the longest x1 1.06 us: body(): kernel(prep_kernel, array((tok_count, width + LANES), bf16), [hbm] * 3 +...]
  transfers between devices with their start and end apart: 20 -> 20, of which waited for: 7 -> 7; matrix products, arithmetic and copies ran while one was open for 0% -> 0% of each run, Pallas kernels for 0% -> 1%
where the time goes in v3:
time: 47.4 us; the launch traced here: 47.3 us
  starting transfers between devices  18.7 us (39%)
  waiting for transfers between devices  15.3 us (32%)
  Pallas kernels  12.6 us (27%)
  between operations  0.73 us (2%)
    ppermute x20, starting transfers between devices, swapped(): lax.ppermute(shard, axis, [(i, i ^ mask) for i in range(lax.axis_size(axi...  18.7 us
    ppermute x20, waiting for transfers between devices, swapped(): lax.ppermute(shard, axis, [(i, i ^ mask) for i in range(lax.axis_size(axi...  15.3 us
    pallas_call x1, Pallas kernels, body(): kernel(functools.partial(experts_kernel, groups, local_count, count, widt...  10.4 us
    pallas_call x1, Pallas kernels, body(): kernel(prep_kernel, array((tok_count, width + LANES), bf16), [hbm] * 3 +...  1.06 us
  transfers between devices with their start and end apart: 20, of which 7 were waited for; matrix products, arithmetic and copies ran while one was open for 0% of the time, Pallas kernels for 1%

profile of v3, /device:TPU:0, one launch (start us, length us, event | category | flops | bytes accessed | tf_op | source)
XLA Modules:
  0.0 47.3 jit_solution(18376600116151387819)
XLA Ops:
  0.7 1.1 %shard_map.103.refs_0_.refs_7_ = bf16[16,2176]{1,0:T(8,128)(2,1)S(1)} custom-call(bf16[16,2048]{1,0:T(8,128)(2,1)} %tokens.1, s32[8,16]{1,0:T(8,128)} %bitcast.3, bf16[8,16]{1,0:T(8,128)(2,1)} %bitcast.6, s32[1,4]{1,0:T(1,128)} %capacity.1), custom_call_target="tpu_custom_call" | custom-call | flops 20000000000 | tf_op jit(solution)/shard_map/pallas_call | solution.py:283
  1.8 4.0 %collective-permute-start.2 = (bf16[16,2176]{1,0:T(8,128)(2,1)S(1)}, bf16[16,2176]{1,0:T(8,128)(2,1)S(1)}, u32[]{:S(2)}, u32[]{:S(2)}) collective-permute-start(bf16[16,2176]{1,0:T(8,128)(2,1)S(1)} %shard_map.103.refs_0_.refs_7_), channel_id=1, source_target_pairs={{0,3},{1,2},{2,1},{3,0},{4,7},{5,6},{6,5},{7,4},{8,11},{9,10},{10,... | collective-permute-start | bytes 208904 | tf_op jit(solution)/shard_map/ppermute | solution.py:23
  5.7 0.5 %collective-permute-start.1 = (bf16[16,2176]{1,0:T(8,128)(2,1)S(1)}, bf16[16,2176]{1,0:T(8,128)(2,1)S(1)}, u32[]{:S(2)}, u32[]{:S(2)}) collective-permute-start(bf16[16,2176]{1,0:T(8,128)(2,1)S(1)} %shard_map.103.refs_0_.refs_7_), channel_id=1, source_target_pairs={{0,2},{1,3},{2,0},{3,1},{4,6},{5,7},{6,4},{7,5},{8,10},{9,11},{10,... | collective-permute-start | bytes 208904 | tf_op jit(solution)/shard_map/ppermute | solution.py:23
  6.2 1.5 %collective-permute-start.11 = (bf16[16,2048]{1,0:T(8,128)(2,1)S(1)}, bf16[16,2048]{1,0:T(8,128)(2,1)S(1)}, u32[]{:S(2)}, u32[]{:S(2)}) collective-permute-start(bf16[16,2048]{1,0:T(8,128)(2,1)S(1)} %copy-done.2), channel_id=1, source_target_pairs={{0,3},{1,2},{2,1},{3,0},{4,7},{5,6},{6,5},{7,4},{8,11},{9,10},{10,... | collective-permute-start | bytes 196616 | tf_op jit(solution)/shard_map/ppermute | solution.py:23
  7.8 1.9 %collective-permute-start = (bf16[16,2176]{1,0:T(8,128)(2,1)S(1)}, bf16[16,2176]{1,0:T(8,128)(2,1)S(1)}, u32[]{:S(2)}, u32[]{:S(2)}) collective-permute-start(bf16[16,2176]{1,0:T(8,128)(2,1)S(1)} %shard_map.103.refs_0_.refs_7_), channel_id=1, source_target_pairs={{0,1},{1,0},{2,3},{3,2},{4,5},{5,4},{6,7},{7,6},{8,9},{9,8},{10,11... | collective-permute-start | bytes 208904 | tf_op jit(solution)/shard_map/ppermute | solution.py:23
  9.7 2.3 %collective-permute-done.11.refs_18_ = bf16[16,2048]{1,0:T(8,128)(2,1)S(1)} collective-permute-done((bf16[16,2048]{1,0:T(8,128)(2,1)S(1)}, bf16[16,2048]{1,0:T(8,128)(2,1)S(1)}, u32[]{:S(2)}, u32[]{:S(2)}) %collective-permute-start.11) | collective-permute-done | bytes 65568 | tf_op jit(solution)/shard_map/ppermute | solution.py:23
  12.1 0.5 %collective-permute-start.6 = (bf16[16,2176]{1,0:T(8,128)(2,1)S(1)}, bf16[16,2176]{1,0:T(8,128)(2,1)S(1)}, u32[]{:S(2)}, u32[]{:S(2)}) collective-permute-start(bf16[16,2176]{1,0:T(8,128)(2,1)S(1)} %collective-permute-done.2.refs_3_.refs_10_), channel_id=1, source_target_pairs={{0,4},{4,0},{8,12},{12,8},{16,20},{20,16},{24,28},{28,24},{1,5},{5... | collective-permute-start | bytes 208904 | tf_op jit(solution)/shard_map/ppermute | solution.py:23
  12.7 1.3 %collective-permute-start.9 = (bf16[16,2048]{1,0:T(8,128)(2,1)S(1)}, bf16[16,2048]{1,0:T(8,128)(2,1)S(1)}, u32[]{:S(2)}, u32[]{:S(2)}) collective-permute-start(bf16[16,2048]{1,0:T(8,128)(2,1)S(1)} %copy-done.2), channel_id=1, source_target_pairs={{0,1},{1,0},{2,3},{3,2},{4,5},{5,4},{6,7},{7,6},{8,9},{9,8},{10,11... | collective-permute-start | bytes 196616 | tf_op jit(solution)/shard_map/ppermute | solution.py:23
  13.9 3.2 %collective-permute-done.9.refs_16_ = bf16[16,2048]{1,0:T(8,128)(2,1)S(1)} collective-permute-done((bf16[16,2048]{1,0:T(8,128)(2,1)S(1)}, bf16[16,2048]{1,0:T(8,128)(2,1)S(1)}, u32[]{:S(2)}, u32[]{:S(2)}) %collective-permute-start.9) | collective-permute-done | bytes 65568 | tf_op jit(solution)/shard_map/ppermute | solution.py:23
  17.1 0.5 %collective-permute-start.15 = (bf16[16,2048]{1,0:T(8,128)(2,1)S(1)}, bf16[16,2048]{1,0:T(8,128)(2,1)S(1)}, u32[]{:S(2)}, u32[]{:S(2)}) collective-permute-start(bf16[16,2048]{1,0:T(8,128)(2,1)S(1)} %collective-permute-done.11.refs_18_), channel_id=1, source_target_pairs={{0,4},{4,0},{8,12},{12,8},{16,20},{20,16},{24,28},{28,24},{1,5},{5... | collective-permute-start | bytes 196616 | tf_op jit(solution)/shard_map/ppermute | solution.py:23
  17.7 0.4 collective-permute-start.13
  18.1 0.2 tables.1
  18.4 2.6 %collective-permute-start.8 = (f32[8,128]{1,0:T(8,128)S(1)}, f32[8,128]{1,0:T(8,128)S(1)}, u32[]{:S(2)}, u32[]{:S(2)}) collective-permute-start(f32[8,128]{1,0:T(8,128)S(1)} %get-tuple-element.17.refs_2_), channel_id=1, source_target_pairs={{0,16},{4,20},{8,24},{12,28},{16,0},{20,4},{24,8},{28,12},{1,17},{... | collective-permute-start | bytes 12296 | tf_op jit(solution)/shard_map/ppermute | solution.py:23
  21.0 1.6 %collective-permute-start.7 = (f32[8,128]{1,0:T(8,128)S(1)}, f32[8,128]{1,0:T(8,128)S(1)}, u32[]{:S(2)}, u32[]{:S(2)}) collective-permute-start(f32[8,128]{1,0:T(8,128)S(1)} %get-tuple-element.17.refs_2_), channel_id=1, source_target_pairs={{0,8},{4,12},{8,0},{12,4},{16,24},{20,28},{24,16},{28,20},{1,9},{5... | collective-permute-start | bytes 12296 | tf_op jit(solution)/shard_map/ppermute | solution.py:23
  22.6 0.3 collective-permute-done.8.refs_1_
  22.9 1.7 %collective-permute-done.7.refs_0_ = f32[8,128]{1,0:T(8,128)S(1)} collective-permute-done((f32[8,128]{1,0:T(8,128)S(1)}, f32[8,128]{1,0:T(8,128)S(1)}, u32[]{:S(2)}, u32[]{:S(2)}) %collective-permute-start.7) | collective-permute-done | bytes 4128 | tf_op jit(solution)/shard_map/ppermute | solution.py:23
  24.6 10.4 %shard_map.104 = (bf16[64,4224]{1,0:T(8,128)(2,1)S(1)}, bf16[64,4224]{1,0:T(8,128)(2,1)S(1)}) custom-call(s32[4]{0:T(128)S(1)} %copy-done.4, f32[8,128]{1,0:T(8,128)S(1)} %collective-permute-done.7.refs_0_, f32[8,128]{1,0:T(8,128)S(1)} %collective-permute-done.8.refs_1_, f32[8,128]{1,0:T(8,128)S(1)} %get-tuple-element.17.refs_2_, ...), custom_call_target="tpu_custom_call" | custom-call | tf_op jit(solution)/shard_map/pallas_call | solution.py:327
  35.1 1.9 %collective-permute-done.16.other = bf16[64,4224]{1,0:T(8,128)(2,1)S(1)} collective-permute-done((bf16[64,4224]{1,0:T(8,128)(2,1)S(1)}, bf16[64,4224]{1,0:T(8,128)(2,1)S(1)}, u32[]{:S(2)}, u32[]{:S(2)}) %collective-permute-start.16) | collective-permute-done | bytes 540704 | tf_op jit(solution)/shard_map/ppermute | solution.py:23
  37.2 1.1 %collective-permute-start.17 = (bf16[16,4224]{1,0:T(8,128)(2,1)S(1)}, bf16[16,4224]{1,0:T(8,128)(2,1)S(1)}, u32[]{:S(2)}, u32[]{:S(2)}) collective-permute-start(bf16[16,4224]{1,0:T(8,128)(2,1)S(1)} %get-tuple-element.25), channel_id=1, source_target_pairs={{0,1},{1,0},{2,3},{3,2},{4,5},{5,4},{6,7},{7,6},{8,9},{9,8},{10,11... | collective-permute-start | bytes 405512 | tf_op jit(solution)/shard_map/ppermute | solution.py:23
  38.3 0.9 %collective-permute-start.18 = (bf16[16,4224]{1,0:T(8,128)(2,1)S(1)}, bf16[16,4224]{1,0:T(8,128)(2,1)S(1)}, u32[]{:S(2)}, u32[]{:S(2)}) collective-permute-start(bf16[16,4224]{1,0:T(8,128)(2,1)S(1)} %get-tuple-element.26), channel_id=1, source_target_pairs={{0,2},{1,3},{2,0},{3,1},{4,6},{5,7},{6,4},{7,5},{8,10},{9,11},{10,... | collective-permute-start | bytes 405512 | tf_op jit(solution)/shard_map/ppermute | solution.py:23
  39.2 1.5 %collective-permute-start.19 = (bf16[16,4224]{1,0:T(8,128)(2,1)S(1)}, bf16[16,4224]{1,0:T(8,128)(2,1)S(1)}, u32[]{:S(2)}, u32[]{:S(2)}) collective-permute-start(bf16[16,4224]{1,0:T(8,128)(2,1)S(1)} %get-tuple-element.27), channel_id=1, source_target_pairs={{0,3},{1,2},{2,1},{3,0},{4,7},{5,6},{6,5},{7,4},{8,11},{9,10},{10,... | collective-permute-start | bytes 405512 | tf_op jit(solution)/shard_map/ppermute | solution.py:23
  40.7 3.0 %collective-permute-done.17.refs_1_ = bf16[16,4224]{1,0:T(8,128)(2,1)S(1)} collective-permute-done((bf16[16,4224]{1,0:T(8,128)(2,1)S(1)}, bf16[16,4224]{1,0:T(8,128)(2,1)S(1)}, u32[]{:S(2)}, u32[]{:S(2)}) %collective-permute-start.17) | collective-permute-done | bytes 135200 | tf_op jit(solution)/shard_map/ppermute | solution.py:23
  43.7 2.9 %collective-permute-done.18.refs_2_ = bf16[16,4224]{1,0:T(8,128)(2,1)S(1)} collective-permute-done((bf16[16,4224]{1,0:T(8,128)(2,1)S(1)}, bf16[16,4224]{1,0:T(8,128)(2,1)S(1)}, u32[]{:S(2)}, u32[]{:S(2)}) %collective-permute-start.18) | collective-permute-done | bytes 135200 | tf_op jit(solution)/shard_map/ppermute | solution.py:23
  46.6 0.7 %shard_map.106 = (bf16[16,2048]{1,0:T(8,128)(2,1)}, bf16[16,2048]{1,0:T(8,128)(2,1)}, f32[8,16]{1,0:T(8,128)}) custom-call(bf16[16,4224]{1,0:T(8,128)(2,1)S(1)} %get-tuple-element.24.refs_0_, bf16[16,4224]{1,0:T(8,128)(2,1)S(1)} %collective-permute-done.17.refs_1_, bf16[16,4224]{1,0:T(8,128)(2,1)S(1)} %collective-permute-done.18.refs_2_, ...), custom_call_target="tpu_custom_call" | custom-call | tf_op jit(solution)/shard_map/pallas_call | solution.py:349
  (31 shorter events, 0.5 us)
Async XLA Ops:
  0.6 24.0 %copy-start = (bf16[4,2048,1536]{2,1,0:T(8,128)(2,1)S(1)}, bf16[4,2048,1536]{2,1,0:T(8,128)(2,1)}, u32[]{:S(2)}) copy-start(bf16[4,2048,1536]{2,1,0:T(8,128)(2,1)} %refs_23_.1) | copy-start | bytes 75497472
  0.7 24.0 %copy-start.1 = (bf16[4,2048,768]{2,1,0:T(8,128)(2,1)S(1)}, bf16[4,2048,768]{2,1,0:T(8,128)(2,1)}, u32[]{:S(2)}) copy-start(bf16[4,2048,768]{2,1,0:T(8,128)(2,1)} %refs_24_.1) | copy-start | bytes 37748740
  0.7 23.9 %copy-start.4 = (s32[4]{0:T(128)S(1)}, s32[4]{0:T(128)}, u32[]{:S(2)}) copy-start(s32[4]{0:T(128)} %mask_ref.1) | copy-start | bytes 52
  1.7 44.8 %copy-start.3 = (s32[16,8]{0,1:T(8,128)S(1)}, s32[16,8]{0,1:T(8,128)}, u32[]{:S(2)}) copy-start(s32[16,8]{0,1:T(8,128)} %param.11) | copy-start | bytes 1540
  1.8 10.3 %collective-permute-start.2 = (bf16[16,2176]{1,0:T(8,128)(2,1)S(1)}, bf16[16,2176]{1,0:T(8,128)(2,1)S(1)}, u32[]{:S(2)}, u32[]{:S(2)}) collective-permute-start(bf16[16,2176]{1,0:T(8,128)(2,1)S(1)} %shard_map.103.refs_0_.refs_7_), channel_id=1, source_target_pairs={{0,3},{1,2},{2,1},{3,0},{4,7},{5,6},{6,5},{7,4},{8,11},{9,10},{10,... | collective-permute-start | bytes 208904 | tf_op jit(solution)/shard_map/ppermute | solution.py:23
  5.7 6.8 %collective-permute-start.1 = (bf16[16,2176]{1,0:T(8,128)(2,1)S(1)}, bf16[16,2176]{1,0:T(8,128)(2,1)S(1)}, u32[]{:S(2)}, u32[]{:S(2)}) collective-permute-start(bf16[16,2176]{1,0:T(8,128)(2,1)S(1)} %shard_map.103.refs_0_.refs_7_), channel_id=1, source_target_pairs={{0,2},{1,3},{2,0},{3,1},{4,6},{5,7},{6,4},{7,5},{8,10},{9,11},{10,... | collective-permute-start | bytes 208904 | tf_op jit(solution)/shard_map/ppermute | solution.py:23
  6.2 5.8 %collective-permute-start.11 = (bf16[16,2048]{1,0:T(8,128)(2,1)S(1)}, bf16[16,2048]{1,0:T(8,128)(2,1)S(1)}, u32[]{:S(2)}, u32[]{:S(2)}) collective-permute-start(bf16[16,2048]{1,0:T(8,128)(2,1)S(1)} %copy-done.2), channel_id=1, source_target_pairs={{0,3},{1,2},{2,1},{3,0},{4,7},{5,6},{6,5},{7,4},{8,11},{9,10},{10,... | collective-permute-start | bytes 196616 | tf_op jit(solution)/shard_map/ppermute | solution.py:23
  7.7 4.9 %collective-permute-start.10 = (bf16[16,2048]{1,0:T(8,128)(2,1)S(1)}, bf16[16,2048]{1,0:T(8,128)(2,1)S(1)}, u32[]{:S(2)}, u32[]{:S(2)}) collective-permute-start(bf16[16,2048]{1,0:T(8,128)(2,1)S(1)} %copy-done.2), channel_id=1, source_target_pairs={{0,2},{1,3},{2,0},{3,1},{4,6},{5,7},{6,4},{7,5},{8,10},{9,11},{10,... | collective-permute-start | bytes 196616 | tf_op jit(solution)/shard_map/ppermute | solution.py:23
  7.8 6.1 %collective-permute-start = (bf16[16,2176]{1,0:T(8,128)(2,1)S(1)}, bf16[16,2176]{1,0:T(8,128)(2,1)S(1)}, u32[]{:S(2)}, u32[]{:S(2)}) collective-permute-start(bf16[16,2176]{1,0:T(8,128)(2,1)S(1)} %shard_map.103.refs_0_.refs_7_), channel_id=1, source_target_pairs={{0,1},{1,0},{2,3},{3,2},{4,5},{5,4},{6,7},{7,6},{8,9},{9,8},{10,11... | collective-permute-start | bytes 208904 | tf_op jit(solution)/shard_map/ppermute | solution.py:23
  12.1 5.0 %collective-permute-start.3 = (bf16[16,2176]{1,0:T(8,128)(2,1)S(1)}, bf16[16,2176]{1,0:T(8,128)(2,1)S(1)}, u32[]{:S(2)}, u32[]{:S(2)}) collective-permute-start(bf16[16,2176]{1,0:T(8,128)(2,1)S(1)} %shard_map.103.refs_0_.refs_7_), channel_id=1, source_target_pairs={{0,4},{4,0},{8,12},{12,8},{16,20},{20,16},{24,28},{28,24},{1,5},{5... | collective-permute-start | bytes 208904 | tf_op jit(solution)/shard_map/ppermute | solution.py:23
  12.1 5.5 %collective-permute-start.6 = (bf16[16,2176]{1,0:T(8,128)(2,1)S(1)}, bf16[16,2176]{1,0:T(8,128)(2,1)S(1)}, u32[]{:S(2)}, u32[]{:S(2)}) collective-permute-start(bf16[16,2176]{1,0:T(8,128)(2,1)S(1)} %collective-permute-done.2.refs_3_.refs_10_), channel_id=1, source_target_pairs={{0,4},{4,0},{8,12},{12,8},{16,20},{20,16},{24,28},{28,24},{1,5},{5... | collective-permute-start | bytes 208904 | tf_op jit(solution)/shard_map/ppermute | solution.py:23
  12.6 5.1 %collective-permute-start.5 = (bf16[16,2176]{1,0:T(8,128)(2,1)S(1)}, bf16[16,2176]{1,0:T(8,128)(2,1)S(1)}, u32[]{:S(2)}, u32[]{:S(2)}) collective-permute-start(bf16[16,2176]{1,0:T(8,128)(2,1)S(1)} %collective-permute-done.1.refs_2_.refs_9_), channel_id=1, source_target_pairs={{0,4},{4,0},{8,12},{12,8},{16,20},{20,16},{24,28},{28,24},{1,5},{5... | collective-permute-start | bytes 208904 | tf_op jit(solution)/shard_map/ppermute | solution.py:23
  12.7 4.4 %collective-permute-start.9 = (bf16[16,2048]{1,0:T(8,128)(2,1)S(1)}, bf16[16,2048]{1,0:T(8,128)(2,1)S(1)}, u32[]{:S(2)}, u32[]{:S(2)}) collective-permute-start(bf16[16,2048]{1,0:T(8,128)(2,1)S(1)} %copy-done.2), channel_id=1, source_target_pairs={{0,1},{1,0},{2,3},{3,2},{4,5},{5,4},{6,7},{7,6},{8,9},{9,8},{10,11... | collective-permute-start | bytes 196616 | tf_op jit(solution)/shard_map/ppermute | solution.py:23
  13.9 4.2 %collective-permute-start.4 = (bf16[16,2176]{1,0:T(8,128)(2,1)S(1)}, bf16[16,2176]{1,0:T(8,128)(2,1)S(1)}, u32[]{:S(2)}, u32[]{:S(2)}) collective-permute-start(bf16[16,2176]{1,0:T(8,128)(2,1)S(1)} %collective-permute-done.refs_1_.refs_8_), channel_id=1, source_target_pairs={{0,4},{4,0},{8,12},{12,8},{16,20},{20,16},{24,28},{28,24},{1,5},{5... | collective-permute-start | bytes 208904 | tf_op jit(solution)/shard_map/ppermute | solution.py:23
  17.1 3.9 %collective-permute-start.12 = (bf16[16,2048]{1,0:T(8,128)(2,1)S(1)}, bf16[16,2048]{1,0:T(8,128)(2,1)S(1)}, u32[]{:S(2)}, u32[]{:S(2)}) collective-permute-start(bf16[16,2048]{1,0:T(8,128)(2,1)S(1)} %copy-done.2), channel_id=1, source_target_pairs={{0,4},{4,0},{8,12},{12,8},{16,20},{20,16},{24,28},{28,24},{1,5},{5... | collective-permute-start | bytes 196616 | tf_op jit(solution)/shard_map/ppermute | solution.py:23
  17.1 5.5 %collective-permute-start.15 = (bf16[16,2048]{1,0:T(8,128)(2,1)S(1)}, bf16[16,2048]{1,0:T(8,128)(2,1)S(1)}, u32[]{:S(2)}, u32[]{:S(2)}) collective-permute-start(bf16[16,2048]{1,0:T(8,128)(2,1)S(1)} %collective-permute-done.11.refs_18_), channel_id=1, source_target_pairs={{0,4},{4,0},{8,12},{12,8},{16,20},{20,16},{24,28},{28,24},{1,5},{5... | collective-permute-start | bytes 196616 | tf_op jit(solution)/shard_map/ppermute | solution.py:23
  17.6 5.0 %collective-permute-start.14 = (bf16[16,2048]{1,0:T(8,128)(2,1)S(1)}, bf16[16,2048]{1,0:T(8,128)(2,1)S(1)}, u32[]{:S(2)}, u32[]{:S(2)}) collective-permute-start(bf16[16,2048]{1,0:T(8,128)(2,1)S(1)} %collective-permute-done.10.refs_17_), channel_id=1, source_target_pairs={{0,4},{4,0},{8,12},{12,8},{16,20},{20,16},{24,28},{28,24},{1,5},{5... | collective-permute-start | bytes 196616 | tf_op jit(solution)/shard_map/ppermute | solution.py:23
  17.7 4.9 %collective-permute-start.13 = (bf16[16,2048]{1,0:T(8,128)(2,1)S(1)}, bf16[16,2048]{1,0:T(8,128)(2,1)S(1)}, u32[]{:S(2)}, u32[]{:S(2)}) collective-permute-start(bf16[16,2048]{1,0:T(8,128)(2,1)S(1)} %collective-permute-done.9.refs_16_), channel_id=1, source_target_pairs={{0,4},{4,0},{8,12},{12,8},{16,20},{20,16},{24,28},{28,24},{1,5},{5... | collective-permute-start | bytes 196616 | tf_op jit(solution)/shard_map/ppermute | solution.py:23
  18.4 4.5 %collective-permute-start.8 = (f32[8,128]{1,0:T(8,128)S(1)}, f32[8,128]{1,0:T(8,128)S(1)}, u32[]{:S(2)}, u32[]{:S(2)}) collective-permute-start(f32[8,128]{1,0:T(8,128)S(1)} %get-tuple-element.17.refs_2_), channel_id=1, source_target_pairs={{0,16},{4,20},{8,24},{12,28},{16,0},{20,4},{24,8},{28,12},{1,17},{... | collective-permute-start | bytes 12296 | tf_op jit(solution)/shard_map/ppermute | solution.py:23
  21.0 3.6 %collective-permute-start.7 = (f32[8,128]{1,0:T(8,128)S(1)}, f32[8,128]{1,0:T(8,128)S(1)}, u32[]{:S(2)}, u32[]{:S(2)}) collective-permute-start(f32[8,128]{1,0:T(8,128)S(1)} %get-tuple-element.17.refs_2_), channel_id=1, source_target_pairs={{0,8},{4,12},{8,0},{12,4},{16,24},{20,28},{24,16},{28,20},{1,9},{5... | collective-permute-start | bytes 12296 | tf_op jit(solution)/shard_map/ppermute | solution.py:23
  35.0 2.0 %collective-permute-start.16 = (bf16[64,4224]{1,0:T(8,128)(2,1)S(1)}, bf16[64,4224]{1,0:T(8,128)(2,1)S(1)}, u32[]{:S(2)}, u32[]{:S(2)}) collective-permute-start(bf16[64,4224]{1,0:T(8,128)(2,1)S(1)} %get-tuple-element.23), channel_id=1, source_target_pairs={{0,4},{4,0},{8,12},{12,8},{16,20},{20,16},{24,28},{28,24},{1,5},{5... | collective-permute-start | bytes 1622024 | tf_op jit(solution)/shard_map/ppermute | solution.py:23
  37.2 6.5 %collective-permute-start.17 = (bf16[16,4224]{1,0:T(8,128)(2,1)S(1)}, bf16[16,4224]{1,0:T(8,128)(2,1)S(1)}, u32[]{:S(2)}, u32[]{:S(2)}) collective-permute-start(bf16[16,4224]{1,0:T(8,128)(2,1)S(1)} %get-tuple-element.25), channel_id=1, source_target_pairs={{0,1},{1,0},{2,3},{3,2},{4,5},{5,4},{6,7},{7,6},{8,9},{9,8},{10,11... | collective-permute-start | bytes 405512 | tf_op jit(solution)/shard_map/ppermute | solution.py:23
  38.3 8.2 %collective-permute-start.18 = (bf16[16,4224]{1,0:T(8,128)(2,1)S(1)}, bf16[16,4224]{1,0:T(8,128)(2,1)S(1)}, u32[]{:S(2)}, u32[]{:S(2)}) collective-permute-start(bf16[16,4224]{1,0:T(8,128)(2,1)S(1)} %get-tuple-element.26), channel_id=1, source_target_pairs={{0,2},{1,3},{2,0},{3,1},{4,6},{5,7},{6,4},{7,5},{8,10},{9,11},{10,... | collective-permute-start | bytes 405512 | tf_op jit(solution)/shard_map/ppermute | solution.py:23
  39.2 7.3 %collective-permute-start.19 = (bf16[16,4224]{1,0:T(8,128)(2,1)S(1)}, bf16[16,4224]{1,0:T(8,128)(2,1)S(1)}, u32[]{:S(2)}, u32[]{:S(2)}) collective-permute-start(bf16[16,4224]{1,0:T(8,128)(2,1)S(1)} %get-tuple-element.27), channel_id=1, source_target_pairs={{0,3},{1,2},{2,1},{3,0},{4,7},{5,6},{6,5},{7,4},{8,11},{9,10},{10,... | collective-permute-start | bytes 405512 | tf_op jit(solution)/shard_map/ppermute | solution.py:23
  (1 other events, 5.6 us)

commit v4 on v3

--- a/solution.py
+++ b/solution.py
@@ -119,7 +119,7 @@
 def first_kernel(groups, local_count, count, width, *refs):
     toks, grds = refs[:count], refs[count : 2 * count]
     gate_t, gate_up, down, hid, dpre, grads, tok, grd = refs[2 * count :]
-    first_expert, first_local = place_of(groups, local_count)
+    _, first_local = place_of(groups, local_count)
     rows = tok.shape[0]
     piece_rows = rows // count
     hidden_units = down.shape[2]
@@ -158,9 +158,8 @@
     far = refs[: len(levels)]
     (spare, named_t, place_t, cap_t, hid, dpre, grads, gate_up, down) = refs[len(levels) : len(levels) + 9]
     outs = refs[len(levels) + 9 : len(levels) + 9 + groups]
-    acc_out, acc_grad = refs[len(levels) + 9 + groups :]
     first_expert, first_local = place_of(groups, local_count)
-    rows = acc_out.shape[0]
+    rows = hid.shape[1]
     group_rows = rows // groups
     sub = iota((SUB, 1), 0)
     mask = jnp.zeros((SUB, 1), jnp.int32)
@@ -177,35 +176,34 @@
         limit = jnp.where(group_of == g, cap_t[:, g : g + 1] + jnp.minimum(other, float(OVF)), limit)
     kept = jnp.where((named_t[...] > 0.0) & (place_t[...] < limit), 1.0, 0.0)
     kept = to_columns(kept, rows)
-    acc_out[...] = jnp.zeros_like(acc_out)
-    acc_grad[...] = jnp.zeros_like(acc_grad)
-
-    def one_expert(i, _):
-        e = first_local + i
-        keep = lane_of(kept, e) > 0.0
-        h = jnp.where(keep, hid[i].astype(jnp.float32), 0.0).astype(jnp.bfloat16)
-        d = jnp.where(keep, dpre[i].astype(jnp.float32), 0.0).astype(jnp.bfloat16)
-        for j in range(width // WIDE):
-            cols = pl.ds(j * WIDE, WIDE)
-            acc_out[:, cols] += lax.dot_general(
-                h, down[e, cols, :], (((1,), (1,)), ((), ())), preferred_element_type=jnp.float32
+    for i in range(hid.shape[0]):
+        keep = lane_of(kept, first_local + i) > 0.0
+        hid[i] = jnp.where(keep, hid[i].astype(jnp.float32), 0.0).astype(jnp.bfloat16)
+        dpre[i] = jnp.where(keep, dpre[i].astype(jnp.float32), 0.0).astype(jnp.bfloat16)
+
+    def product(left, right, cols):
+        total = None
+        for i in range(hid.shape[0]):
+            part = lax.dot_general(
+                right[first_local + i, cols, :], left[i], (((1,), (1,)), ((), ())), preferred_element_type=jnp.float32
             )
-            acc_grad[:, cols] += lax.dot_general(
-                d, gate_up[e, cols, :], (((1,), (1,)), ((), ())), preferred_element_type=jnp.float32
-            )
-        return _
-
-    lax.fori_loop(0, local_count // groups, one_expert, 0)
+            total = part if total is None else total + part
+        return jnp.transpose(total).astype(jnp.bfloat16)
+
+    def store(value, to):
+        for g in range(groups):
+            outs[g][:, to] = value[g * group_rows : (g + 1) * group_rows]
+
+    for j in range(width // WIDE):
+        cols = pl.ds(j * WIDE, WIDE)
+        store(product(hid, down, cols), cols)
+        store(product(dpre, gate_up, cols), pl.ds(width + j * WIDE, WIDE))
     value = jnp.where(kept > 0.0, grads[...], 0.0)
     high = value.astype(jnp.bfloat16).astype(jnp.float32)
     high_at = pltpu.roll(high, first_expert, 1)
     low_at = pltpu.roll(value - high, first_expert + EXPERTS, 1)
     table = high_at + low_at
-    for g in range(groups):
-        at = slice(g * group_rows, (g + 1) * group_rows)
-        outs[g][:, :width] = acc_out[at, :].astype(jnp.bfloat16)
-        outs[g][:, width : 2 * width] = acc_grad[at, :].astype(jnp.bfloat16)
-        outs[g][:, 2 * width :] = table[at, :].astype(jnp.bfloat16)
+    store(table.astype(jnp.bfloat16), pl.ds(2 * width, LANES))
 
 
 def experts_kernel(groups, local_count, count, width, levels, mask_ref, *refs):
@@ -214,11 +212,11 @@
     (spare, named_t, place_t, cap_t, gate_t), refs = refs[:5], refs[5:]
     pieces, refs = refs[: 2 * count], refs[2 * count :]
     (gate_up, down), refs = refs[:2], refs[2:]
-    outs, (tok, grd, hid, dpre, grads, acc_out, acc_grad) = refs[:groups], refs[groups:]
+    outs, (tok, grd, hid, dpre, grads) = refs[:groups], refs[groups:]
     first_kernel(groups, local_count, count, width, *pieces, gate_t, gate_up, down, hid, dpre, grads, tok, grd)
     second_kernel(
         groups, local_count, width, levels, mask_ref,
-        *far, spare, named_t, place_t, cap_t, hid, dpre, grads, gate_up, down, *outs, acc_out, acc_grad,
+        *far, spare, named_t, place_t, cap_t, hid, dpre, grads, gate_up, down, *outs,
     )
 
 
@@ -334,8 +332,6 @@
             VM((per_device, rows, hidden_units), bf16),
             VM((per_device, rows, 2 * hidden_units), bf16),
             VM((rows, LANES), f32),
-            VM((rows, width), f32),
-            VM((rows, width), f32),
         ],
         12,
     )(pair_mask, *far, spare, named_t, place_t, cap_t, gate_t, *toks, *grds, gate_up, down)

time: 47.4 us -> 46.2 us (0.975)
  Pallas kernels: 12.6 us -> 11.3 us
    pallas_call x1, Pallas kernels: 10.4 us -> 9.17 us  [body(): kernel(functools.partial(experts_kernel, groups, local_count, count, widt...]
where the time goes in v4:
time: 46.2 us; the launch traced here: 46 us
  starting transfers between devices  18.6 us (40%)
  waiting for transfers between devices  15.3 us (33%)
  Pallas kernels  11.3 us (24%)
  between operations  0.72 us (2%)
    ppermute x20, starting transfers between devices, swapped(): lax.ppermute(shard, axis, [(i, i ^ mask) for i in range(lax.axis_size(axi...  18.6 us
    ppermute x20, waiting for transfers between devices, swapped(): lax.ppermute(shard, axis, [(i, i ^ mask) for i in range(lax.axis_size(axi...  15.3 us
    pallas_call x1, Pallas kernels, body(): kernel(functools.partial(experts_kernel, groups, local_count, count, widt...  9.17 us
    pallas_call x1, Pallas kernels, body(): kernel(prep_kernel, array((tok_count, width + LANES), bf16), [hbm] * 3 +...  1.06 us
  transfers between devices with their start and end apart: 20, of which 7 were waited for; matrix products, arithmetic and copies ran while one was open for 0% of the time, Pallas kernels for 1%

profile of v4, /device:TPU:0, one launch (start us, length us, event | category | flops | bytes accessed | tf_op | source)
XLA Modules:
  0.0 46.0 jit_solution(6057547090480125042)
XLA Ops:
  0.7 1.1 %shard_map.103.refs_0_.refs_7_ = bf16[16,2176]{1,0:T(8,128)(2,1)S(1)} custom-call(bf16[16,2048]{1,0:T(8,128)(2,1)} %tokens.1, s32[8,16]{1,0:T(8,128)} %bitcast.3, bf16[8,16]{1,0:T(8,128)(2,1)} %bitcast.6, s32[1,4]{1,0:T(1,128)} %capacity.1), custom_call_target="tpu_custom_call" | custom-call | flops 20000000000 | tf_op jit(solution)/shard_map/pallas_call | solution.py:281
  1.8 4.0 %collective-permute-start.2 = (bf16[16,2176]{1,0:T(8,128)(2,1)S(1)}, bf16[16,2176]{1,0:T(8,128)(2,1)S(1)}, u32[]{:S(2)}, u32[]{:S(2)}) collective-permute-start(bf16[16,2176]{1,0:T(8,128)(2,1)S(1)} %shard_map.103.refs_0_.refs_7_), channel_id=1, source_target_pairs={{0,3},{1,2},{2,1},{3,0},{4,7},{5,6},{6,5},{7,4},{8,11},{9,10},{10,... | collective-permute-start | bytes 208904 | tf_op jit(solution)/shard_map/ppermute | solution.py:23
  5.7 0.5 %collective-permute-start.1 = (bf16[16,2176]{1,0:T(8,128)(2,1)S(1)}, bf16[16,2176]{1,0:T(8,128)(2,1)S(1)}, u32[]{:S(2)}, u32[]{:S(2)}) collective-permute-start(bf16[16,2176]{1,0:T(8,128)(2,1)S(1)} %shard_map.103.refs_0_.refs_7_), channel_id=1, source_target_pairs={{0,2},{1,3},{2,0},{3,1},{4,6},{5,7},{6,4},{7,5},{8,10},{9,11},{10,... | collective-permute-start | bytes 208904 | tf_op jit(solution)/shard_map/ppermute | solution.py:23
  6.2 1.5 %collective-permute-start.11 = (bf16[16,2048]{1,0:T(8,128)(2,1)S(1)}, bf16[16,2048]{1,0:T(8,128)(2,1)S(1)}, u32[]{:S(2)}, u32[]{:S(2)}) collective-permute-start(bf16[16,2048]{1,0:T(8,128)(2,1)S(1)} %copy-done.2), channel_id=1, source_target_pairs={{0,3},{1,2},{2,1},{3,0},{4,7},{5,6},{6,5},{7,4},{8,11},{9,10},{10,... | collective-permute-start | bytes 196616 | tf_op jit(solution)/shard_map/ppermute | solution.py:23
  7.8 1.9 %collective-permute-start = (bf16[16,2176]{1,0:T(8,128)(2,1)S(1)}, bf16[16,2176]{1,0:T(8,128)(2,1)S(1)}, u32[]{:S(2)}, u32[]{:S(2)}) collective-permute-start(bf16[16,2176]{1,0:T(8,128)(2,1)S(1)} %shard_map.103.refs_0_.refs_7_), channel_id=1, source_target_pairs={{0,1},{1,0},{2,3},{3,2},{4,5},{5,4},{6,7},{7,6},{8,9},{9,8},{10,11... | collective-permute-start | bytes 208904 | tf_op jit(solution)/shard_map/ppermute | solution.py:23
  9.7 2.3 %collective-permute-done.11.refs_18_ = bf16[16,2048]{1,0:T(8,128)(2,1)S(1)} collective-permute-done((bf16[16,2048]{1,0:T(8,128)(2,1)S(1)}, bf16[16,2048]{1,0:T(8,128)(2,1)S(1)}, u32[]{:S(2)}, u32[]{:S(2)}) %collective-permute-start.11) | collective-permute-done | bytes 65568 | tf_op jit(solution)/shard_map/ppermute | solution.py:23
  12.1 0.5 %collective-permute-start.6 = (bf16[16,2176]{1,0:T(8,128)(2,1)S(1)}, bf16[16,2176]{1,0:T(8,128)(2,1)S(1)}, u32[]{:S(2)}, u32[]{:S(2)}) collective-permute-start(bf16[16,2176]{1,0:T(8,128)(2,1)S(1)} %collective-permute-done.2.refs_3_.refs_10_), channel_id=1, source_target_pairs={{0,4},{4,0},{8,12},{12,8},{16,20},{20,16},{24,28},{28,24},{1,5},{5... | collective-permute-start | bytes 208904 | tf_op jit(solution)/shard_map/ppermute | solution.py:23
  12.7 1.3 %collective-permute-start.9 = (bf16[16,2048]{1,0:T(8,128)(2,1)S(1)}, bf16[16,2048]{1,0:T(8,128)(2,1)S(1)}, u32[]{:S(2)}, u32[]{:S(2)}) collective-permute-start(bf16[16,2048]{1,0:T(8,128)(2,1)S(1)} %copy-done.2), channel_id=1, source_target_pairs={{0,1},{1,0},{2,3},{3,2},{4,5},{5,4},{6,7},{7,6},{8,9},{9,8},{10,11... | collective-permute-start | bytes 196616 | tf_op jit(solution)/shard_map/ppermute | solution.py:23
  13.9 3.2 %collective-permute-done.9.refs_16_ = bf16[16,2048]{1,0:T(8,128)(2,1)S(1)} collective-permute-done((bf16[16,2048]{1,0:T(8,128)(2,1)S(1)}, bf16[16,2048]{1,0:T(8,128)(2,1)S(1)}, u32[]{:S(2)}, u32[]{:S(2)}) %collective-permute-start.9) | collective-permute-done | bytes 65568 | tf_op jit(solution)/shard_map/ppermute | solution.py:23
  17.1 0.5 %collective-permute-start.15 = (bf16[16,2048]{1,0:T(8,128)(2,1)S(1)}, bf16[16,2048]{1,0:T(8,128)(2,1)S(1)}, u32[]{:S(2)}, u32[]{:S(2)}) collective-permute-start(bf16[16,2048]{1,0:T(8,128)(2,1)S(1)} %collective-permute-done.11.refs_18_), channel_id=1, source_target_pairs={{0,4},{4,0},{8,12},{12,8},{16,20},{20,16},{24,28},{28,24},{1,5},{5... | collective-permute-start | bytes 196616 | tf_op jit(solution)/shard_map/ppermute | solution.py:23
  17.7 0.4 collective-permute-start.13
  18.1 0.2 tables.1
  18.4 2.6 %collective-permute-start.8 = (f32[8,128]{1,0:T(8,128)S(1)}, f32[8,128]{1,0:T(8,128)S(1)}, u32[]{:S(2)}, u32[]{:S(2)}) collective-permute-start(f32[8,128]{1,0:T(8,128)S(1)} %get-tuple-element.17.refs_2_), channel_id=1, source_target_pairs={{0,16},{4,20},{8,24},{12,28},{16,0},{20,4},{24,8},{28,12},{1,17},{... | collective-permute-start | bytes 12296 | tf_op jit(solution)/shard_map/ppermute | solution.py:23
  21.0 1.6 %collective-permute-start.7 = (f32[8,128]{1,0:T(8,128)S(1)}, f32[8,128]{1,0:T(8,128)S(1)}, u32[]{:S(2)}, u32[]{:S(2)}) collective-permute-start(f32[8,128]{1,0:T(8,128)S(1)} %get-tuple-element.17.refs_2_), channel_id=1, source_target_pairs={{0,8},{4,12},{8,0},{12,4},{16,24},{20,28},{24,16},{28,20},{1,9},{5... | collective-permute-start | bytes 12296 | tf_op jit(solution)/shard_map/ppermute | solution.py:23
  22.6 0.3 collective-permute-done.8.refs_1_
  22.9 1.7 %collective-permute-done.7.refs_0_ = f32[8,128]{1,0:T(8,128)S(1)} collective-permute-done((f32[8,128]{1,0:T(8,128)S(1)}, f32[8,128]{1,0:T(8,128)S(1)}, u32[]{:S(2)}, u32[]{:S(2)}) %collective-permute-start.7) | collective-permute-done | bytes 4128 | tf_op jit(solution)/shard_map/ppermute | solution.py:23
  24.6 9.2 %shard_map.104 = (bf16[64,4224]{1,0:T(8,128)(2,1)S(1)}, bf16[64,4224]{1,0:T(8,128)(2,1)S(1)}) custom-call(s32[4]{0:T(128)S(1)} %copy-done.4, f32[8,128]{1,0:T(8,128)S(1)} %collective-permute-done.7.refs_0_, f32[8,128]{1,0:T(8,128)S(1)} %collective-permute-done.8.refs_1_, f32[8,128]{1,0:T(8,128)S(1)} %get-tuple-element.17.refs_2_, ...), custom_call_target="tpu_custom_call" | custom-call | tf_op jit(solution)/shard_map/pallas_call | solution.py:325
  33.9 1.9 %collective-permute-done.16.other = bf16[64,4224]{1,0:T(8,128)(2,1)S(1)} collective-permute-done((bf16[64,4224]{1,0:T(8,128)(2,1)S(1)}, bf16[64,4224]{1,0:T(8,128)(2,1)S(1)}, u32[]{:S(2)}, u32[]{:S(2)}) %collective-permute-start.16) | collective-permute-done | bytes 540704 | tf_op jit(solution)/shard_map/ppermute | solution.py:23
  35.9 1.2 %collective-permute-start.17 = (bf16[16,4224]{1,0:T(8,128)(2,1)S(1)}, bf16[16,4224]{1,0:T(8,128)(2,1)S(1)}, u32[]{:S(2)}, u32[]{:S(2)}) collective-permute-start(bf16[16,4224]{1,0:T(8,128)(2,1)S(1)} %get-tuple-element.25), channel_id=1, source_target_pairs={{0,1},{1,0},{2,3},{3,2},{4,5},{5,4},{6,7},{7,6},{8,9},{9,8},{10,11... | collective-permute-start | bytes 405512 | tf_op jit(solution)/shard_map/ppermute | solution.py:23
  37.1 0.9 %collective-permute-start.18 = (bf16[16,4224]{1,0:T(8,128)(2,1)S(1)}, bf16[16,4224]{1,0:T(8,128)(2,1)S(1)}, u32[]{:S(2)}, u32[]{:S(2)}) collective-permute-start(bf16[16,4224]{1,0:T(8,128)(2,1)S(1)} %get-tuple-element.26), channel_id=1, source_target_pairs={{0,2},{1,3},{2,0},{3,1},{4,6},{5,7},{6,4},{7,5},{8,10},{9,11},{10,... | collective-permute-start | bytes 405512 | tf_op jit(solution)/shard_map/ppermute | solution.py:23
  38.0 1.5 %collective-permute-start.19 = (bf16[16,4224]{1,0:T(8,128)(2,1)S(1)}, bf16[16,4224]{1,0:T(8,128)(2,1)S(1)}, u32[]{:S(2)}, u32[]{:S(2)}) collective-permute-start(bf16[16,4224]{1,0:T(8,128)(2,1)S(1)} %get-tuple-element.27), channel_id=1, source_target_pairs={{0,3},{1,2},{2,1},{3,0},{4,7},{5,6},{6,5},{7,4},{8,11},{9,10},{10,... | collective-permute-start | bytes 405512 | tf_op jit(solution)/shard_map/ppermute | solution.py:23
  39.5 3.0 %collective-permute-done.17.refs_1_ = bf16[16,4224]{1,0:T(8,128)(2,1)S(1)} collective-permute-done((bf16[16,4224]{1,0:T(8,128)(2,1)S(1)}, bf16[16,4224]{1,0:T(8,128)(2,1)S(1)}, u32[]{:S(2)}, u32[]{:S(2)}) %collective-permute-start.17) | collective-permute-done | bytes 135200 | tf_op jit(solution)/shard_map/ppermute | solution.py:23
  42.4 2.9 %collective-permute-done.18.refs_2_ = bf16[16,4224]{1,0:T(8,128)(2,1)S(1)} collective-permute-done((bf16[16,4224]{1,0:T(8,128)(2,1)S(1)}, bf16[16,4224]{1,0:T(8,128)(2,1)S(1)}, u32[]{:S(2)}, u32[]{:S(2)}) %collective-permute-start.18) | collective-permute-done | bytes 135200 | tf_op jit(solution)/shard_map/ppermute | solution.py:23
  45.3 0.7 %shard_map.106 = (bf16[16,2048]{1,0:T(8,128)(2,1)}, bf16[16,2048]{1,0:T(8,128)(2,1)}, f32[8,16]{1,0:T(8,128)}) custom-call(bf16[16,4224]{1,0:T(8,128)(2,1)S(1)} %get-tuple-element.24.refs_0_, bf16[16,4224]{1,0:T(8,128)(2,1)S(1)} %collective-permute-done.17.refs_1_, bf16[16,4224]{1,0:T(8,128)(2,1)S(1)} %collective-permute-done.18.refs_2_, ...), custom_call_target="tpu_custom_call" | custom-call | tf_op jit(solution)/shard_map/pallas_call | solution.py:345
  (31 shorter events, 0.5 us)
Async XLA Ops:
  0.6 24.0 %copy-start = (bf16[4,2048,1536]{2,1,0:T(8,128)(2,1)S(1)}, bf16[4,2048,1536]{2,1,0:T(8,128)(2,1)}, u32[]{:S(2)}) copy-start(bf16[4,2048,1536]{2,1,0:T(8,128)(2,1)} %refs_23_.1) | copy-start | bytes 75497472
  0.7 24.0 %copy-start.1 = (bf16[4,2048,768]{2,1,0:T(8,128)(2,1)S(1)}, bf16[4,2048,768]{2,1,0:T(8,128)(2,1)}, u32[]{:S(2)}) copy-start(bf16[4,2048,768]{2,1,0:T(8,128)(2,1)} %refs_24_.1) | copy-start | bytes 37748740
  0.7 23.9 %copy-start.4 = (s32[4]{0:T(128)S(1)}, s32[4]{0:T(128)}, u32[]{:S(2)}) copy-start(s32[4]{0:T(128)} %mask_ref.1) | copy-start | bytes 52
  1.7 43.6 %copy-start.3 = (s32[16,8]{0,1:T(8,128)S(1)}, s32[16,8]{0,1:T(8,128)}, u32[]{:S(2)}) copy-start(s32[16,8]{0,1:T(8,128)} %param.11) | copy-start | bytes 1540
  1.8 10.3 %collective-permute-start.2 = (bf16[16,2176]{1,0:T(8,128)(2,1)S(1)}, bf16[16,2176]{1,0:T(8,128)(2,1)S(1)}, u32[]{:S(2)}, u32[]{:S(2)}) collective-permute-start(bf16[16,2176]{1,0:T(8,128)(2,1)S(1)} %shard_map.103.refs_0_.refs_7_), channel_id=1, source_target_pairs={{0,3},{1,2},{2,1},{3,0},{4,7},{5,6},{6,5},{7,4},{8,11},{9,10},{10,... | collective-permute-start | bytes 208904 | tf_op jit(solution)/shard_map/ppermute | solution.py:23
  5.7 6.8 %collective-permute-start.1 = (bf16[16,2176]{1,0:T(8,128)(2,1)S(1)}, bf16[16,2176]{1,0:T(8,128)(2,1)S(1)}, u32[]{:S(2)}, u32[]{:S(2)}) collective-permute-start(bf16[16,2176]{1,0:T(8,128)(2,1)S(1)} %shard_map.103.refs_0_.refs_7_), channel_id=1, source_target_pairs={{0,2},{1,3},{2,0},{3,1},{4,6},{5,7},{6,4},{7,5},{8,10},{9,11},{10,... | collective-permute-start | bytes 208904 | tf_op jit(solution)/shard_map/ppermute | solution.py:23
  6.2 5.8 %collective-permute-start.11 = (bf16[16,2048]{1,0:T(8,128)(2,1)S(1)}, bf16[16,2048]{1,0:T(8,128)(2,1)S(1)}, u32[]{:S(2)}, u32[]{:S(2)}) collective-permute-start(bf16[16,2048]{1,0:T(8,128)(2,1)S(1)} %copy-done.2), channel_id=1, source_target_pairs={{0,3},{1,2},{2,1},{3,0},{4,7},{5,6},{6,5},{7,4},{8,11},{9,10},{10,... | collective-permute-start | bytes 196616 | tf_op jit(solution)/shard_map/ppermute | solution.py:23
  7.7 4.9 %collective-permute-start.10 = (bf16[16,2048]{1,0:T(8,128)(2,1)S(1)}, bf16[16,2048]{1,0:T(8,128)(2,1)S(1)}, u32[]{:S(2)}, u32[]{:S(2)}) collective-permute-start(bf16[16,2048]{1,0:T(8,128)(2,1)S(1)} %copy-done.2), channel_id=1, source_target_pairs={{0,2},{1,3},{2,0},{3,1},{4,6},{5,7},{6,4},{7,5},{8,10},{9,11},{10,... | collective-permute-start | bytes 196616 | tf_op jit(solution)/shard_map/ppermute | solution.py:23
  7.8 6.1 %collective-permute-start = (bf16[16,2176]{1,0:T(8,128)(2,1)S(1)}, bf16[16,2176]{1,0:T(8,128)(2,1)S(1)}, u32[]{:S(2)}, u32[]{:S(2)}) collective-permute-start(bf16[16,2176]{1,0:T(8,128)(2,1)S(1)} %shard_map.103.refs_0_.refs_7_), channel_id=1, source_target_pairs={{0,1},{1,0},{2,3},{3,2},{4,5},{5,4},{6,7},{7,6},{8,9},{9,8},{10,11... | collective-permute-start | bytes 208904 | tf_op jit(solution)/shard_map/ppermute | solution.py:23
  12.1 5.0 %collective-permute-start.3 = (bf16[16,2176]{1,0:T(8,128)(2,1)S(1)}, bf16[16,2176]{1,0:T(8,128)(2,1)S(1)}, u32[]{:S(2)}, u32[]{:S(2)}) collective-permute-start(bf16[16,2176]{1,0:T(8,128)(2,1)S(1)} %shard_map.103.refs_0_.refs_7_), channel_id=1, source_target_pairs={{0,4},{4,0},{8,12},{12,8},{16,20},{20,16},{24,28},{28,24},{1,5},{5... | collective-permute-start | bytes 208904 | tf_op jit(solution)/shard_map/ppermute | solution.py:23
  12.1 5.5 %collective-permute-start.6 = (bf16[16,2176]{1,0:T(8,128)(2,1)S(1)}, bf16[16,2176]{1,0:T(8,128)(2,1)S(1)}, u32[]{:S(2)}, u32[]{:S(2)}) collective-permute-start(bf16[16,2176]{1,0:T(8,128)(2,1)S(1)} %collective-permute-done.2.refs_3_.refs_10_), channel_id=1, source_target_pairs={{0,4},{4,0},{8,12},{12,8},{16,20},{20,16},{24,28},{28,24},{1,5},{5... | collective-permute-start | bytes 208904 | tf_op jit(solution)/shard_map/ppermute | solution.py:23
  12.6 5.1 %collective-permute-start.5 = (bf16[16,2176]{1,0:T(8,128)(2,1)S(1)}, bf16[16,2176]{1,0:T(8,128)(2,1)S(1)}, u32[]{:S(2)}, u32[]{:S(2)}) collective-permute-start(bf16[16,2176]{1,0:T(8,128)(2,1)S(1)} %collective-permute-done.1.refs_2_.refs_9_), channel_id=1, source_target_pairs={{0,4},{4,0},{8,12},{12,8},{16,20},{20,16},{24,28},{28,24},{1,5},{5... | collective-permute-start | bytes 208904 | tf_op jit(solution)/shard_map/ppermute | solution.py:23
  12.7 4.4 %collective-permute-start.9 = (bf16[16,2048]{1,0:T(8,128)(2,1)S(1)}, bf16[16,2048]{1,0:T(8,128)(2,1)S(1)}, u32[]{:S(2)}, u32[]{:S(2)}) collective-permute-start(bf16[16,2048]{1,0:T(8,128)(2,1)S(1)} %copy-done.2), channel_id=1, source_target_pairs={{0,1},{1,0},{2,3},{3,2},{4,5},{5,4},{6,7},{7,6},{8,9},{9,8},{10,11... | collective-permute-start | bytes 196616 | tf_op jit(solution)/shard_map/ppermute | solution.py:23
  13.9 4.2 %collective-permute-start.4 = (bf16[16,2176]{1,0:T(8,128)(2,1)S(1)}, bf16[16,2176]{1,0:T(8,128)(2,1)S(1)}, u32[]{:S(2)}, u32[]{:S(2)}) collective-permute-start(bf16[16,2176]{1,0:T(8,128)(2,1)S(1)} %collective-permute-done.refs_1_.refs_8_), channel_id=1, source_target_pairs={{0,4},{4,0},{8,12},{12,8},{16,20},{20,16},{24,28},{28,24},{1,5},{5... | collective-permute-start | bytes 208904 | tf_op jit(solution)/shard_map/ppermute | solution.py:23
  17.1 3.9 %collective-permute-start.12 = (bf16[16,2048]{1,0:T(8,128)(2,1)S(1)}, bf16[16,2048]{1,0:T(8,128)(2,1)S(1)}, u32[]{:S(2)}, u32[]{:S(2)}) collective-permute-start(bf16[16,2048]{1,0:T(8,128)(2,1)S(1)} %copy-done.2), channel_id=1, source_target_pairs={{0,4},{4,0},{8,12},{12,8},{16,20},{20,16},{24,28},{28,24},{1,5},{5... | collective-permute-start | bytes 196616 | tf_op jit(solution)/shard_map/ppermute | solution.py:23
  17.1 5.5 %collective-permute-start.15 = (bf16[16,2048]{1,0:T(8,128)(2,1)S(1)}, bf16[16,2048]{1,0:T(8,128)(2,1)S(1)}, u32[]{:S(2)}, u32[]{:S(2)}) collective-permute-start(bf16[16,2048]{1,0:T(8,128)(2,1)S(1)} %collective-permute-done.11.refs_18_), channel_id=1, source_target_pairs={{0,4},{4,0},{8,12},{12,8},{16,20},{20,16},{24,28},{28,24},{1,5},{5... | collective-permute-start | bytes 196616 | tf_op jit(solution)/shard_map/ppermute | solution.py:23
  17.6 5.0 %collective-permute-start.14 = (bf16[16,2048]{1,0:T(8,128)(2,1)S(1)}, bf16[16,2048]{1,0:T(8,128)(2,1)S(1)}, u32[]{:S(2)}, u32[]{:S(2)}) collective-permute-start(bf16[16,2048]{1,0:T(8,128)(2,1)S(1)} %collective-permute-done.10.refs_17_), channel_id=1, source_target_pairs={{0,4},{4,0},{8,12},{12,8},{16,20},{20,16},{24,28},{28,24},{1,5},{5... | collective-permute-start | bytes 196616 | tf_op jit(solution)/shard_map/ppermute | solution.py:23
  17.7 4.9 %collective-permute-start.13 = (bf16[16,2048]{1,0:T(8,128)(2,1)S(1)}, bf16[16,2048]{1,0:T(8,128)(2,1)S(1)}, u32[]{:S(2)}, u32[]{:S(2)}) collective-permute-start(bf16[16,2048]{1,0:T(8,128)(2,1)S(1)} %collective-permute-done.9.refs_16_), channel_id=1, source_target_pairs={{0,4},{4,0},{8,12},{12,8},{16,20},{20,16},{24,28},{28,24},{1,5},{5... | collective-permute-start | bytes 196616 | tf_op jit(solution)/shard_map/ppermute | solution.py:23
  18.4 4.5 %collective-permute-start.8 = (f32[8,128]{1,0:T(8,128)S(1)}, f32[8,128]{1,0:T(8,128)S(1)}, u32[]{:S(2)}, u32[]{:S(2)}) collective-permute-start(f32[8,128]{1,0:T(8,128)S(1)} %get-tuple-element.17.refs_2_), channel_id=1, source_target_pairs={{0,16},{4,20},{8,24},{12,28},{16,0},{20,4},{24,8},{28,12},{1,17},{... | collective-permute-start | bytes 12296 | tf_op jit(solution)/shard_map/ppermute | solution.py:23
  21.0 3.6 %collective-permute-start.7 = (f32[8,128]{1,0:T(8,128)S(1)}, f32[8,128]{1,0:T(8,128)S(1)}, u32[]{:S(2)}, u32[]{:S(2)}) collective-permute-start(f32[8,128]{1,0:T(8,128)S(1)} %get-tuple-element.17.refs_2_), channel_id=1, source_target_pairs={{0,8},{4,12},{8,0},{12,4},{16,24},{20,28},{24,16},{28,20},{1,9},{5... | collective-permute-start | bytes 12296 | tf_op jit(solution)/shard_map/ppermute | solution.py:23
  33.8 2.0 %collective-permute-start.16 = (bf16[64,4224]{1,0:T(8,128)(2,1)S(1)}, bf16[64,4224]{1,0:T(8,128)(2,1)S(1)}, u32[]{:S(2)}, u32[]{:S(2)}) collective-permute-start(bf16[64,4224]{1,0:T(8,128)(2,1)S(1)} %get-tuple-element.23), channel_id=1, source_target_pairs={{0,4},{4,0},{8,12},{12,8},{16,20},{20,16},{24,28},{28,24},{1,5},{5... | collective-permute-start | bytes 1622024 | tf_op jit(solution)/shard_map/ppermute | solution.py:23
  35.9 6.5 %collective-permute-start.17 = (bf16[16,4224]{1,0:T(8,128)(2,1)S(1)}, bf16[16,4224]{1,0:T(8,128)(2,1)S(1)}, u32[]{:S(2)}, u32[]{:S(2)}) collective-permute-start(bf16[16,4224]{1,0:T(8,128)(2,1)S(1)} %get-tuple-element.25), channel_id=1, source_target_pairs={{0,1},{1,0},{2,3},{3,2},{4,5},{5,4},{6,7},{7,6},{8,9},{9,8},{10,11... | collective-permute-start | bytes 405512 | tf_op jit(solution)/shard_map/ppermute | solution.py:23
  37.1 8.2 %collective-permute-start.18 = (bf16[16,4224]{1,0:T(8,128)(2,1)S(1)}, bf16[16,4224]{1,0:T(8,128)(2,1)S(1)}, u32[]{:S(2)}, u32[]{:S(2)}) collective-permute-start(bf16[16,4224]{1,0:T(8,128)(2,1)S(1)} %get-tuple-element.26), channel_id=1, source_target_pairs={{0,2},{1,3},{2,0},{3,1},{4,6},{5,7},{6,4},{7,5},{8,10},{9,11},{10,... | collective-permute-start | bytes 405512 | tf_op jit(solution)/shard_map/ppermute | solution.py:23
  38.0 7.3 %collective-permute-start.19 = (bf16[16,4224]{1,0:T(8,128)(2,1)S(1)}, bf16[16,4224]{1,0:T(8,128)(2,1)S(1)}, u32[]{:S(2)}, u32[]{:S(2)}) collective-permute-start(bf16[16,4224]{1,0:T(8,128)(2,1)S(1)} %get-tuple-element.27), channel_id=1, source_target_pairs={{0,3},{1,2},{2,1},{3,0},{4,7},{5,6},{6,5},{7,4},{8,11},{9,10},{10,... | collective-permute-start | bytes 405512 | tf_op jit(solution)/shard_map/ppermute | solution.py:23
  (1 other events, 5.6 us)

commit v5 on v4

--- a/solution.py
+++ b/solution.py
@@ -21,6 +21,11 @@
 
 def swapped(shard, axis, mask):
     return lax.ppermute(shard, axis, [(i, i ^ mask) for i in range(lax.axis_size(axis))])
+
+
+def swapped_by_core(shard, even, odd):
+    pairs = [(i, i ^ (odd if i % 2 else even)) for i in range(lax.axis_size("dp"))]
+    return lax.ppermute(shard, "dp", pairs)
 
 
 def iota(shape, axis):
@@ -116,31 +121,41 @@
     return jnp.sum(jnp.where(iota(columns.shape, 1) == index, columns, 0.0), axis=1, keepdims=True)
 
 
+def back_kernel(groups, local_count, *refs):
+    grds, (down, back, grd) = refs[:-3], refs[-3:]
+    _, first_local = place_of(groups, local_count)
+    piece_rows = grd.shape[0] // len(grds)
+    for n, piece in enumerate(grds):
+        grd[pl.ds(n * piece_rows, piece_rows), :] = piece[...]
+    g = grd[...]
+    for i in range(back.shape[0]):
+        for j in range(back.shape[2] // STEP):
+            cols = pl.ds(j * STEP, STEP)
+            back[i, :, cols] = jnp.dot(g, down[first_local + i, :, cols], preferred_element_type=jnp.float32)
+
+
 def first_kernel(groups, local_count, count, width, *refs):
-    toks, grds = refs[:count], refs[count : 2 * count]
-    gate_t, gate_up, down, hid, dpre, grads, tok, grd = refs[2 * count :]
+    toks, (backs, gate_t, gate_up, hid, dpre, grads, tok) = refs[:count], refs[count:]
     _, first_local = place_of(groups, local_count)
     rows = tok.shape[0]
     piece_rows = rows // count
-    hidden_units = down.shape[2]
+    hidden_units = hid.shape[2]
     for n in range(count):
-        at = pl.ds(n * piece_rows, piece_rows)
-        tok[at, :] = toks[n][:, :width]
-        grd[at, :] = grds[n][...]
+        tok[pl.ds(n * piece_rows, piece_rows), :] = toks[n][:, :width]
     gates = to_columns(gate_t[...], rows)
     lane = iota((rows, LANES), 1)
-
-    def one_expert(i, gate_grads):
+    t = tok[...]
+    gate_grads = jnp.zeros((rows, LANES), jnp.float32)
+    for i in range(hid.shape[0]):
         e = first_local + i
         weight = lane_of(gates, e)
-        t, g = tok[...], grd[...]
         total = jnp.zeros((rows, 1), jnp.float32)
         for j in range(hidden_units // STEP):
             cols = pl.ds(j * STEP, STEP)
             ups = pl.ds(hidden_units + j * STEP, STEP)
             a = jnp.dot(t, gate_up[e, :, cols], preferred_element_type=jnp.float32)
             b = jnp.dot(t, gate_up[e, :, ups], preferred_element_type=jnp.float32)
-            back = jnp.dot(g, down[e, :, cols], preferred_element_type=jnp.float32)
+            back = backs[i, :, cols]
             s = jax.nn.sigmoid(a)
             swish = a * s
             hidden = swish * b
@@ -149,15 +164,17 @@
             hid[i, :, cols] = (hidden * weight).astype(jnp.bfloat16)
             dpre[i, :, cols] = (back * b * s * (1.0 + a * (1.0 - s))).astype(jnp.bfloat16)
             dpre[i, :, ups] = (back * swish).astype(jnp.bfloat16)
-        return jnp.where(lane == e, total, gate_grads)
-
-    grads[...] = lax.fori_loop(0, local_count // groups, one_expert, jnp.zeros((rows, LANES), jnp.float32))
+        gate_grads = jnp.where(lane == e, total, gate_grads)
+    grads[...] = gate_grads
 
 
 def second_kernel(groups, local_count, width, levels, mask_ref, *refs):
-    far = refs[: len(levels)]
-    (spare, named_t, place_t, cap_t, hid, dpre, grads, gate_up, down) = refs[len(levels) : len(levels) + 9]
-    outs = refs[len(levels) + 9 : len(levels) + 9 + groups]
+    far_pairs = []
+    for even, odd in levels:
+        n = 1 if even == odd else 2
+        far_pairs.append(refs[:n])
+        refs = refs[n:]
+    (spare, named_t, place_t, cap_t, hid, dpre, grads, gate_up, down), outs = refs[:9], refs[9 : 9 + groups]
     first_expert, first_local = place_of(groups, local_count)
     rows = hid.shape[1]
     group_rows = rows // groups
@@ -171,8 +188,14 @@
         other = jnp.zeros((SUB, 1), jnp.float32)
         if groups == 2:
             other = jnp.where(mask == 1, spare[:, 1 - g : 2 - g], other)
-        for level, ref in zip(levels, far):
-            other = jnp.where(mask == level, ref[:, g : g + 1], other)
+        for (even, odd), refs_at in zip(levels, far_pairs):
+            if even == odd:
+                other = jnp.where(mask == even, refs_at[0][:, g : g + 1], other)
+                continue
+            core = lax.axis_index("dp") % 2
+            level, crossed = jnp.where(core == 0, even, odd), jnp.where(core == 0, odd, even)
+            other = jnp.where(mask == level, refs_at[0][:, g : g + 1], other)
+            other = jnp.where(mask == crossed, refs_at[1][:, 1 - g : 2 - g], other)
         limit = jnp.where(group_of == g, cap_t[:, g : g + 1] + jnp.minimum(other, float(OVF)), limit)
     kept = jnp.where((named_t[...] > 0.0) & (place_t[...] < limit), 1.0, 0.0)
     kept = to_columns(kept, rows)
@@ -207,13 +230,13 @@
 
 
 def experts_kernel(groups, local_count, count, width, levels, mask_ref, *refs):
-    n = len(levels)
+    n = sum(1 if even == odd else 2 for even, odd in levels)
     far, refs = refs[:n], refs[n:]
     (spare, named_t, place_t, cap_t, gate_t), refs = refs[:5], refs[5:]
-    pieces, refs = refs[: 2 * count], refs[2 * count :]
+    toks, backs, refs = refs[:count], refs[count], refs[count + 1 :]
     (gate_up, down), refs = refs[:2], refs[2:]
-    outs, (tok, grd, hid, dpre, grads) = refs[:groups], refs[groups:]
-    first_kernel(groups, local_count, count, width, *pieces, gate_t, gate_up, down, hid, dpre, grads, tok, grd)
+    outs, (tok, hid, dpre, grads) = refs[:groups], refs[groups:]
+    first_kernel(groups, local_count, count, width, *toks, backs, gate_t, gate_up, hid, dpre, grads, tok)
     second_kernel(
         groups, local_count, width, levels, mask_ref,
         *far, spare, named_t, place_t, cap_t, hid, dpre, grads, gate_up, down, *outs,
@@ -318,23 +341,35 @@
         compiler_params=pltpu.CompilerParams(vmem_limit_bytes=4 * MIB),
         name="tables",
     )(*toks)
-    levels = tuple(1 << b for b in range(groups - 1, replicas.bit_length() - 1))
-    far = [swapped(spare, "dp", level) for level in levels]
-
     group_rows = rows // groups
+    masks = [1 << b for b in range(groups - 1, replicas.bit_length() - 1)]
+    if groups == 2:
+        levels = tuple(zip(masks[::2], masks[1::2])) + ((masks[-1],) * 2,) * (len(masks) % 2)
+    else:
+        levels = tuple(zip(masks, masks))
+    far = []
+    for even, odd in levels:
+        far.append(swapped_by_core(spare, even, odd))
+        if even != odd:
+            far.append(swapped(far[-1], "dp", 1))
+    backs = kernel(
+        functools.partial(back_kernel, groups, local_count),
+        array((per_device, rows, hidden_units), f32),
+        [vm] * (count + 1),
+        [VM((rows, width), bf16)],
+    )(*grds, down)
     parts = kernel(
         functools.partial(experts_kernel, groups, local_count, count, width, levels),
         [array((group_rows, total_width), bf16)] * groups,
-        [sm] + [vm] * (len(far) + 7 + 2 * count),
+        [sm] + [vm] * (len(far) + 8 + count),
         [
-            VM((rows, width), bf16),
             VM((rows, width), bf16),
             VM((per_device, rows, hidden_units), bf16),
             VM((per_device, rows, 2 * hidden_units), bf16),
             VM((rows, LANES), f32),
         ],
-        12,
-    )(pair_mask, *far, spare, named_t, place_t, cap_t, gate_t, *toks, *grds, gate_up, down)
+        8,
+    )(pair_mask, *far, spare, named_t, place_t, cap_t, gate_t, *toks, backs, gate_up, down)
     block = array((tok_count, total_width), bf16)
     if groups == 2:
         other = swapped(parts[1], "dp", 1)

time: 46.2 us -> 43.5 us (0.942)
  starting transfers between devices: 18.6 us -> 16.5 us
  Pallas kernels: 11.3 us -> 10.7 us
    ppermute x20 -> x19, starting transfers between devices: 18.6 us -> 14.9 us  [swapped(): lax.ppermute(shard, axis, [(i, i ^ mask) for i in range(lax.axis_size(axi...]
    ppermute x0 -> x1, waiting for transfers between devices: none -> 2.07 us  [swapped_by_core(): return lax.ppermute(shard, 'dp', pairs)]
    ppermute x20 -> x19, waiting for transfers between devices: 15.3 us -> 13.3 us  [swapped(): lax.ppermute(shard, axis, [(i, i ^ mask) for i in range(lax.axis_size(axi...]
    ppermute x0 -> x1, starting transfers between devices: none -> 1.61 us  [swapped_by_core(): return lax.ppermute(shard, 'dp', pairs)]
    pallas_call x1, Pallas kernels: 9.17 us -> 7.59 us  [body(): kernel(functools.partial(experts_kernel, groups, local_count, count, widt...]
    pallas_call x0 -> x1, Pallas kernels: none -> 1 us  [body(): kernel(functools.partial(back_kernel, groups, local_count), array((per_de...]
  transfers between devices with their start and end apart: 20 -> 20, of which waited for: 7 -> 7; matrix products, arithmetic and copies ran while one was open for 0% -> 0% of each run, Pallas kernels for 1% -> 3%
where the time goes in v5:
time: 43.5 us; the launch traced here: 43.4 us
  starting transfers between devices  16.5 us (38%)
  waiting for transfers between devices  15.4 us (35%)
  Pallas kernels  10.7 us (25%)
  between operations  0.82 us (2%)
    ppermute x19, starting transfers between devices, swapped(): lax.ppermute(shard, axis, [(i, i ^ mask) for i in range(lax.axis_size(axi...  14.9 us
    ppermute x19, waiting for transfers between devices, swapped(): lax.ppermute(shard, axis, [(i, i ^ mask) for i in range(lax.axis_size(axi...  13.3 us
    pallas_call x1, Pallas kernels, body(): kernel(functools.partial(experts_kernel, groups, local_count, count, widt...  7.59 us
    ppermute x1, waiting for transfers between devices, swapped_by_core(): return lax.ppermute(shard, 'dp', pairs)  2.07 us
    ppermute x1, starting transfers between devices, swapped_by_core(): return lax.ppermute(shard, 'dp', pairs)  1.61 us
    pallas_call x1, Pallas kernels, body(): kernel(prep_kernel, array((tok_count, width + LANES), bf16), [hbm] * 3 +...  1.03 us
    pallas_call x1, Pallas kernels, body(): kernel(functools.partial(back_kernel, groups, local_count), array((per_de...  1 us
  transfers between devices with their start and end apart: 20, of which 7 were waited for; matrix products, arithmetic and copies ran while one was open for 0% of the time, Pallas kernels for 3%

profile of v5, /device:TPU:0, one launch (start us, length us, event | category | flops | bytes accessed | tf_op | source)
XLA Modules:
  0.0 43.4 jit_solution(9927376297680573048)
XLA Ops:
  0.7 1.0 %shard_map.103.refs_0_.refs_7_ = bf16[16,2176]{1,0:T(8,128)(2,1)S(1)} custom-call(bf16[16,2048]{1,0:T(8,128)(2,1)} %tokens.1, s32[8,16]{1,0:T(8,128)} %bitcast.5, bf16[8,16]{1,0:T(8,128)(2,1)} %bitcast.8, s32[1,4]{1,0:T(1,128)} %capacity.1), custom_call_target="tpu_custom_call" | custom-call | flops 20000000000 | tf_op jit(solution)/shard_map/pallas_call | solution.py:304
  1.8 4.0 %collective-permute-start.2 = (bf16[16,2176]{1,0:T(8,128)(2,1)S(1)}, bf16[16,2176]{1,0:T(8,128)(2,1)S(1)}, u32[]{:S(2)}, u32[]{:S(2)}) collective-permute-start(bf16[16,2176]{1,0:T(8,128)(2,1)S(1)} %shard_map.103.refs_0_.refs_7_), channel_id=1, source_target_pairs={{0,3},{1,2},{2,1},{3,0},{4,7},{5,6},{6,5},{7,4},{8,11},{9,10},{10,... | collective-permute-start | bytes 208904 | tf_op jit(solution)/shard_map/ppermute | solution.py:23
  5.8 0.5 %collective-permute-start.1 = (bf16[16,2176]{1,0:T(8,128)(2,1)S(1)}, bf16[16,2176]{1,0:T(8,128)(2,1)S(1)}, u32[]{:S(2)}, u32[]{:S(2)}) collective-permute-start(bf16[16,2176]{1,0:T(8,128)(2,1)S(1)} %shard_map.103.refs_0_.refs_7_), channel_id=1, source_target_pairs={{0,2},{1,3},{2,0},{3,1},{4,6},{5,7},{6,4},{7,5},{8,10},{9,11},{10,... | collective-permute-start | bytes 208904 | tf_op jit(solution)/shard_map/ppermute | solution.py:23
  6.3 1.5 %collective-permute-start.11 = (bf16[16,2048]{1,0:T(8,128)(2,1)S(1)}, bf16[16,2048]{1,0:T(8,128)(2,1)S(1)}, u32[]{:S(2)}, u32[]{:S(2)}) collective-permute-start(bf16[16,2048]{1,0:T(8,128)(2,1)S(1)} %copy-done.1), channel_id=1, source_target_pairs={{0,3},{1,2},{2,1},{3,0},{4,7},{5,6},{6,5},{7,4},{8,11},{9,10},{10,... | collective-permute-start | bytes 196616 | tf_op jit(solution)/shard_map/ppermute | solution.py:23
  7.9 1.9 %collective-permute-start = (bf16[16,2176]{1,0:T(8,128)(2,1)S(1)}, bf16[16,2176]{1,0:T(8,128)(2,1)S(1)}, u32[]{:S(2)}, u32[]{:S(2)}) collective-permute-start(bf16[16,2176]{1,0:T(8,128)(2,1)S(1)} %shard_map.103.refs_0_.refs_7_), channel_id=1, source_target_pairs={{0,1},{1,0},{2,3},{3,2},{4,5},{5,4},{6,7},{7,6},{8,9},{9,8},{10,11... | collective-permute-start | bytes 208904 | tf_op jit(solution)/shard_map/ppermute | solution.py:23
  9.8 2.3 %collective-permute-done.11.refs_3_ = bf16[16,2048]{1,0:T(8,128)(2,1)S(1)} collective-permute-done((bf16[16,2048]{1,0:T(8,128)(2,1)S(1)}, bf16[16,2048]{1,0:T(8,128)(2,1)S(1)}, u32[]{:S(2)}, u32[]{:S(2)}) %collective-permute-start.11) | collective-permute-done | bytes 65568 | tf_op jit(solution)/shard_map/ppermute | solution.py:23
  12.1 0.5 %collective-permute-start.6 = (bf16[16,2176]{1,0:T(8,128)(2,1)S(1)}, bf16[16,2176]{1,0:T(8,128)(2,1)S(1)}, u32[]{:S(2)}, u32[]{:S(2)}) collective-permute-start(bf16[16,2176]{1,0:T(8,128)(2,1)S(1)} %collective-permute-done.2.refs_3_.refs_10_), channel_id=1, source_target_pairs={{0,4},{4,0},{8,12},{12,8},{16,20},{20,16},{24,28},{28,24},{1,5},{5... | collective-permute-start | bytes 208904 | tf_op jit(solution)/shard_map/ppermute | solution.py:23
  12.7 1.3 %collective-permute-start.9 = (bf16[16,2048]{1,0:T(8,128)(2,1)S(1)}, bf16[16,2048]{1,0:T(8,128)(2,1)S(1)}, u32[]{:S(2)}, u32[]{:S(2)}) collective-permute-start(bf16[16,2048]{1,0:T(8,128)(2,1)S(1)} %copy-done.1), channel_id=1, source_target_pairs={{0,1},{1,0},{2,3},{3,2},{4,5},{5,4},{6,7},{7,6},{8,9},{9,8},{10,11... | collective-permute-start | bytes 196616 | tf_op jit(solution)/shard_map/ppermute | solution.py:23
  13.9 3.2 %collective-permute-done.9.refs_1_ = bf16[16,2048]{1,0:T(8,128)(2,1)S(1)} collective-permute-done((bf16[16,2048]{1,0:T(8,128)(2,1)S(1)}, bf16[16,2048]{1,0:T(8,128)(2,1)S(1)}, u32[]{:S(2)}, u32[]{:S(2)}) %collective-permute-start.9) | collective-permute-done | bytes 65568 | tf_op jit(solution)/shard_map/ppermute | solution.py:23
  17.1 0.5 %collective-permute-start.15 = (bf16[16,2048]{1,0:T(8,128)(2,1)S(1)}, bf16[16,2048]{1,0:T(8,128)(2,1)S(1)}, u32[]{:S(2)}, u32[]{:S(2)}) collective-permute-start(bf16[16,2048]{1,0:T(8,128)(2,1)S(1)} %collective-permute-done.11.refs_3_), channel_id=1, source_target_pairs={{0,4},{4,0},{8,12},{12,8},{16,20},{20,16},{24,28},{28,24},{1,5},{5... | collective-permute-start | bytes 196616 | tf_op jit(solution)/shard_map/ppermute | solution.py:23
  17.7 0.4 %collective-permute-start.13 = (bf16[16,2048]{1,0:T(8,128)(2,1)S(1)}, bf16[16,2048]{1,0:T(8,128)(2,1)S(1)}, u32[]{:S(2)}, u32[]{:S(2)}) collective-permute-start(bf16[16,2048]{1,0:T(8,128)(2,1)S(1)} %collective-permute-done.9.refs_1_), channel_id=1, source_target_pairs={{0,4},{4,0},{8,12},{12,8},{16,20},{20,16},{24,28},{28,24},{1,5},{5... | collective-permute-start | bytes 196616 | tf_op jit(solution)/shard_map/ppermute | solution.py:23
  18.1 0.2 tables.1
  18.4 1.6 %collective-permute-start.7 = (f32[8,128]{1,0:T(8,128)S(1)}, f32[8,128]{1,0:T(8,128)S(1)}, u32[]{:S(2)}, u32[]{:S(2)}) collective-permute-start(f32[8,128]{1,0:T(8,128)S(1)} %get-tuple-element.17.refs_2_), channel_id=1, source_target_pairs={{0,8},{4,20},{8,0},{12,28},{16,24},{20,4},{24,16},{28,12},{1,9},{5... | collective-permute-start | bytes 12296 | tf_op jit(solution)/shard_map/ppermute | solution.py:28
  20.0 2.1 %collective-permute-done.7.refs_0_ = f32[8,128]{1,0:T(8,128)S(1)} collective-permute-done((f32[8,128]{1,0:T(8,128)S(1)}, f32[8,128]{1,0:T(8,128)S(1)}, u32[]{:S(2)}, u32[]{:S(2)}) %collective-permute-start.7) | collective-permute-done | bytes 4128 | tf_op jit(solution)/shard_map/ppermute | solution.py:28
  22.1 1.0 %shard_map.104.refs_15_ = f32[2,128,768]{2,1,0:T(8,128)S(1)} custom-call(bf16[16,2048]{1,0:T(8,128)(2,1)S(1)} %copy-done.1, bf16[16,2048]{1,0:T(8,128)(2,1)S(1)} %collective-permute-done.9.refs_1_, bf16[16,2048]{1,0:T(8,128)(2,1)S(1)} %collective-permute-done.10.refs_2_, bf16[16,2048]{1,0:T(8,128)(2,1)S(1)} %collective-permute-done.11.refs_3_, ...), custom_call_target="tpu_custom_call" | custom-call | tf_op jit(solution)/shard_map/pallas_call | solution.py:355
  23.3 7.6 %shard_map.105 = (bf16[64,4224]{1,0:T(8,128)(2,1)S(1)}, bf16[64,4224]{1,0:T(8,128)(2,1)S(1)}) custom-call(s32[4]{0:T(128)S(1)} %copy-done.3, f32[8,128]{1,0:T(8,128)S(1)} %collective-permute-done.7.refs_0_, f32[8,128]{1,0:T(8,128)S(1)} %collective-permute-done.8.refs_1_, f32[8,128]{1,0:T(8,128)S(1)} %get-tuple-element.17.refs_2_, ...), custom_call_target="tpu_custom_call" | custom-call | tf_op jit(solution)/shard_map/pallas_call | solution.py:361
  30.9 0.5 %collective-permute-start.16 = (bf16[64,4224]{1,0:T(8,128)(2,1)S(1)}, bf16[64,4224]{1,0:T(8,128)(2,1)S(1)}, u32[]{:S(2)}, u32[]{:S(2)}) collective-permute-start(bf16[64,4224]{1,0:T(8,128)(2,1)S(1)} %get-tuple-element.23), channel_id=1, source_target_pairs={{0,4},{4,0},{8,12},{12,8},{16,20},{20,16},{24,28},{28,24},{1,5},{5... | collective-permute-start | bytes 1622024 | tf_op jit(solution)/shard_map/ppermute | solution.py:23
  31.4 1.6 %collective-permute-done.16.other = bf16[64,4224]{1,0:T(8,128)(2,1)S(1)} collective-permute-done((bf16[64,4224]{1,0:T(8,128)(2,1)S(1)}, bf16[64,4224]{1,0:T(8,128)(2,1)S(1)}, u32[]{:S(2)}, u32[]{:S(2)}) %collective-permute-start.16) | collective-permute-done | bytes 540704 | tf_op jit(solution)/shard_map/ppermute | solution.py:23
  33.1 1.1 %collective-permute-start.17 = (bf16[16,4224]{1,0:T(8,128)(2,1)S(1)}, bf16[16,4224]{1,0:T(8,128)(2,1)S(1)}, u32[]{:S(2)}, u32[]{:S(2)}) collective-permute-start(bf16[16,4224]{1,0:T(8,128)(2,1)S(1)} %get-tuple-element.25), channel_id=1, source_target_pairs={{0,1},{1,0},{2,3},{3,2},{4,5},{5,4},{6,7},{7,6},{8,9},{9,8},{10,11... | collective-permute-start | bytes 405512 | tf_op jit(solution)/shard_map/ppermute | solution.py:23
  34.2 0.9 %collective-permute-start.18 = (bf16[16,4224]{1,0:T(8,128)(2,1)S(1)}, bf16[16,4224]{1,0:T(8,128)(2,1)S(1)}, u32[]{:S(2)}, u32[]{:S(2)}) collective-permute-start(bf16[16,4224]{1,0:T(8,128)(2,1)S(1)} %get-tuple-element.26), channel_id=1, source_target_pairs={{0,2},{1,3},{2,0},{3,1},{4,6},{5,7},{6,4},{7,5},{8,10},{9,11},{10,... | collective-permute-start | bytes 405512 | tf_op jit(solution)/shard_map/ppermute | solution.py:23
  35.1 1.5 %collective-permute-start.19 = (bf16[16,4224]{1,0:T(8,128)(2,1)S(1)}, bf16[16,4224]{1,0:T(8,128)(2,1)S(1)}, u32[]{:S(2)}, u32[]{:S(2)}) collective-permute-start(bf16[16,4224]{1,0:T(8,128)(2,1)S(1)} %get-tuple-element.27), channel_id=1, source_target_pairs={{0,3},{1,2},{2,1},{3,0},{4,7},{5,6},{6,5},{7,4},{8,11},{9,10},{10,... | collective-permute-start | bytes 405512 | tf_op jit(solution)/shard_map/ppermute | solution.py:23
  36.6 3.0 %collective-permute-done.17.refs_1_ = bf16[16,4224]{1,0:T(8,128)(2,1)S(1)} collective-permute-done((bf16[16,4224]{1,0:T(8,128)(2,1)S(1)}, bf16[16,4224]{1,0:T(8,128)(2,1)S(1)}, u32[]{:S(2)}, u32[]{:S(2)}) %collective-permute-start.17) | collective-permute-done | bytes 135200 | tf_op jit(solution)/shard_map/ppermute | solution.py:23
  39.6 3.1 %collective-permute-done.18.refs_2_ = bf16[16,4224]{1,0:T(8,128)(2,1)S(1)} collective-permute-done((bf16[16,4224]{1,0:T(8,128)(2,1)S(1)}, bf16[16,4224]{1,0:T(8,128)(2,1)S(1)}, u32[]{:S(2)}, u32[]{:S(2)}) %collective-permute-start.18) | collective-permute-done | bytes 135200 | tf_op jit(solution)/shard_map/ppermute | solution.py:23
  42.7 0.7 %shard_map.107 = (bf16[16,2048]{1,0:T(8,128)(2,1)}, bf16[16,2048]{1,0:T(8,128)(2,1)}, f32[8,16]{1,0:T(8,128)}) custom-call(bf16[16,4224]{1,0:T(8,128)(2,1)S(1)} %get-tuple-element.24.refs_0_, bf16[16,4224]{1,0:T(8,128)(2,1)S(1)} %collective-permute-done.17.refs_1_, bf16[16,4224]{1,0:T(8,128)(2,1)S(1)} %collective-permute-done.18.refs_2_, ...), custom_call_target="tpu_custom_call" | custom-call | tf_op jit(solution)/shard_map/pallas_call | solution.py:380
  (43 shorter events, 0.6 us)
Async XLA Ops:
  0.6 22.6 %slice-start = ((s8[25165824]{0:T(1024)(128)(4,1)}), s8[4194304]{0:T(1024)(128)(4,1)S(1)}, s32[]{:S(2)}) async-start(s8[25165824]{0:T(1024)(128)(4,1)} %bitcast.3), calls=%async_computation | async-start | bytes 8388608
  0.7 22.6 %slice-start.1 = ((s8[25165824]{0:T(1024)(128)(4,1)}), s8[4194304]{0:T(1024)(128)(4,1)S(1)}, s32[]{:S(2)}) async-start(s8[25165824]{0:T(1024)(128)(4,1)} %bitcast.3), calls=%async_computation.1 | async-start | bytes 8388608
  0.7 22.6 %slice-start.2 = ((s8[25165824]{0:T(1024)(128)(4,1)}), s8[4194304]{0:T(1024)(128)(4,1)S(1)}, s32[]{:S(2)}) async-start(s8[25165824]{0:T(1024)(128)(4,1)} %bitcast.3), calls=%async_computation.2 | async-start | bytes 8388608
  1.8 10.3 %collective-permute-start.2 = (bf16[16,2176]{1,0:T(8,128)(2,1)S(1)}, bf16[16,2176]{1,0:T(8,128)(2,1)S(1)}, u32[]{:S(2)}, u32[]{:S(2)}) collective-permute-start(bf16[16,2176]{1,0:T(8,128)(2,1)S(1)} %shard_map.103.refs_0_.refs_7_), channel_id=1, source_target_pairs={{0,3},{1,2},{2,1},{3,0},{4,7},{5,6},{6,5},{7,4},{8,11},{9,10},{10,... | collective-permute-start | bytes 208904 | tf_op jit(solution)/shard_map/ppermute | solution.py:23
  5.8 6.8 %collective-permute-start.1 = (bf16[16,2176]{1,0:T(8,128)(2,1)S(1)}, bf16[16,2176]{1,0:T(8,128)(2,1)S(1)}, u32[]{:S(2)}, u32[]{:S(2)}) collective-permute-start(bf16[16,2176]{1,0:T(8,128)(2,1)S(1)} %shard_map.103.refs_0_.refs_7_), channel_id=1, source_target_pairs={{0,2},{1,3},{2,0},{3,1},{4,6},{5,7},{6,4},{7,5},{8,10},{9,11},{10,... | collective-permute-start | bytes 208904 | tf_op jit(solution)/shard_map/ppermute | solution.py:23
  6.3 5.8 %collective-permute-start.11 = (bf16[16,2048]{1,0:T(8,128)(2,1)S(1)}, bf16[16,2048]{1,0:T(8,128)(2,1)S(1)}, u32[]{:S(2)}, u32[]{:S(2)}) collective-permute-start(bf16[16,2048]{1,0:T(8,128)(2,1)S(1)} %copy-done.1), channel_id=1, source_target_pairs={{0,3},{1,2},{2,1},{3,0},{4,7},{5,6},{6,5},{7,4},{8,11},{9,10},{10,... | collective-permute-start | bytes 196616 | tf_op jit(solution)/shard_map/ppermute | solution.py:23
  7.8 4.9 %collective-permute-start.10 = (bf16[16,2048]{1,0:T(8,128)(2,1)S(1)}, bf16[16,2048]{1,0:T(8,128)(2,1)S(1)}, u32[]{:S(2)}, u32[]{:S(2)}) collective-permute-start(bf16[16,2048]{1,0:T(8,128)(2,1)S(1)} %copy-done.1), channel_id=1, source_target_pairs={{0,2},{1,3},{2,0},{3,1},{4,6},{5,7},{6,4},{7,5},{8,10},{9,11},{10,... | collective-permute-start | bytes 196616 | tf_op jit(solution)/shard_map/ppermute | solution.py:23
  7.9 6.1 %collective-permute-start = (bf16[16,2176]{1,0:T(8,128)(2,1)S(1)}, bf16[16,2176]{1,0:T(8,128)(2,1)S(1)}, u32[]{:S(2)}, u32[]{:S(2)}) collective-permute-start(bf16[16,2176]{1,0:T(8,128)(2,1)S(1)} %shard_map.103.refs_0_.refs_7_), channel_id=1, source_target_pairs={{0,1},{1,0},{2,3},{3,2},{4,5},{5,4},{6,7},{7,6},{8,9},{9,8},{10,11... | collective-permute-start | bytes 208904 | tf_op jit(solution)/shard_map/ppermute | solution.py:23
  12.1 5.0 %collective-permute-start.3 = (bf16[16,2176]{1,0:T(8,128)(2,1)S(1)}, bf16[16,2176]{1,0:T(8,128)(2,1)S(1)}, u32[]{:S(2)}, u32[]{:S(2)}) collective-permute-start(bf16[16,2176]{1,0:T(8,128)(2,1)S(1)} %shard_map.103.refs_0_.refs_7_), channel_id=1, source_target_pairs={{0,4},{4,0},{8,12},{12,8},{16,20},{20,16},{24,28},{28,24},{1,5},{5... | collective-permute-start | bytes 208904 | tf_op jit(solution)/shard_map/ppermute | solution.py:23
  12.1 5.5 %collective-permute-start.6 = (bf16[16,2176]{1,0:T(8,128)(2,1)S(1)}, bf16[16,2176]{1,0:T(8,128)(2,1)S(1)}, u32[]{:S(2)}, u32[]{:S(2)}) collective-permute-start(bf16[16,2176]{1,0:T(8,128)(2,1)S(1)} %collective-permute-done.2.refs_3_.refs_10_), channel_id=1, source_target_pairs={{0,4},{4,0},{8,12},{12,8},{16,20},{20,16},{24,28},{28,24},{1,5},{5... | collective-permute-start | bytes 208904 | tf_op jit(solution)/shard_map/ppermute | solution.py:23
  12.6 5.1 %collective-permute-start.5 = (bf16[16,2176]{1,0:T(8,128)(2,1)S(1)}, bf16[16,2176]{1,0:T(8,128)(2,1)S(1)}, u32[]{:S(2)}, u32[]{:S(2)}) collective-permute-start(bf16[16,2176]{1,0:T(8,128)(2,1)S(1)} %collective-permute-done.1.refs_2_.refs_9_), channel_id=1, source_target_pairs={{0,4},{4,0},{8,12},{12,8},{16,20},{20,16},{24,28},{28,24},{1,5},{5... | collective-permute-start | bytes 208904 | tf_op jit(solution)/shard_map/ppermute | solution.py:23
  12.7 4.4 %collective-permute-start.9 = (bf16[16,2048]{1,0:T(8,128)(2,1)S(1)}, bf16[16,2048]{1,0:T(8,128)(2,1)S(1)}, u32[]{:S(2)}, u32[]{:S(2)}) collective-permute-start(bf16[16,2048]{1,0:T(8,128)(2,1)S(1)} %copy-done.1), channel_id=1, source_target_pairs={{0,1},{1,0},{2,3},{3,2},{4,5},{5,4},{6,7},{7,6},{8,9},{9,8},{10,11... | collective-permute-start | bytes 196616 | tf_op jit(solution)/shard_map/ppermute | solution.py:23
  13.9 4.2 %collective-permute-start.4 = (bf16[16,2176]{1,0:T(8,128)(2,1)S(1)}, bf16[16,2176]{1,0:T(8,128)(2,1)S(1)}, u32[]{:S(2)}, u32[]{:S(2)}) collective-permute-start(bf16[16,2176]{1,0:T(8,128)(2,1)S(1)} %collective-permute-done.refs_1_.refs_8_), channel_id=1, source_target_pairs={{0,4},{4,0},{8,12},{12,8},{16,20},{20,16},{24,28},{28,24},{1,5},{5... | collective-permute-start | bytes 208904 | tf_op jit(solution)/shard_map/ppermute | solution.py:23
  17.1 5.0 %collective-permute-start.12 = (bf16[16,2048]{1,0:T(8,128)(2,1)S(1)}, bf16[16,2048]{1,0:T(8,128)(2,1)S(1)}, u32[]{:S(2)}, u32[]{:S(2)}) collective-permute-start(bf16[16,2048]{1,0:T(8,128)(2,1)S(1)} %copy-done.1), channel_id=1, source_target_pairs={{0,4},{4,0},{8,12},{12,8},{16,20},{20,16},{24,28},{28,24},{1,5},{5... | collective-permute-start | bytes 196616 | tf_op jit(solution)/shard_map/ppermute | solution.py:23
  17.1 5.0 %collective-permute-start.15 = (bf16[16,2048]{1,0:T(8,128)(2,1)S(1)}, bf16[16,2048]{1,0:T(8,128)(2,1)S(1)}, u32[]{:S(2)}, u32[]{:S(2)}) collective-permute-start(bf16[16,2048]{1,0:T(8,128)(2,1)S(1)} %collective-permute-done.11.refs_3_), channel_id=1, source_target_pairs={{0,4},{4,0},{8,12},{12,8},{16,20},{20,16},{24,28},{28,24},{1,5},{5... | collective-permute-start | bytes 196616 | tf_op jit(solution)/shard_map/ppermute | solution.py:23
  17.6 4.5 %collective-permute-start.14 = (bf16[16,2048]{1,0:T(8,128)(2,1)S(1)}, bf16[16,2048]{1,0:T(8,128)(2,1)S(1)}, u32[]{:S(2)}, u32[]{:S(2)}) collective-permute-start(bf16[16,2048]{1,0:T(8,128)(2,1)S(1)} %collective-permute-done.10.refs_2_), channel_id=1, source_target_pairs={{0,4},{4,0},{8,12},{12,8},{16,20},{20,16},{24,28},{28,24},{1,5},{5... | collective-permute-start | bytes 196616 | tf_op jit(solution)/shard_map/ppermute | solution.py:23
  17.7 4.4 %collective-permute-start.13 = (bf16[16,2048]{1,0:T(8,128)(2,1)S(1)}, bf16[16,2048]{1,0:T(8,128)(2,1)S(1)}, u32[]{:S(2)}, u32[]{:S(2)}) collective-permute-start(bf16[16,2048]{1,0:T(8,128)(2,1)S(1)} %collective-permute-done.9.refs_1_), channel_id=1, source_target_pairs={{0,4},{4,0},{8,12},{12,8},{16,20},{20,16},{24,28},{28,24},{1,5},{5... | collective-permute-start | bytes 196616 | tf_op jit(solution)/shard_map/ppermute | solution.py:23
  18.4 24.3 %copy-start.2 = (s32[16,8]{0,1:T(8,128)S(1)}, s32[16,8]{0,1:T(8,128)}, u32[]{:S(2)}) copy-start(s32[16,8]{0,1:T(8,128)} %param.11) | copy-start | bytes 1540
  18.4 3.7 %collective-permute-start.7 = (f32[8,128]{1,0:T(8,128)S(1)}, f32[8,128]{1,0:T(8,128)S(1)}, u32[]{:S(2)}, u32[]{:S(2)}) collective-permute-start(f32[8,128]{1,0:T(8,128)S(1)} %get-tuple-element.17.refs_2_), channel_id=1, source_target_pairs={{0,8},{4,20},{8,0},{12,28},{16,24},{20,4},{24,16},{28,12},{1,9},{5... | collective-permute-start | bytes 12296 | tf_op jit(solution)/shard_map/ppermute | solution.py:28
  22.1 1.2 %collective-permute-start.8 = (f32[8,128]{1,0:T(8,128)S(1)}, f32[8,128]{1,0:T(8,128)S(1)}, u32[]{:S(2)}, u32[]{:S(2)}) collective-permute-start(f32[8,128]{1,0:T(8,128)S(1)} %collective-permute-done.7.refs_0_), channel_id=1, source_target_pairs={{0,4},{4,0},{8,12},{12,8},{16,20},{20,16},{24,28},{28,24},{1,5},{5... | collective-permute-start | bytes 12296 | tf_op jit(solution)/shard_map/ppermute | solution.py:23
  30.9 2.0 %collective-permute-start.16 = (bf16[64,4224]{1,0:T(8,128)(2,1)S(1)}, bf16[64,4224]{1,0:T(8,128)(2,1)S(1)}, u32[]{:S(2)}, u32[]{:S(2)}) collective-permute-start(bf16[64,4224]{1,0:T(8,128)(2,1)S(1)} %get-tuple-element.23), channel_id=1, source_target_pairs={{0,4},{4,0},{8,12},{12,8},{16,20},{20,16},{24,28},{28,24},{1,5},{5... | collective-permute-start | bytes 1622024 | tf_op jit(solution)/shard_map/ppermute | solution.py:23
  33.1 6.5 %collective-permute-start.17 = (bf16[16,4224]{1,0:T(8,128)(2,1)S(1)}, bf16[16,4224]{1,0:T(8,128)(2,1)S(1)}, u32[]{:S(2)}, u32[]{:S(2)}) collective-permute-start(bf16[16,4224]{1,0:T(8,128)(2,1)S(1)} %get-tuple-element.25), channel_id=1, source_target_pairs={{0,1},{1,0},{2,3},{3,2},{4,5},{5,4},{6,7},{7,6},{8,9},{9,8},{10,11... | collective-permute-start | bytes 405512 | tf_op jit(solution)/shard_map/ppermute | solution.py:23
  34.2 8.5 %collective-permute-start.18 = (bf16[16,4224]{1,0:T(8,128)(2,1)S(1)}, bf16[16,4224]{1,0:T(8,128)(2,1)S(1)}, u32[]{:S(2)}, u32[]{:S(2)}) collective-permute-start(bf16[16,4224]{1,0:T(8,128)(2,1)S(1)} %get-tuple-element.26), channel_id=1, source_target_pairs={{0,2},{1,3},{2,0},{3,1},{4,6},{5,7},{6,4},{7,5},{8,10},{9,11},{10,... | collective-permute-start | bytes 405512 | tf_op jit(solution)/shard_map/ppermute | solution.py:23
  35.1 7.6 %collective-permute-start.19 = (bf16[16,4224]{1,0:T(8,128)(2,1)S(1)}, bf16[16,4224]{1,0:T(8,128)(2,1)S(1)}, u32[]{:S(2)}, u32[]{:S(2)}) collective-permute-start(bf16[16,4224]{1,0:T(8,128)(2,1)S(1)} %get-tuple-element.27), channel_id=1, source_target_pairs={{0,3},{1,2},{2,1},{3,0},{4,7},{5,6},{6,5},{7,4},{8,11},{9,10},{10,... | collective-permute-start | bytes 405512 | tf_op jit(solution)/shard_map/ppermute | solution.py:23
  (6 other events, 117.3 us)

commit v6 on v5

--- a/solution.py
+++ b/solution.py
@@ -134,7 +134,7 @@
             back[i, :, cols] = jnp.dot(g, down[first_local + i, :, cols], preferred_element_type=jnp.float32)
 
 
-def first_kernel(groups, local_count, count, width, *refs):
+def first_kernel(groups, local_count, count, width, kept, *refs):
     toks, (backs, gate_t, gate_up, hid, dpre, grads, tok) = refs[:count], refs[count:]
     _, first_local = place_of(groups, local_count)
     rows = tok.shape[0]
@@ -142,7 +142,7 @@
     hidden_units = hid.shape[2]
     for n in range(count):
         tok[pl.ds(n * piece_rows, piece_rows), :] = toks[n][:, :width]
-    gates = to_columns(gate_t[...], rows)
+    gates = to_columns(gate_t[...], rows) * kept
     lane = iota((rows, LANES), 1)
     t = tok[...]
     gate_grads = jnp.zeros((rows, LANES), jnp.float32)
@@ -168,15 +168,13 @@
     grads[...] = gate_grads
 
 
-def second_kernel(groups, local_count, width, levels, mask_ref, *refs):
+def kept_columns(groups, local_count, levels, mask_ref, far, spare, named_t, place_t, cap_t):
     far_pairs = []
     for even, odd in levels:
         n = 1 if even == odd else 2
-        far_pairs.append(refs[:n])
-        refs = refs[n:]
-    (spare, named_t, place_t, cap_t, hid, dpre, grads, gate_up, down), outs = refs[:9], refs[9 : 9 + groups]
-    first_expert, first_local = place_of(groups, local_count)
-    rows = hid.shape[1]
+        far_pairs.append(far[:n])
+        far = far[n:]
+    rows = named_t.shape[1]
     group_rows = rows // groups
     sub = iota((SUB, 1), 0)
     mask = jnp.zeros((SUB, 1), jnp.int32)
@@ -198,11 +196,12 @@
             other = jnp.where(mask == crossed, refs_at[1][:, 1 - g : 2 - g], other)
         limit = jnp.where(group_of == g, cap_t[:, g : g + 1] + jnp.minimum(other, float(OVF)), limit)
     kept = jnp.where((named_t[...] > 0.0) & (place_t[...] < limit), 1.0, 0.0)
-    kept = to_columns(kept, rows)
-    for i in range(hid.shape[0]):
-        keep = lane_of(kept, first_local + i) > 0.0
-        hid[i] = jnp.where(keep, hid[i].astype(jnp.float32), 0.0).astype(jnp.bfloat16)
-        dpre[i] = jnp.where(keep, dpre[i].astype(jnp.float32), 0.0).astype(jnp.bfloat16)
+    return to_columns(kept, rows)
+
+
+def second_kernel(groups, local_count, width, kept, hid, dpre, grads, gate_up, down, *outs):
+    first_expert, first_local = place_of(groups, local_count)
+    group_rows = hid.shape[1] // groups
 
     def product(left, right, cols):
         total = None
@@ -236,11 +235,9 @@
     toks, backs, refs = refs[:count], refs[count], refs[count + 1 :]
     (gate_up, down), refs = refs[:2], refs[2:]
     outs, (tok, hid, dpre, grads) = refs[:groups], refs[groups:]
-    first_kernel(groups, local_count, count, width, *toks, backs, gate_t, gate_up, hid, dpre, grads, tok)
-    second_kernel(
-        groups, local_count, width, levels, mask_ref,
-        *far, spare, named_t, place_t, cap_t, hid, dpre, grads, gate_up, down, *outs,
-    )
+    kept = kept_columns(groups, local_count, levels, mask_ref, far, spare, named_t, place_t, cap_t)
+    first_kernel(groups, local_count, count, width, kept, *toks, backs, gate_t, gate_up, hid, dpre, grads, tok)
+    second_kernel(groups, local_count, width, kept, hid, dpre, grads, gate_up, down, *outs)
 
 
 def join_kernel(own, other, *outs):

time: 43.5 us -> 43.5 us (level)
  no operation moved by 1% of the time
where the time goes in v6:
time: 43.5 us; the launch traced here: 43.4 us
  starting transfers between devices  16.5 us (38%)
  waiting for transfers between devices  15.4 us (35%)
  Pallas kernels  10.7 us (25%)
  between operations  0.82 us (2%)
    ppermute x19, starting transfers between devices, swapped(): lax.ppermute(shard, axis, [(i, i ^ mask) for i in range(lax.axis_size(axi...  14.9 us
    ppermute x19, waiting for transfers between devices, swapped(): lax.ppermute(shard, axis, [(i, i ^ mask) for i in range(lax.axis_size(axi...  13.3 us
    pallas_call x1, Pallas kernels, body(): kernel(functools.partial(experts_kernel, groups, local_count, count, widt...  7.56 us
    ppermute x1, waiting for transfers between devices, swapped_by_core(): return lax.ppermute(shard, 'dp', pairs)  2.07 us
    ppermute x1, starting transfers between devices, swapped_by_core(): return lax.ppermute(shard, 'dp', pairs)  1.61 us
    pallas_call x1, Pallas kernels, body(): kernel(prep_kernel, array((tok_count, width + LANES), bf16), [hbm] * 3 +...  1.03 us
    pallas_call x1, Pallas kernels, body(): kernel(functools.partial(back_kernel, groups, local_count), array((per_de...  1 us
  transfers between devices with their start and end apart: 20, of which 7 were waited for; matrix products, arithmetic and copies ran while one was open for 0% of the time, Pallas kernels for 3%

profile of v6, /device:TPU:0, one launch (start us, length us, event | category | flops | bytes accessed | tf_op | source)
XLA Modules:
  0.0 43.4 jit_solution(162573799894295658)
XLA Ops:
  0.7 1.0 %shard_map.103.refs_0_.refs_7_ = bf16[16,2176]{1,0:T(8,128)(2,1)S(1)} custom-call(bf16[16,2048]{1,0:T(8,128)(2,1)} %tokens.1, s32[8,16]{1,0:T(8,128)} %bitcast.5, bf16[8,16]{1,0:T(8,128)(2,1)} %bitcast.8, s32[1,4]{1,0:T(1,128)} %capacity.1), custom_call_target="tpu_custom_call" | custom-call | flops 20000000000 | tf_op jit(solution)/shard_map/pallas_call | solution.py:301
  1.8 4.0 %collective-permute-start.2 = (bf16[16,2176]{1,0:T(8,128)(2,1)S(1)}, bf16[16,2176]{1,0:T(8,128)(2,1)S(1)}, u32[]{:S(2)}, u32[]{:S(2)}) collective-permute-start(bf16[16,2176]{1,0:T(8,128)(2,1)S(1)} %shard_map.103.refs_0_.refs_7_), channel_id=1, source_target_pairs={{0,3},{1,2},{2,1},{3,0},{4,7},{5,6},{6,5},{7,4},{8,11},{9,10},{10,... | collective-permute-start | bytes 208904 | tf_op jit(solution)/shard_map/ppermute | solution.py:23
  5.8 0.5 %collective-permute-start.1 = (bf16[16,2176]{1,0:T(8,128)(2,1)S(1)}, bf16[16,2176]{1,0:T(8,128)(2,1)S(1)}, u32[]{:S(2)}, u32[]{:S(2)}) collective-permute-start(bf16[16,2176]{1,0:T(8,128)(2,1)S(1)} %shard_map.103.refs_0_.refs_7_), channel_id=1, source_target_pairs={{0,2},{1,3},{2,0},{3,1},{4,6},{5,7},{6,4},{7,5},{8,10},{9,11},{10,... | collective-permute-start | bytes 208904 | tf_op jit(solution)/shard_map/ppermute | solution.py:23
  6.3 1.5 %collective-permute-start.11 = (bf16[16,2048]{1,0:T(8,128)(2,1)S(1)}, bf16[16,2048]{1,0:T(8,128)(2,1)S(1)}, u32[]{:S(2)}, u32[]{:S(2)}) collective-permute-start(bf16[16,2048]{1,0:T(8,128)(2,1)S(1)} %copy-done.1), channel_id=1, source_target_pairs={{0,3},{1,2},{2,1},{3,0},{4,7},{5,6},{6,5},{7,4},{8,11},{9,10},{10,... | collective-permute-start | bytes 196616 | tf_op jit(solution)/shard_map/ppermute | solution.py:23
  7.9 1.9 %collective-permute-start = (bf16[16,2176]{1,0:T(8,128)(2,1)S(1)}, bf16[16,2176]{1,0:T(8,128)(2,1)S(1)}, u32[]{:S(2)}, u32[]{:S(2)}) collective-permute-start(bf16[16,2176]{1,0:T(8,128)(2,1)S(1)} %shard_map.103.refs_0_.refs_7_), channel_id=1, source_target_pairs={{0,1},{1,0},{2,3},{3,2},{4,5},{5,4},{6,7},{7,6},{8,9},{9,8},{10,11... | collective-permute-start | bytes 208904 | tf_op jit(solution)/shard_map/ppermute | solution.py:23
  9.8 2.3 %collective-permute-done.11.refs_3_ = bf16[16,2048]{1,0:T(8,128)(2,1)S(1)} collective-permute-done((bf16[16,2048]{1,0:T(8,128)(2,1)S(1)}, bf16[16,2048]{1,0:T(8,128)(2,1)S(1)}, u32[]{:S(2)}, u32[]{:S(2)}) %collective-permute-start.11) | collective-permute-done | bytes 65568 | tf_op jit(solution)/shard_map/ppermute | solution.py:23
  12.1 0.5 %collective-permute-start.6 = (bf16[16,2176]{1,0:T(8,128)(2,1)S(1)}, bf16[16,2176]{1,0:T(8,128)(2,1)S(1)}, u32[]{:S(2)}, u32[]{:S(2)}) collective-permute-start(bf16[16,2176]{1,0:T(8,128)(2,1)S(1)} %collective-permute-done.2.refs_3_.refs_10_), channel_id=1, source_target_pairs={{0,4},{4,0},{8,12},{12,8},{16,20},{20,16},{24,28},{28,24},{1,5},{5... | collective-permute-start | bytes 208904 | tf_op jit(solution)/shard_map/ppermute | solution.py:23
  12.7 1.3 %collective-permute-start.9 = (bf16[16,2048]{1,0:T(8,128)(2,1)S(1)}, bf16[16,2048]{1,0:T(8,128)(2,1)S(1)}, u32[]{:S(2)}, u32[]{:S(2)}) collective-permute-start(bf16[16,2048]{1,0:T(8,128)(2,1)S(1)} %copy-done.1), channel_id=1, source_target_pairs={{0,1},{1,0},{2,3},{3,2},{4,5},{5,4},{6,7},{7,6},{8,9},{9,8},{10,11... | collective-permute-start | bytes 196616 | tf_op jit(solution)/shard_map/ppermute | solution.py:23
  13.9 3.2 %collective-permute-done.9.refs_1_ = bf16[16,2048]{1,0:T(8,128)(2,1)S(1)} collective-permute-done((bf16[16,2048]{1,0:T(8,128)(2,1)S(1)}, bf16[16,2048]{1,0:T(8,128)(2,1)S(1)}, u32[]{:S(2)}, u32[]{:S(2)}) %collective-permute-start.9) | collective-permute-done | bytes 65568 | tf_op jit(solution)/shard_map/ppermute | solution.py:23
  17.1 0.5 %collective-permute-start.15 = (bf16[16,2048]{1,0:T(8,128)(2,1)S(1)}, bf16[16,2048]{1,0:T(8,128)(2,1)S(1)}, u32[]{:S(2)}, u32[]{:S(2)}) collective-permute-start(bf16[16,2048]{1,0:T(8,128)(2,1)S(1)} %collective-permute-done.11.refs_3_), channel_id=1, source_target_pairs={{0,4},{4,0},{8,12},{12,8},{16,20},{20,16},{24,28},{28,24},{1,5},{5... | collective-permute-start | bytes 196616 | tf_op jit(solution)/shard_map/ppermute | solution.py:23
  17.7 0.4 %collective-permute-start.13 = (bf16[16,2048]{1,0:T(8,128)(2,1)S(1)}, bf16[16,2048]{1,0:T(8,128)(2,1)S(1)}, u32[]{:S(2)}, u32[]{:S(2)}) collective-permute-start(bf16[16,2048]{1,0:T(8,128)(2,1)S(1)} %collective-permute-done.9.refs_1_), channel_id=1, source_target_pairs={{0,4},{4,0},{8,12},{12,8},{16,20},{20,16},{24,28},{28,24},{1,5},{5... | collective-permute-start | bytes 196616 | tf_op jit(solution)/shard_map/ppermute | solution.py:23
  18.1 0.2 tables.1
  18.4 1.6 %collective-permute-start.7 = (f32[8,128]{1,0:T(8,128)S(1)}, f32[8,128]{1,0:T(8,128)S(1)}, u32[]{:S(2)}, u32[]{:S(2)}) collective-permute-start(f32[8,128]{1,0:T(8,128)S(1)} %get-tuple-element.17.refs_2_), channel_id=1, source_target_pairs={{0,8},{4,20},{8,0},{12,28},{16,24},{20,4},{24,16},{28,12},{1,9},{5... | collective-permute-start | bytes 12296 | tf_op jit(solution)/shard_map/ppermute | solution.py:28
  20.0 2.1 %collective-permute-done.7.refs_0_ = f32[8,128]{1,0:T(8,128)S(1)} collective-permute-done((f32[8,128]{1,0:T(8,128)S(1)}, f32[8,128]{1,0:T(8,128)S(1)}, u32[]{:S(2)}, u32[]{:S(2)}) %collective-permute-start.7) | collective-permute-done | bytes 4128 | tf_op jit(solution)/shard_map/ppermute | solution.py:28
  22.1 1.0 %shard_map.104.refs_15_ = f32[2,128,768]{2,1,0:T(8,128)S(1)} custom-call(bf16[16,2048]{1,0:T(8,128)(2,1)S(1)} %copy-done.1, bf16[16,2048]{1,0:T(8,128)(2,1)S(1)} %collective-permute-done.9.refs_1_, bf16[16,2048]{1,0:T(8,128)(2,1)S(1)} %collective-permute-done.10.refs_2_, bf16[16,2048]{1,0:T(8,128)(2,1)S(1)} %collective-permute-done.11.refs_3_, ...), custom_call_target="tpu_custom_call" | custom-call | tf_op jit(solution)/shard_map/pallas_call | solution.py:352
  23.3 7.6 %shard_map.105 = (bf16[64,4224]{1,0:T(8,128)(2,1)S(1)}, bf16[64,4224]{1,0:T(8,128)(2,1)S(1)}) custom-call(s32[4]{0:T(128)S(1)} %copy-done.3, f32[8,128]{1,0:T(8,128)S(1)} %collective-permute-done.7.refs_0_, f32[8,128]{1,0:T(8,128)S(1)} %collective-permute-done.8.refs_1_, f32[8,128]{1,0:T(8,128)S(1)} %get-tuple-element.17.refs_2_, ...), custom_call_target="tpu_custom_call" | custom-call | tf_op jit(solution)/shard_map/pallas_call | solution.py:358
  30.9 0.5 %collective-permute-start.16 = (bf16[64,4224]{1,0:T(8,128)(2,1)S(1)}, bf16[64,4224]{1,0:T(8,128)(2,1)S(1)}, u32[]{:S(2)}, u32[]{:S(2)}) collective-permute-start(bf16[64,4224]{1,0:T(8,128)(2,1)S(1)} %get-tuple-element.23), channel_id=1, source_target_pairs={{0,4},{4,0},{8,12},{12,8},{16,20},{20,16},{24,28},{28,24},{1,5},{5... | collective-permute-start | bytes 1622024 | tf_op jit(solution)/shard_map/ppermute | solution.py:23
  31.3 1.6 %collective-permute-done.16.other = bf16[64,4224]{1,0:T(8,128)(2,1)S(1)} collective-permute-done((bf16[64,4224]{1,0:T(8,128)(2,1)S(1)}, bf16[64,4224]{1,0:T(8,128)(2,1)S(1)}, u32[]{:S(2)}, u32[]{:S(2)}) %collective-permute-start.16) | collective-permute-done | bytes 540704 | tf_op jit(solution)/shard_map/ppermute | solution.py:23
  33.0 1.1 %collective-permute-start.17 = (bf16[16,4224]{1,0:T(8,128)(2,1)S(1)}, bf16[16,4224]{1,0:T(8,128)(2,1)S(1)}, u32[]{:S(2)}, u32[]{:S(2)}) collective-permute-start(bf16[16,4224]{1,0:T(8,128)(2,1)S(1)} %get-tuple-element.25), channel_id=1, source_target_pairs={{0,1},{1,0},{2,3},{3,2},{4,5},{5,4},{6,7},{7,6},{8,9},{9,8},{10,11... | collective-permute-start | bytes 405512 | tf_op jit(solution)/shard_map/ppermute | solution.py:23
  34.2 0.9 %collective-permute-start.18 = (bf16[16,4224]{1,0:T(8,128)(2,1)S(1)}, bf16[16,4224]{1,0:T(8,128)(2,1)S(1)}, u32[]{:S(2)}, u32[]{:S(2)}) collective-permute-start(bf16[16,4224]{1,0:T(8,128)(2,1)S(1)} %get-tuple-element.26), channel_id=1, source_target_pairs={{0,2},{1,3},{2,0},{3,1},{4,6},{5,7},{6,4},{7,5},{8,10},{9,11},{10,... | collective-permute-start | bytes 405512 | tf_op jit(solution)/shard_map/ppermute | solution.py:23
  35.1 1.5 %collective-permute-start.19 = (bf16[16,4224]{1,0:T(8,128)(2,1)S(1)}, bf16[16,4224]{1,0:T(8,128)(2,1)S(1)}, u32[]{:S(2)}, u32[]{:S(2)}) collective-permute-start(bf16[16,4224]{1,0:T(8,128)(2,1)S(1)} %get-tuple-element.27), channel_id=1, source_target_pairs={{0,3},{1,2},{2,1},{3,0},{4,7},{5,6},{6,5},{7,4},{8,11},{9,10},{10,... | collective-permute-start | bytes 405512 | tf_op jit(solution)/shard_map/ppermute | solution.py:23
  36.6 3.0 %collective-permute-done.17.refs_1_ = bf16[16,4224]{1,0:T(8,128)(2,1)S(1)} collective-permute-done((bf16[16,4224]{1,0:T(8,128)(2,1)S(1)}, bf16[16,4224]{1,0:T(8,128)(2,1)S(1)}, u32[]{:S(2)}, u32[]{:S(2)}) %collective-permute-start.17) | collective-permute-done | bytes 135200 | tf_op jit(solution)/shard_map/ppermute | solution.py:23
  39.6 3.1 %collective-permute-done.18.refs_2_ = bf16[16,4224]{1,0:T(8,128)(2,1)S(1)} collective-permute-done((bf16[16,4224]{1,0:T(8,128)(2,1)S(1)}, bf16[16,4224]{1,0:T(8,128)(2,1)S(1)}, u32[]{:S(2)}, u32[]{:S(2)}) %collective-permute-start.18) | collective-permute-done | bytes 135200 | tf_op jit(solution)/shard_map/ppermute | solution.py:23
  42.7 0.7 %shard_map.107 = (bf16[16,2048]{1,0:T(8,128)(2,1)}, bf16[16,2048]{1,0:T(8,128)(2,1)}, f32[8,16]{1,0:T(8,128)}) custom-call(bf16[16,4224]{1,0:T(8,128)(2,1)S(1)} %get-tuple-element.24.refs_0_, bf16[16,4224]{1,0:T(8,128)(2,1)S(1)} %collective-permute-done.17.refs_1_, bf16[16,4224]{1,0:T(8,128)(2,1)S(1)} %collective-permute-done.18.refs_2_, ...), custom_call_target="tpu_custom_call" | custom-call | tf_op jit(solution)/shard_map/pallas_call | solution.py:377
  (43 shorter events, 0.6 us)
Async XLA Ops:
  0.6 22.6 %slice-start = ((s8[25165824]{0:T(1024)(128)(4,1)}), s8[4194304]{0:T(1024)(128)(4,1)S(1)}, s32[]{:S(2)}) async-start(s8[25165824]{0:T(1024)(128)(4,1)} %bitcast.3), calls=%async_computation | async-start | bytes 8388608
  0.7 22.6 %slice-start.1 = ((s8[25165824]{0:T(1024)(128)(4,1)}), s8[4194304]{0:T(1024)(128)(4,1)S(1)}, s32[]{:S(2)}) async-start(s8[25165824]{0:T(1024)(128)(4,1)} %bitcast.3), calls=%async_computation.1 | async-start | bytes 8388608
  0.7 22.6 %slice-start.2 = ((s8[25165824]{0:T(1024)(128)(4,1)}), s8[4194304]{0:T(1024)(128)(4,1)S(1)}, s32[]{:S(2)}) async-start(s8[25165824]{0:T(1024)(128)(4,1)} %bitcast.3), calls=%async_computation.2 | async-start | bytes 8388608
  1.8 10.3 %collective-permute-start.2 = (bf16[16,2176]{1,0:T(8,128)(2,1)S(1)}, bf16[16,2176]{1,0:T(8,128)(2,1)S(1)}, u32[]{:S(2)}, u32[]{:S(2)}) collective-permute-start(bf16[16,2176]{1,0:T(8,128)(2,1)S(1)} %shard_map.103.refs_0_.refs_7_), channel_id=1, source_target_pairs={{0,3},{1,2},{2,1},{3,0},{4,7},{5,6},{6,5},{7,4},{8,11},{9,10},{10,... | collective-permute-start | bytes 208904 | tf_op jit(solution)/shard_map/ppermute | solution.py:23
  5.8 6.8 %collective-permute-start.1 = (bf16[16,2176]{1,0:T(8,128)(2,1)S(1)}, bf16[16,2176]{1,0:T(8,128)(2,1)S(1)}, u32[]{:S(2)}, u32[]{:S(2)}) collective-permute-start(bf16[16,2176]{1,0:T(8,128)(2,1)S(1)} %shard_map.103.refs_0_.refs_7_), channel_id=1, source_target_pairs={{0,2},{1,3},{2,0},{3,1},{4,6},{5,7},{6,4},{7,5},{8,10},{9,11},{10,... | collective-permute-start | bytes 208904 | tf_op jit(solution)/shard_map/ppermute | solution.py:23
  6.3 5.8 %collective-permute-start.11 = (bf16[16,2048]{1,0:T(8,128)(2,1)S(1)}, bf16[16,2048]{1,0:T(8,128)(2,1)S(1)}, u32[]{:S(2)}, u32[]{:S(2)}) collective-permute-start(bf16[16,2048]{1,0:T(8,128)(2,1)S(1)} %copy-done.1), channel_id=1, source_target_pairs={{0,3},{1,2},{2,1},{3,0},{4,7},{5,6},{6,5},{7,4},{8,11},{9,10},{10,... | collective-permute-start | bytes 196616 | tf_op jit(solution)/shard_map/ppermute | solution.py:23
  7.8 4.9 %collective-permute-start.10 = (bf16[16,2048]{1,0:T(8,128)(2,1)S(1)}, bf16[16,2048]{1,0:T(8,128)(2,1)S(1)}, u32[]{:S(2)}, u32[]{:S(2)}) collective-permute-start(bf16[16,2048]{1,0:T(8,128)(2,1)S(1)} %copy-done.1), channel_id=1, source_target_pairs={{0,2},{1,3},{2,0},{3,1},{4,6},{5,7},{6,4},{7,5},{8,10},{9,11},{10,... | collective-permute-start | bytes 196616 | tf_op jit(solution)/shard_map/ppermute | solution.py:23
  7.9 6.1 %collective-permute-start = (bf16[16,2176]{1,0:T(8,128)(2,1)S(1)}, bf16[16,2176]{1,0:T(8,128)(2,1)S(1)}, u32[]{:S(2)}, u32[]{:S(2)}) collective-permute-start(bf16[16,2176]{1,0:T(8,128)(2,1)S(1)} %shard_map.103.refs_0_.refs_7_), channel_id=1, source_target_pairs={{0,1},{1,0},{2,3},{3,2},{4,5},{5,4},{6,7},{7,6},{8,9},{9,8},{10,11... | collective-permute-start | bytes 208904 | tf_op jit(solution)/shard_map/ppermute | solution.py:23
  12.1 5.0 %collective-permute-start.3 = (bf16[16,2176]{1,0:T(8,128)(2,1)S(1)}, bf16[16,2176]{1,0:T(8,128)(2,1)S(1)}, u32[]{:S(2)}, u32[]{:S(2)}) collective-permute-start(bf16[16,2176]{1,0:T(8,128)(2,1)S(1)} %shard_map.103.refs_0_.refs_7_), channel_id=1, source_target_pairs={{0,4},{4,0},{8,12},{12,8},{16,20},{20,16},{24,28},{28,24},{1,5},{5... | collective-permute-start | bytes 208904 | tf_op jit(solution)/shard_map/ppermute | solution.py:23
  12.1 5.5 %collective-permute-start.6 = (bf16[16,2176]{1,0:T(8,128)(2,1)S(1)}, bf16[16,2176]{1,0:T(8,128)(2,1)S(1)}, u32[]{:S(2)}, u32[]{:S(2)}) collective-permute-start(bf16[16,2176]{1,0:T(8,128)(2,1)S(1)} %collective-permute-done.2.refs_3_.refs_10_), channel_id=1, source_target_pairs={{0,4},{4,0},{8,12},{12,8},{16,20},{20,16},{24,28},{28,24},{1,5},{5... | collective-permute-start | bytes 208904 | tf_op jit(solution)/shard_map/ppermute | solution.py:23
  12.6 5.1 %collective-permute-start.5 = (bf16[16,2176]{1,0:T(8,128)(2,1)S(1)}, bf16[16,2176]{1,0:T(8,128)(2,1)S(1)}, u32[]{:S(2)}, u32[]{:S(2)}) collective-permute-start(bf16[16,2176]{1,0:T(8,128)(2,1)S(1)} %collective-permute-done.1.refs_2_.refs_9_), channel_id=1, source_target_pairs={{0,4},{4,0},{8,12},{12,8},{16,20},{20,16},{24,28},{28,24},{1,5},{5... | collective-permute-start | bytes 208904 | tf_op jit(solution)/shard_map/ppermute | solution.py:23
  12.7 4.4 %collective-permute-start.9 = (bf16[16,2048]{1,0:T(8,128)(2,1)S(1)}, bf16[16,2048]{1,0:T(8,128)(2,1)S(1)}, u32[]{:S(2)}, u32[]{:S(2)}) collective-permute-start(bf16[16,2048]{1,0:T(8,128)(2,1)S(1)} %copy-done.1), channel_id=1, source_target_pairs={{0,1},{1,0},{2,3},{3,2},{4,5},{5,4},{6,7},{7,6},{8,9},{9,8},{10,11... | collective-permute-start | bytes 196616 | tf_op jit(solution)/shard_map/ppermute | solution.py:23
  13.9 4.2 %collective-permute-start.4 = (bf16[16,2176]{1,0:T(8,128)(2,1)S(1)}, bf16[16,2176]{1,0:T(8,128)(2,1)S(1)}, u32[]{:S(2)}, u32[]{:S(2)}) collective-permute-start(bf16[16,2176]{1,0:T(8,128)(2,1)S(1)} %collective-permute-done.refs_1_.refs_8_), channel_id=1, source_target_pairs={{0,4},{4,0},{8,12},{12,8},{16,20},{20,16},{24,28},{28,24},{1,5},{5... | collective-permute-start | bytes 208904 | tf_op jit(solution)/shard_map/ppermute | solution.py:23
  17.1 5.0 %collective-permute-start.12 = (bf16[16,2048]{1,0:T(8,128)(2,1)S(1)}, bf16[16,2048]{1,0:T(8,128)(2,1)S(1)}, u32[]{:S(2)}, u32[]{:S(2)}) collective-permute-start(bf16[16,2048]{1,0:T(8,128)(2,1)S(1)} %copy-done.1), channel_id=1, source_target_pairs={{0,4},{4,0},{8,12},{12,8},{16,20},{20,16},{24,28},{28,24},{1,5},{5... | collective-permute-start | bytes 196616 | tf_op jit(solution)/shard_map/ppermute | solution.py:23
  17.1 5.0 %collective-permute-start.15 = (bf16[16,2048]{1,0:T(8,128)(2,1)S(1)}, bf16[16,2048]{1,0:T(8,128)(2,1)S(1)}, u32[]{:S(2)}, u32[]{:S(2)}) collective-permute-start(bf16[16,2048]{1,0:T(8,128)(2,1)S(1)} %collective-permute-done.11.refs_3_), channel_id=1, source_target_pairs={{0,4},{4,0},{8,12},{12,8},{16,20},{20,16},{24,28},{28,24},{1,5},{5... | collective-permute-start | bytes 196616 | tf_op jit(solution)/shard_map/ppermute | solution.py:23
  17.6 4.5 %collective-permute-start.14 = (bf16[16,2048]{1,0:T(8,128)(2,1)S(1)}, bf16[16,2048]{1,0:T(8,128)(2,1)S(1)}, u32[]{:S(2)}, u32[]{:S(2)}) collective-permute-start(bf16[16,2048]{1,0:T(8,128)(2,1)S(1)} %collective-permute-done.10.refs_2_), channel_id=1, source_target_pairs={{0,4},{4,0},{8,12},{12,8},{16,20},{20,16},{24,28},{28,24},{1,5},{5... | collective-permute-start | bytes 196616 | tf_op jit(solution)/shard_map/ppermute | solution.py:23
  17.7 4.4 %collective-permute-start.13 = (bf16[16,2048]{1,0:T(8,128)(2,1)S(1)}, bf16[16,2048]{1,0:T(8,128)(2,1)S(1)}, u32[]{:S(2)}, u32[]{:S(2)}) collective-permute-start(bf16[16,2048]{1,0:T(8,128)(2,1)S(1)} %collective-permute-done.9.refs_1_), channel_id=1, source_target_pairs={{0,4},{4,0},{8,12},{12,8},{16,20},{20,16},{24,28},{28,24},{1,5},{5... | collective-permute-start | bytes 196616 | tf_op jit(solution)/shard_map/ppermute | solution.py:23
  18.4 24.3 %copy-start.2 = (s32[16,8]{0,1:T(8,128)S(1)}, s32[16,8]{0,1:T(8,128)}, u32[]{:S(2)}) copy-start(s32[16,8]{0,1:T(8,128)} %param.11) | copy-start | bytes 1540
  18.4 3.7 %collective-permute-start.7 = (f32[8,128]{1,0:T(8,128)S(1)}, f32[8,128]{1,0:T(8,128)S(1)}, u32[]{:S(2)}, u32[]{:S(2)}) collective-permute-start(f32[8,128]{1,0:T(8,128)S(1)} %get-tuple-element.17.refs_2_), channel_id=1, source_target_pairs={{0,8},{4,20},{8,0},{12,28},{16,24},{20,4},{24,16},{28,12},{1,9},{5... | collective-permute-start | bytes 12296 | tf_op jit(solution)/shard_map/ppermute | solution.py:28
  22.1 1.2 %collective-permute-start.8 = (f32[8,128]{1,0:T(8,128)S(1)}, f32[8,128]{1,0:T(8,128)S(1)}, u32[]{:S(2)}, u32[]{:S(2)}) collective-permute-start(f32[8,128]{1,0:T(8,128)S(1)} %collective-permute-done.7.refs_0_), channel_id=1, source_target_pairs={{0,4},{4,0},{8,12},{12,8},{16,20},{20,16},{24,28},{28,24},{1,5},{5... | collective-permute-start | bytes 12296 | tf_op jit(solution)/shard_map/ppermute | solution.py:23
  30.9 2.0 %collective-permute-start.16 = (bf16[64,4224]{1,0:T(8,128)(2,1)S(1)}, bf16[64,4224]{1,0:T(8,128)(2,1)S(1)}, u32[]{:S(2)}, u32[]{:S(2)}) collective-permute-start(bf16[64,4224]{1,0:T(8,128)(2,1)S(1)} %get-tuple-element.23), channel_id=1, source_target_pairs={{0,4},{4,0},{8,12},{12,8},{16,20},{20,16},{24,28},{28,24},{1,5},{5... | collective-permute-start | bytes 1622024 | tf_op jit(solution)/shard_map/ppermute | solution.py:23
  33.0 6.5 %collective-permute-start.17 = (bf16[16,4224]{1,0:T(8,128)(2,1)S(1)}, bf16[16,4224]{1,0:T(8,128)(2,1)S(1)}, u32[]{:S(2)}, u32[]{:S(2)}) collective-permute-start(bf16[16,4224]{1,0:T(8,128)(2,1)S(1)} %get-tuple-element.25), channel_id=1, source_target_pairs={{0,1},{1,0},{2,3},{3,2},{4,5},{5,4},{6,7},{7,6},{8,9},{9,8},{10,11... | collective-permute-start | bytes 405512 | tf_op jit(solution)/shard_map/ppermute | solution.py:23
  34.2 8.5 %collective-permute-start.18 = (bf16[16,4224]{1,0:T(8,128)(2,1)S(1)}, bf16[16,4224]{1,0:T(8,128)(2,1)S(1)}, u32[]{:S(2)}, u32[]{:S(2)}) collective-permute-start(bf16[16,4224]{1,0:T(8,128)(2,1)S(1)} %get-tuple-element.26), channel_id=1, source_target_pairs={{0,2},{1,3},{2,0},{3,1},{4,6},{5,7},{6,4},{7,5},{8,10},{9,11},{10,... | collective-permute-start | bytes 405512 | tf_op jit(solution)/shard_map/ppermute | solution.py:23
  35.1 7.6 %collective-permute-start.19 = (bf16[16,4224]{1,0:T(8,128)(2,1)S(1)}, bf16[16,4224]{1,0:T(8,128)(2,1)S(1)}, u32[]{:S(2)}, u32[]{:S(2)}) collective-permute-start(bf16[16,4224]{1,0:T(8,128)(2,1)S(1)} %get-tuple-element.27), channel_id=1, source_target_pairs={{0,3},{1,2},{2,1},{3,0},{4,7},{5,6},{6,5},{7,4},{8,11},{9,10},{10,... | collective-permute-start | bytes 405512 | tf_op jit(solution)/shard_map/ppermute | solution.py:23
  (6 other events, 117.3 us)
